TPU v7x, 256 devices: a whole 4x4x8 slice. The times are simulated.
256 devices in a mesh: seq: 32 (over z_hi, y, core), tp: 8 (over z_lo, x).
Axes of the slice: x: 4, y: 4, z: 8 (z_hi: 4, z_lo: 2; z = z_hi * 2 + z_lo), core: 2. Of those that a mesh axis runs over, the one named last changes fastest.
Arguments:
- pixels: bfloat16 [64, 256, 1664], P('seq', 'tp'), may hold values from -6 to 6
- text_rows: bfloat16 [16384, 1664], P(('seq', 'tp')), may hold values from -6 to 6
- patch_counts: int32 [64], replicated, may hold values from 4 to 256, as said below
- picture_starts: int32 [64], replicated, may hold values from 0 to 16320, as said below
- block_lengths: int32 [32], replicated, may hold values from 256 to 512
- vision_gain: float32 [1664], replicated, may hold values from 0.25 to 1.75
- vision_project: bfloat16 [1664, 3, 1664], P(None, None, 'tp')
- vision_output: bfloat16 [1664, 1664], P('tp'), may hold values from -0.15625 to 0.15625
- merge_gain: float32 [1664], replicated, may hold values from 0.25 to 1.75
- merge_weight: bfloat16 [6656, 1664], P('tp'), may hold values from -0.078125 to 0.078125
- text_gain: float32 [1664], replicated, may hold values from 0.25 to 1.75
- text_project: bfloat16 [1664, 3, 1664], P(None, None, 'tp')
- text_output: bfloat16 [1664, 1664], P('tp'), may hold values from -0.15625 to 0.15625
Outputs:
- hidden: bfloat16 [16384, 1664], P(('seq', 'tp'))
- key_cache: bfloat16 [16384, 1664], P('seq', 'tp')
- value_cache: bfloat16 [16384, 1664], P('seq', 'tp')
Inputs may be any that keep to these rules, and one draw needn't show every extreme that they name: `patch_counts`: every count is a multiple of 4. Picture p's merged tokens take positions picture_starts[p] to picture_starts[p] + 63 inside one block of 512 positions, and these ranges of different pictures are disjoint; every block holds exactly one picture of each rank k < 2, rank k meaning the pictures s * 2 + k; the pictures of one index of seq lie in different blocks.
All inputs are finite; a program needn't handle non-finite values.
Results may differ from a plain program's by a relative error of at most 0.034.
The roundings to bfloat16 on the way count: a program that leaves them out, or rounds other values in their place, can miss the bound.
Values may be sent and summed in bfloat16 or wider, within the bound.
A program may use at most 128 MiB of HBM per device.

v0:
```python
import math

import jax
import jax.numpy as jnp
from jax import lax
from jax.sharding import PartitionSpec as P

HEAD = 104


LN_EPS = 1e-05
RMS_EPS = 1e-06
MASKED_SCORE = -1e30
KEY_SPAN = 512


def layer_normed(row_values, gain_vector):
    floats = row_values.astype(jnp.float32)
    centre = floats - jnp.mean(floats, -1, keepdims=True)
    spread = jnp.mean(centre * centre, -1, keepdims=True)
    return centre * lax.rsqrt(spread + LN_EPS) * gain_vector


def rms_normed(row_values, gain_vector):
    floats = row_values.astype(jnp.float32)
    return floats * lax.rsqrt(jnp.mean(floats * floats, -1, keepdims=True) + RMS_EPS) * gain_vector


def rotary(heads_in, positions):
    halfway = heads_in.shape[-1] // 2
    rates = 10000.0 ** (-2.0 * jnp.arange(halfway, dtype=jnp.float32) / heads_in.shape[-1])
    angles = positions.astype(jnp.float32)[:, None] * rates[None, :]
    cosine_table = jnp.cos(angles)[:, None, :]
    sine_table = jnp.sin(angles)[:, None, :]
    leading = heads_in[..., :halfway]
    trailing = heads_in[..., halfway:]
    return jnp.concatenate(
        [
            leading * cosine_table - trailing * sine_table,
            trailing * cosine_table + leading * sine_table,
        ],
        -1,
    )


def summed_rows(term_task, own_rows):
    return lax.psum_scatter(
        term_task(jnp.int32(0), own_rows * lax.axis_size("tp")),
        "tp",
        scatter_dimension=0,
        tiled=True,
    )


def causal_attention(
    group_query, group_positions, key_flat, value_rows, block_lengths, rows_per_block, head_count
):
    groups_total = group_query.shape[0]
    group_rows = group_query.shape[1]
    block_total = block_lengths.shape[0]
    score_scale = 1.0 / math.sqrt(HEAD)
    latest = jnp.max(group_positions, 1)
    initial = tuple(
        (
            (
                jnp.full((head_count, group_rows), MASKED_SCORE, jnp.float32),
                jnp.zeros((head_count, group_rows), jnp.float32),
                jnp.zeros((head_count, group_rows, HEAD), jnp.float32),
            )
            for member in range(groups_total)
        )
    )
    carried = initial
    key_piece = lax.all_gather(key_flat, "seq", axis=0, tiled=True)
    value_piece = lax.all_gather(value_rows, "seq", axis=0, tiled=True)
    length = key_piece.shape[0]
    block_span = math.gcd(length, KEY_SPAN)
    step_total = length // block_span
    key_steps = key_piece.reshape(step_total, block_span, head_count, HEAD)
    value_steps = value_piece.reshape(step_total, block_span, head_count, HEAD)

    def advance(running, inputs):
        key_block, value_block, step_index = inputs
        first_key = step_index * block_span
        key_positions = first_key + jnp.arange(block_span, dtype=jnp.int32)
        owners = key_positions // rows_per_block
        limits = jnp.sum(
            jnp.where(
                owners[:, None] == jnp.arange(block_total, dtype=jnp.int32)[None, :],
                block_lengths[None, :],
                0,
            ),
            1,
        )
        usable = key_positions - owners * rows_per_block < limits
        updated = []
        for member in range(groups_total):

            def refresh(status, member=member):
                highest, weight_sum, weighted = status
                scores = (
                    jnp.einsum(
                        "qhd,khd->hqk",
                        group_query[member],
                        key_block,
                        preferred_element_type=jnp.float32,
                    )
                    * score_scale
                )
                allowed = (key_positions[None, :] <= group_positions[member][:, None]) & usable[
                    None, :
                ]
                scores = jnp.where(allowed[None], scores, MASKED_SCORE)
                new_highest = jnp.maximum(highest, jnp.max(scores, -1))
                weights = jnp.where(allowed[None], jnp.exp(scores - new_highest[..., None]), 0.0)
                factor = jnp.exp(highest - new_highest)
                weight_sum = weight_sum * factor + jnp.sum(weights, -1)
                weighted = weighted * factor[..., None] + jnp.einsum(
                    "hqk,khd->hqd",
                    weights.astype(jnp.bfloat16),
                    value_block,
                    preferred_element_type=jnp.float32,
                )
                return (new_highest, weight_sum, weighted)

            def unchanged(status):
                return status

            updated.append(
                lax.cond(first_key <= latest[member], refresh, unchanged, running[member])
            )
        return (tuple(updated), None)

    carried, ignored = lax.scan(
        advance, carried, (key_steps, value_steps, jnp.arange(step_total, dtype=jnp.int32))
    )
    outputs = []
    for member in range(groups_total):
        highest, weight_sum, weighted = carried[member]
        mixture = weighted / weight_sum[..., None]
        outputs.append(
            jnp.transpose(mixture, (1, 0, 2))
            .reshape(group_rows, head_count * HEAD)
            .astype(jnp.bfloat16)
        )
    return jnp.stack(outputs)


def shards(
    pixels,
    text_rows,
    patch_counts,
    picture_starts,
    block_lengths,
    vision_gain,
    vision_project,
    vision_output,
    merge_gain,
    merge_weight,
    text_gain,
    text_project,
    text_output,
):
    seq_ways = lax.axis_size("seq")
    tp_ways = lax.axis_size("tp")
    seq_index = lax.axis_index("seq")
    tp_index = lax.axis_index("tp")
    picture_total, local_patches, model_width = pixels.shape
    patch_total = local_patches * tp_ways
    local_width = vision_project.shape[2]
    head_count = local_width // HEAD
    patch_normed = layer_normed(pixels, vision_gain).astype(jnp.bfloat16)
    packed_project = vision_project.reshape(model_width, 3 * local_width)
    projected = jnp.einsum(
        "npd,de->npe",
        lax.all_gather(patch_normed, "tp", axis=1, tiled=True),
        packed_project,
        preferred_element_type=jnp.float32,
    ).astype(jnp.bfloat16)
    queries = projected[..., :local_width].reshape(picture_total, patch_total, head_count, HEAD)
    key_heads = projected[..., local_width : 2 * local_width].reshape(
        picture_total, patch_total, head_count, HEAD
    )
    value_heads = projected[..., 2 * local_width :].reshape(
        picture_total, patch_total, head_count, HEAD
    )
    live_counts = lax.dynamic_slice_in_dim(
        patch_counts, seq_index * picture_total, picture_total, 0
    )
    score_scale = 1.0 / math.sqrt(HEAD)
    scores = (
        jnp.einsum("nqhd,nkhd->nhqk", queries, key_heads, preferred_element_type=jnp.float32)
        * score_scale
    )
    allowed = (jnp.arange(patch_total, dtype=jnp.int32)[None, :] < live_counts[:, None])[
        :, None, None, :
    ]
    scores = jnp.where(allowed, scores, MASKED_SCORE)
    highest = jnp.max(scores, -1, keepdims=True)
    weights = jnp.where(allowed, jnp.exp(scores - highest), 0.0)
    mixture = jnp.einsum(
        "nhqk,nkhd->nqhd",
        weights.astype(jnp.bfloat16),
        value_heads,
        preferred_element_type=jnp.float32,
    )
    mixture = mixture / jnp.transpose(jnp.sum(weights, -1), (0, 2, 1))[..., None]
    attended = mixture.astype(jnp.bfloat16).reshape(picture_total, patch_total, local_width)
    patch_major = jnp.transpose(attended, (1, 0, 2)).reshape(
        patch_total * picture_total, local_width
    )

    def vision_term(offset, row_count):
        return jnp.dot(patch_major, vision_output, preferred_element_type=jnp.float32)

    vision_sum = summed_rows(vision_term, local_patches * picture_total)
    vision_sum = jnp.transpose(
        vision_sum.reshape(local_patches, picture_total, model_width), (1, 0, 2)
    )
    vision_rows = (pixels.astype(jnp.float32) + vision_sum).astype(jnp.bfloat16)
    merge_input = layer_normed(vision_rows, merge_gain).astype(jnp.bfloat16)
    merged_total = patch_total // 4
    input_share = merge_weight.shape[0]
    whole_pictures = lax.all_gather(merge_input, "tp", axis=1, tiled=True)
    merged_rows = whole_pictures.reshape(picture_total * merged_total, 4 * model_width)
    owned_inputs = lax.dynamic_slice_in_dim(merged_rows, tp_index * input_share, input_share, 1)

    def merge_term(offset, row_count):
        return jnp.dot(owned_inputs, merge_weight, preferred_element_type=jnp.float32)

    part_rows = picture_total * merged_total // tp_ways
    visual_part = summed_rows(merge_term, part_rows).astype(jnp.bfloat16)
    rows_per_block = text_rows.shape[0] * tp_ways
    start_table = picture_starts.reshape(seq_ways, picture_total)
    dest_table = start_table // rows_per_block
    picture_rank = tp_index * part_rows // merged_total
    rank_dest = jnp.sum(
        jnp.where(
            jnp.arange(picture_total, dtype=jnp.int32)[None, :] == picture_rank, dest_table, 0
        ),
        1,
    )
    senders = rank_dest == seq_index
    segment = lax.all_gather(visual_part, "seq", axis=0, tiled=True)
    row_count = segment.shape[0]
    sources = jnp.arange(row_count, dtype=jnp.int32) // part_rows
    wanted = jnp.any(
        (sources[:, None] == jnp.arange(seq_ways, dtype=jnp.int32)[None, :]) & senders[None, :], 1
    )
    selector = (
        (jnp.arange(row_count, dtype=jnp.int32) % part_rows)[None, :]
        == jnp.arange(part_rows, dtype=jnp.int32)[:, None]
    ) & wanted[None, :]
    arrived = jnp.dot(
        selector.astype(jnp.bfloat16), segment, preferred_element_type=jnp.float32
    ).astype(jnp.bfloat16)
    text_block, visual_block = (
        lax.all_gather(text_rows, "tp", axis=0, tiled=True),
        lax.all_gather(arrived, "tp", axis=0, tiled=True),
    )
    landed = dest_table == seq_index
    local_starts = jnp.sum(jnp.where(landed, start_table - seq_index * rows_per_block, 0), 0)
    live_groups = jnp.sum(
        jnp.where(landed, patch_counts.reshape(seq_ways, picture_total) // 4, 0), 0
    )
    slot_index = jnp.arange(merged_total, dtype=jnp.int32)
    targets = (local_starts[:, None] + slot_index[None, :]).reshape(-1)
    in_use = (slot_index[None, :] < live_groups[:, None]).reshape(-1)
    placement = (jnp.arange(rows_per_block, dtype=jnp.int32)[:, None] == targets[None, :]) & in_use[
        None, :
    ]
    covered = jnp.any(placement, 1)
    placed = jnp.dot(
        placement.astype(jnp.bfloat16), visual_block, preferred_element_type=jnp.float32
    ).astype(jnp.bfloat16)
    embedded = jnp.where(covered[:, None], placed, text_block)
    text_normed = rms_normed(embedded, text_gain).astype(jnp.bfloat16)
    text_heads = jnp.dot(
        text_normed,
        text_project.reshape(model_width, 3 * local_width),
        preferred_element_type=jnp.float32,
    )
    positions = seq_index * rows_per_block + jnp.arange(rows_per_block, dtype=jnp.int32)
    query_rows = rotary(
        text_heads[:, :local_width].reshape(rows_per_block, head_count, HEAD), positions
    ).astype(jnp.bfloat16)
    key_rows = rotary(
        text_heads[:, local_width : 2 * local_width].reshape(rows_per_block, head_count, HEAD),
        positions,
    ).astype(jnp.bfloat16)
    value_rows = text_heads[:, 2 * local_width :].astype(jnp.bfloat16)
    key_flat = key_rows.reshape(rows_per_block, local_width)
    halfway = rows_per_block // 2
    group_query = query_rows.reshape(2, halfway, head_count, HEAD)
    group_positions = positions.reshape(2, halfway)
    results = causal_attention(
        group_query,
        group_positions,
        key_flat,
        value_rows,
        block_lengths,
        rows_per_block,
        head_count,
    )
    attended_rows = results.reshape(rows_per_block, local_width)
    own_rows = text_rows.shape[0]

    def text_term(offset, row_count):
        return jnp.dot(attended_rows, text_output, preferred_element_type=jnp.float32)

    text_sum = summed_rows(text_term, own_rows)
    residual = lax.dynamic_slice_in_dim(embedded, tp_index * own_rows, own_rows, 0)
    hidden = (residual.astype(jnp.float32) + text_sum).astype(jnp.bfloat16)
    return (hidden, key_flat, value_rows)


def solution(mesh):
    placed = (
        P("seq", "tp", None),
        P(("seq", "tp"), None),
        P(),
        P(),
        P(),
        P(),
        P(None, None, "tp"),
        P("tp", None),
        P(),
        P("tp", None),
        P(),
        P(None, None, "tp"),
        P("tp", None),
    )
    return jax.shard_map(
        shards,
        mesh=mesh,
        in_specs=placed,
        out_specs=(P(("seq", "tp"), None), P("seq", "tp"), P("seq", "tp")),
        check_vma=False,
    )
```

profile of v0, /device:TPU:223, one launch (start us, length us, event | category | flops | bytes accessed | tf_op | source)
XLA Modules:
  0.0 783.0 jit_solution(2109778435494565102)
XLA Ops:
  9.6 1.8 fusion.47
  12.2 36.6 %all-gather.7.cloned.1.call-done = bf16[2,256,1664]{2,1,0:T(8,128)(2,1)} async-done(((bf16[2,32,1664]{2,1,0:T(8,128)(2,1)}), bf16[2,256,1664]{2,1,0:T(8,128)(2,1)}) %all-gather.7.cloned.1.call-update) | async-done | bytes 1703952 | tf_op jit(solution)/shard_map/all_gather | solution.py:176
  48.9 3.4 convolution_convert_fusion.2
  54.3 1.9 fusion.39
  56.7 3.5 fusion.90
  60.2 51.1 %reduce-scatter.4.cloned.1.call-done = f32[64,1664]{1,0:T(8,128)} async-done(((f32[512,1664]{1,0:T(8,128)}), f32[64,1664]{1,0:T(8,128)}) %reduce-scatter.4.cloned.1.call-update) | async-done | bytes 426000 | tf_op jit(solution)/shard_map/reduce_scatter | solution.py:47
  113.8 41.2 %all-gather.9.cloned.1.call-done = bf16[2,256,1664]{2,1,0:T(8,128)(2,1)} async-done(((bf16[2,32,1664]{2,1,0:T(8,128)(2,1)}), bf16[2,256,1664]{2,1,0:T(8,128)(2,1)}) %all-gather.9.cloned.1.call-update) | async-done | bytes 1703952 | tf_op jit(solution)/shard_map/all_gather | solution.py:224
  155.0 3.9 reshape.388
  158.9 2.6 fusion.55
  161.6 40.2 %reduce-scatter.6.cloned.1.call-done = f32[16,1664]{1,0:T(8,128)} async-done(((f32[128,1664]{1,0:T(8,128)}), f32[16,1664]{1,0:T(8,128)}) %reduce-scatter.6.cloned.1.call-update) | async-done | bytes 106512 | tf_op jit(solution)/shard_map/reduce_scatter | solution.py:47
  205.4 56.5 %all-gather.11.cloned.1.call-done = bf16[512,1664]{1,0:T(8,128)(2,1)} async-done(((bf16[16,1664]{1,0:T(8,128)(2,1)}), bf16[512,1664]{1,0:T(8,128)(2,1)}) %all-gather.11.cloned.1.call-update) | async-done | bytes 1703952 | tf_op jit(solution)/shard_map/all_gather | solution.py:244
  261.9 1.8 convolution_convert_fusion.1
  263.7 24.1 %all_gather.24 = bf16[128,1664]{1,0:T(8,128)(2,1)S(1)} all-gather(bf16[16,1664]{1,0:T(8,128)(2,1)S(1)} %convolution_convert_fusion.1), channel_id=1, replica_groups=mesh['seq'=32,'tp'=8] {'tp'}, dimensions={0}, use_global_device_ids=true | all-gather | bytes 479232 | tf_op jit(solution)/shard_map/all_gather | solution.py:259
  287.8 13.2 %all-gather.13.cloned.1.call-done = bf16[512,1664]{1,0:T(8,128)(2,1)} async-done(((bf16[64,1664]{1,0:T(8,128)(2,1)}), bf16[512,1664]{1,0:T(8,128)(2,1)}) %all-gather.13.cloned.1.call-update) | async-done | bytes 1703952 | tf_op jit(solution)/shard_map/all_gather | solution.py:258
  301.0 2.4 fusion.26
  307.9 1.7 slice.86
  310.5 79.0 %all-gather.15.cloned.1.call-done = bf16[16384,208]{0,1:T(8,128)(2,1)} async-done(((bf16[512,208]{0,1:T(8,128)(2,1)}), bf16[16384,208]{0,1:T(8,128)(2,1)}) %all-gather.15.cloned.1.call-update) | async-done | bytes 6815760 | tf_op jit(solution)/shard_map/all_gather | solution.py:74
  389.4 5.9 copy.50
  395.4 6.7 copy.40
  402.1 66.7 %all-gather.17.cloned.1.call-done = bf16[16384,208]{0,1:T(8,128)(2,1)} async-done(((bf16[512,208]{0,1:T(8,128)(2,1)}), bf16[16384,208]{0,1:T(8,128)(2,1)}) %all-gather.17.cloned.1.call-update) | async-done | bytes 6815760 | tf_op jit(solution)/shard_map/all_gather | solution.py:75
  468.8 5.9 copy.51
  474.7 7.0 copy.41
  481.8 245.2 %while.23 = (s32[]{:T(128)}, f32[2,256]{1,0:T(2,128)S(1)}, f32[2,256]{1,0:T(2,128)S(1)}, f32[2,256,104]{1,2,0:T(8,128)S(1)}, f32[2,256]{1,0:T(2,128)S(1)}, /*ind...) while((s32[]{:T(128)}, f32[2,256]{1,0:T(2,128)S(1)}, ...), condition=%wide.region_25.26_spmd.clone, body=%wide.region_15.25_spmd.clone.sunk | while | flops 223629824 | bytes 10199145 | solution.py:134
  485.7 1.6 conditional.7
  501.0 1.6 conditional.7
  524.0 1.6 conditional.7
  531.6 1.6 conditional.7
  539.3 1.6 conditional.7
  554.6 1.6 conditional.7
  562.3 1.6 conditional.7
  569.9 1.6 conditional.7
  577.6 1.6 conditional.7
  592.9 1.6 conditional.7
  600.6 1.6 conditional.7
  608.3 1.6 conditional.7
  615.9 1.6 conditional.7
  631.2 1.6 conditional.7
  638.9 1.6 conditional.7
  646.6 1.6 conditional.7
  654.2 1.6 conditional.7
  677.2 1.6 conditional.7
  684.9 1.6 conditional.7
  692.5 1.6 conditional.7
  715.5 1.6 conditional.7
  723.2 1.6 conditional.7
  728.1 2.4 fusion.91
  730.5 44.2 %reduce-scatter.8.cloned.1.call-done = f32[64,1664]{1,0:T(8,128)} async-done(((f32[512,1664]{1,0:T(8,128)}), f32[64,1664]{1,0:T(8,128)}) %reduce-scatter.8.cloned.1.call-update) | async-done | bytes 426000 | tf_op jit(solution)/shard_map/reduce_scatter | solution.py:47
  774.7 1.8 add_convert_fusion
  (879 shorter events, 262.2 us)
Async XLA Ops:
  7.2 151.8 %copy-start = (bf16[832,1664]{1,0:T(8,128)(2,1)S(1)}, bf16[832,1664]{1,0:T(8,128)(2,1)}, u32[]{:S(2)}) copy-start(bf16[832,1664]{1,0:T(8,128)(2,1)} %param.28) | copy-start | bytes 8306692
  7.2 41.7 %all-gather.7.cloned.1.call-start = ((), (), s32[]{:S(2)}) async-start(), calls=%async_computation.3 | async-start | bytes 1916928 | tf_op jit(solution)/shard_map/all_gather | solution.py:176
  11.4 99.9 %reduce-scatter.4.cloned.1.call-start = ((), (), s32[]{:S(2)}) async-start(), calls=%async_computation.4 | async-start | bytes 3833856 | tf_op jit(solution)/shard_map/reduce_scatter | solution.py:47
  60.1 52.4 %copy-start.2 = (bf16[2,32,1664]{2,1,0:T(8,128)(2,1)S(1)}, bf16[2,32,1664]{2,1,0:T(8,128)(2,1)}, u32[]{:S(2)}) copy-start(bf16[2,32,1664]{2,1,0:T(8,128)(2,1)} %param.19) | copy-start | bytes 638980
  60.1 52.8 %copy-start.7 = (f32[1664]{0:T(1024)S(1)}, f32[1664]{0:T(1024)}, u32[]{:S(2)}) copy-start(f32[1664]{0:T(1024)} %param.27) | copy-start | bytes 19972
  60.1 94.9 %all-gather.9.cloned.1.call-start = ((), (), s32[]{:S(2)}) async-start(), calls=%async_computation.5 | async-start | bytes 1916928 | tf_op jit(solution)/shard_map/all_gather | solution.py:224
  113.8 88.0 %reduce-scatter.6.cloned.1.call-start = ((), (), s32[]{:S(2)}) async-start(), calls=%async_computation.6 | async-start | bytes 958464 | tf_op jit(solution)/shard_map/reduce_scatter | solution.py:47
  158.9 45.0 %copy-start.8 = (s32[64]{0:T(128)S(1)}, s32[64]{0:T(128)}, u32[]{:S(2)}) copy-start(s32[64]{0:T(128)} %param.21) | copy-start | bytes 772
  158.9 45.1 %copy-start.9 = (s32[64]{0:T(128)S(1)}, s32[64]{0:T(128)}, u32[]{:S(2)}) copy-start(s32[64]{0:T(128)} %param.22) | copy-start | bytes 772
  161.5 100.4 %all-gather.11.cloned.1.call-start = ((), (), s32[]{:S(2)}) async-start(), calls=%async_computation.7 | async-start | bytes 1757184 | tf_op jit(solution)/shard_map/all_gather | solution.py:244
  203.3 97.6 %all-gather.13.cloned.1.call-start = ((), (), s32[]{:S(2)}) async-start(), calls=%async_computation.8 | async-start | bytes 1916928 | tf_op jit(solution)/shard_map/all_gather | solution.py:258
  203.9 185.6 %all-gather.15.cloned.1.call-start = ((), (), s32[]{:S(2)}) async-start(), calls=%async_computation.9 | async-start | bytes 7028736 | tf_op jit(solution)/shard_map/all_gather | solution.py:74
  287.8 15.7 %copy-start.11 = (f32[1664]{0:T(1024)S(1)}, f32[1664]{0:T(1024)}, u32[]{:S(2)}) copy-start(f32[1664]{0:T(1024)} %param.29) | copy-start | bytes 19972
  301.0 2.5 copy-start.10
  303.4 1.5 copy-start.5
  304.9 1.1 copy-start.3
  307.8 160.9 %all-gather.17.cloned.1.call-start = ((), (), s32[]{:S(2)}) async-start(), calls=%async_computation.10 | async-start | bytes 7028736 | tf_op jit(solution)/shard_map/all_gather | solution.py:75
  309.6 465.1 %reduce-scatter.8.cloned.1.call-start = ((), (), s32[]{:S(2)}) async-start(), calls=%async_computation.11 | async-start | bytes 3833856 | tf_op jit(solution)/shard_map/reduce_scatter | solution.py:47
  474.7 7.1 copy-start.6
  727.0 1.1 copy-start.4
  730.5 46.0 %copy-start.1 = (bf16[832,1664]{1,0:T(8,128)(2,1)S(1)}, bf16[832,1664]{1,0:T(8,128)(2,1)}, u32[]{:S(2)}) copy-start(bf16[832,1664]{1,0:T(8,128)(2,1)} %param.28) | copy-start | bytes 8306692
Sparse Core Ops, SparseCore 0:
  11.5 37.3 all-gather.6
  60.3 50.9 reduce-scatter.3
  113.9 41.0 all-gather.8
  161.6 40.0 reduce-scatter.5
  205.1 56.7 all-gather.10
  263.7 37.2 all-gather.12
  308.0 81.4 all-gather.14
  392.8 75.9 all-gather.16
  730.6 44.0 reduce-scatter.7
where the time goes:
time: 792 us; the launch traced here: 783 us
  waiting for transfers between devices  429 us (54%)
  local copies, waits for them, and re-layouts  113 us (14%)
  matrix products  81.5 us (10%)
  loops' own time  67.3 us (8%)
  other arithmetic  53.2 us (7%)
  blocking collectives  24.1 us (3%)
  between operations  14.3 us (2%)
    reduce_scatter x3, waiting for transfers between devices, summed_rows(): lax.psum_scatter(term_task(jnp.int32(0), own_rows * lax.axis_size('tp')),...  135 us
    all_gather x1, waiting for transfers between devices, causal_attention(): key_piece = lax.all_gather(key_flat, 'seq', axis=0, tiled=True)  79 us
    all_gather x1, waiting for transfers between devices, causal_attention(): value_piece = lax.all_gather(value_rows, 'seq', axis=0, tiled=True)  66.7 us
    another operation x1, loops' own time, causal_attention(): lax.scan(advance, carried, (key_steps, value_steps, jnp.arange(step_total...  64.4 us
    all_gather x1, waiting for transfers between devices, shards(): segment = lax.all_gather(visual_part, 'seq', axis=0, tiled=True)  56.5 us
    all_gather x1, waiting for transfers between devices, shards(): whole_pictures = lax.all_gather(merge_input, 'tp', axis=1, tiled=True)  41.2 us
    all_gather x1, waiting for transfers between devices, shards(): lax.all_gather(patch_normed, 'tp', axis=1, tiled=True)  36.6 us
    squeeze x32, local copies, waits for them, and re-layouts, causal_attention(): lax.scan(advance, carried, (key_steps, value_steps, jnp.arange(step_total...  34.2 us
  transfers between devices with their start and end apart: 9, of which 9 were waited for; matrix products, arithmetic and copies ran while one was open for 2% of the time, Pallas kernels for 0%

commit v1 on v0

--- a/solution.py
+++ b/solution.py
@@ -3,6 +3,8 @@
 import jax
 import jax.numpy as jnp
 from jax import lax
+from jax.experimental import pallas as pl
+from jax.experimental.pallas import tpu as pltpu
 from jax.sharding import PartitionSpec as P
 
 HEAD = 104
@@ -52,98 +54,92 @@
     )
 
 
-def causal_attention(
-    group_query, group_positions, key_flat, value_rows, block_lengths, rows_per_block, head_count
-):
-    groups_total = group_query.shape[0]
-    group_rows = group_query.shape[1]
-    block_total = block_lengths.shape[0]
+def attention_kernel(meta_ref, lengths_ref, q_ref, k_ref, v_ref, o_ref, m_sc, l_sc, acc_sc):
+    step = pl.program_id(0)
+    seq = meta_ref[0]
+    rows, width = q_ref.shape
+    span = k_ref.shape[0]
+    heads = width // HEAD
     score_scale = 1.0 / math.sqrt(HEAD)
-    latest = jnp.max(group_positions, 1)
-    initial = tuple(
-        (
-            (
-                jnp.full((head_count, group_rows), MASKED_SCORE, jnp.float32),
-                jnp.zeros((head_count, group_rows), jnp.float32),
-                jnp.zeros((head_count, group_rows, HEAD), jnp.float32),
+
+    @pl.when(step == 0)
+    def _():
+        m_sc[...] = jnp.full(m_sc.shape, MASKED_SCORE, jnp.float32)
+        l_sc[...] = jnp.zeros(l_sc.shape, jnp.float32)
+        acc_sc[...] = jnp.zeros(acc_sc.shape, jnp.float32)
+
+    @pl.when(step <= seq)
+    def _():
+        q = q_ref[...]
+        k = k_ref[...]
+        v = v_ref[...]
+        column = lax.broadcasted_iota(jnp.int32, (rows, width), 1)
+        query_pos = seq * rows + lax.broadcasted_iota(jnp.int32, (rows, span), 0)
+        key_index = lax.broadcasted_iota(jnp.int32, (rows, span), 1)
+        allowed = (step * span + key_index <= query_pos) & (key_index < lengths_ref[step])
+        for h in range(heads):
+            in_head = (column >= h * HEAD) & (column < (h + 1) * HEAD)
+            q_head = jnp.where(in_head, q, jnp.zeros_like(q))
+            scores = (
+                lax.dot_general(
+                    q_head, k, (((1,), (1,)), ((), ())), preferred_element_type=jnp.float32
+                )
+                * score_scale
             )
-            for member in range(groups_total)
-        )
-    )
-    carried = initial
-    key_piece = lax.all_gather(key_flat, "seq", axis=0, tiled=True)
-    value_piece = lax.all_gather(value_rows, "seq", axis=0, tiled=True)
-    length = key_piece.shape[0]
-    block_span = math.gcd(length, KEY_SPAN)
-    step_total = length // block_span
-    key_steps = key_piece.reshape(step_total, block_span, head_count, HEAD)
-    value_steps = value_piece.reshape(step_total, block_span, head_count, HEAD)
-
-    def advance(running, inputs):
-        key_block, value_block, step_index = inputs
-        first_key = step_index * block_span
-        key_positions = first_key + jnp.arange(block_span, dtype=jnp.int32)
-        owners = key_positions // rows_per_block
-        limits = jnp.sum(
-            jnp.where(
-                owners[:, None] == jnp.arange(block_total, dtype=jnp.int32)[None, :],
-                block_lengths[None, :],
-                0,
-            ),
-            1,
-        )
-        usable = key_positions - owners * rows_per_block < limits
-        updated = []
-        for member in range(groups_total):
-
-            def refresh(status, member=member):
-                highest, weight_sum, weighted = status
-                scores = (
-                    jnp.einsum(
-                        "qhd,khd->hqk",
-                        group_query[member],
-                        key_block,
-                        preferred_element_type=jnp.float32,
-                    )
-                    * score_scale
-                )
-                allowed = (key_positions[None, :] <= group_positions[member][:, None]) & usable[
-                    None, :
-                ]
-                scores = jnp.where(allowed[None], scores, MASKED_SCORE)
-                new_highest = jnp.maximum(highest, jnp.max(scores, -1))
-                weights = jnp.where(allowed[None], jnp.exp(scores - new_highest[..., None]), 0.0)
-                factor = jnp.exp(highest - new_highest)
-                weight_sum = weight_sum * factor + jnp.sum(weights, -1)
-                weighted = weighted * factor[..., None] + jnp.einsum(
-                    "hqk,khd->hqd",
-                    weights.astype(jnp.bfloat16),
-                    value_block,
-                    preferred_element_type=jnp.float32,
-                )
-                return (new_highest, weight_sum, weighted)
-
-            def unchanged(status):
-                return status
-
-            updated.append(
-                lax.cond(first_key <= latest[member], refresh, unchanged, running[member])
-            )
-        return (tuple(updated), None)
-
-    carried, ignored = lax.scan(
-        advance, carried, (key_steps, value_steps, jnp.arange(step_total, dtype=jnp.int32))
-    )
-    outputs = []
-    for member in range(groups_total):
-        highest, weight_sum, weighted = carried[member]
-        mixture = weighted / weight_sum[..., None]
-        outputs.append(
-            jnp.transpose(mixture, (1, 0, 2))
-            .reshape(group_rows, head_count * HEAD)
-            .astype(jnp.bfloat16)
-        )
-    return jnp.stack(outputs)
+            scores = jnp.where(allowed, scores, MASKED_SCORE)
+            m_prev = m_sc[h][:, :1]
+            m_new = jnp.maximum(m_prev, jnp.max(scores, axis=1, keepdims=True))
+            weights = jnp.where(allowed, jnp.exp(scores - m_new), 0.0)
+            alpha = jnp.exp(m_prev - m_new)
+            l_new = alpha * l_sc[h][:, :1] + jnp.sum(weights, axis=1, keepdims=True)
+            mixed = jnp.dot(weights.astype(jnp.bfloat16), v, preferred_element_type=jnp.float32)
+            acc_sc[h] = acc_sc[h] * alpha + mixed
+            m_sc[h] = jnp.broadcast_to(m_new, m_sc.shape[1:])
+            l_sc[h] = jnp.broadcast_to(l_new, l_sc.shape[1:])
+
+    @pl.when(step == pl.num_programs(0) - 1)
+    def _():
+        column = lax.broadcasted_iota(jnp.int32, (rows, width), 1)
+        result = jnp.zeros((rows, width), jnp.float32)
+        for h in range(heads):
+            in_head = (column >= h * HEAD) & (column < (h + 1) * HEAD)
+            result = jnp.where(in_head, acc_sc[h] / l_sc[h][:, :1], result)
+        o_ref[...] = result.astype(o_ref.dtype)
+
+
+def causal_attention(query_flat, key_all, value_all, seq_index, block_lengths, rows_per_block):
+    rows, width = query_flat.shape
+    span = rows_per_block
+    steps = key_all.shape[0] // span
+    heads = width // HEAD
+    meta = jnp.reshape(seq_index, (1,)).astype(jnp.int32)
+    grid_spec = pltpu.PrefetchScalarGridSpec(
+        num_scalar_prefetch=2,
+        grid=(steps,),
+        in_specs=[
+            pl.BlockSpec((rows, width), lambda i, m, n: (0, 0)),
+            pl.BlockSpec((span, width), lambda i, m, n: (jnp.minimum(i, m[0]), 0)),
+            pl.BlockSpec((span, width), lambda i, m, n: (jnp.minimum(i, m[0]), 0)),
+        ],
+        out_specs=pl.BlockSpec((rows, width), lambda i, m, n: (0, 0)),
+        scratch_shapes=[
+            pltpu.VMEM((heads, rows, 128), jnp.float32),
+            pltpu.VMEM((heads, rows, 128), jnp.float32),
+            pltpu.VMEM((heads, rows, width), jnp.float32),
+        ],
+    )
+    flops = 4 * heads * rows * key_all.shape[0] * width
+    return pl.pallas_call(
+        attention_kernel,
+        grid_spec=grid_spec,
+        out_shape=jax.ShapeDtypeStruct((rows, width), jnp.bfloat16),
+        compiler_params=pltpu.CompilerParams(dimension_semantics=("arbitrary",)),
+        cost_estimate=pl.CostEstimate(
+            flops=flops,
+            transcendentals=heads * rows * key_all.shape[0],
+            bytes_accessed=2 * key_all.size * 2 + 2 * query_flat.size * 2,
+        ),
+    )(meta, block_lengths, query_flat, key_all, value_all)
 
 
 def shards(
@@ -290,19 +286,16 @@
     ).astype(jnp.bfloat16)
     value_rows = text_heads[:, 2 * local_width :].astype(jnp.bfloat16)
     key_flat = key_rows.reshape(rows_per_block, local_width)
-    halfway = rows_per_block // 2
-    group_query = query_rows.reshape(2, halfway, head_count, HEAD)
-    group_positions = positions.reshape(2, halfway)
-    results = causal_attention(
-        group_query,
-        group_positions,
-        key_flat,
-        value_rows,
+    key_all = lax.all_gather(key_flat, "seq", axis=0, tiled=True)
+    value_all = lax.all_gather(value_rows, "seq", axis=0, tiled=True)
+    attended_rows = causal_attention(
+        query_rows.reshape(rows_per_block, local_width),
+        key_all,
+        value_all,
+        seq_index,
         block_lengths,
         rows_per_block,
-        head_count,
-    )
-    attended_rows = results.reshape(rows_per_block, local_width)
+    )
     own_rows = text_rows.shape[0]
 
     def text_term(offset, row_count):

time: 792 us -> 651 us (0.82)
  Pallas kernels: 0 us -> 117 us
  local copies, waits for them, and re-layouts: 113 us -> 11.2 us
  loops' own time: 67.3 us -> 0 us
  matrix products: 81.5 us -> 22.5 us
  other arithmetic: 53.2 us -> 9.95 us
  waiting for transfers between devices: 429 us -> 444 us
    pallas_call x0 -> x1, Pallas kernels: none -> 117 us  [causal_attention(): pl.pallas_call(attention_kernel, grid_spec=grid_spec, out_shape=jax.Shape...]
    another operation x65 -> x0, loops' own time: 67.3 us -> none  [the longest x1 64.4 us: causal_attention(): lax.scan(advance, carried, (key_steps, value_steps, jnp.arange(step_total...]
    dot_general x128 -> x0, matrix products: 60.1 us -> none  [the longest x64 30.1 us: refresh(): jnp.einsum('qhd,khd->hqk', group_query[member], key_block, preferred_elem...]
    squeeze x32 -> x0, local copies, waits for them, and re-layouts: 34.2 us -> none  [causal_attention(): lax.scan(advance, carried, (key_steps, value_steps, jnp.arange(step_total...]
    reduce_sum x96 -> x0, other arithmetic: 29.2 us -> none  [the longest x64 26.3 us: refresh(): weight_sum = weight_sum * factor + jnp.sum(weights, -1)]
    unnamed x30 -> x23, local copies, waits for them, and re-layouts: 26.8 us -> 1.73 us
    dynamic_slice x32 -> x0, local copies, waits for them, and re-layouts: 21.3 us -> none  [causal_attention(): lax.scan(advance, carried, (key_steps, value_steps, jnp.arange(step_total...]
    slice x98 -> x1, local copies, waits for them, and re-layouts: 20.7 us -> 0.06 us  [shards(): text_heads[:, local_width:2 * local_width]]
  transfers between devices with their start and end apart: 9 -> 9, of which waited for: 9 -> 9; matrix products, arithmetic and copies ran while one was open for 2% -> 1% of each run, Pallas kernels for 0% -> 0%
where the time goes in v1:
time: 651 us; the launch traced here: 643 us
  waiting for transfers between devices  444 us (68%)
  Pallas kernels  117 us (18%)
  blocking collectives  24.1 us (4%)
  matrix products  22.5 us (3%)
  between operations  14.1 us (2%)
  local copies, waits for them, and re-layouts  11.2 us (2%)
  other arithmetic  9.95 us (2%)
    reduce_scatter x3, waiting for transfers between devices, summed_rows(): lax.psum_scatter(term_task(jnp.int32(0), own_rows * lax.axis_size('tp')),...  136 us
    pallas_call x1, Pallas kernels, causal_attention(): pl.pallas_call(attention_kernel, grid_spec=grid_spec, out_shape=jax.Shape...  117 us
    all_gather x1, waiting for transfers between devices, shards(): key_all = lax.all_gather(key_flat, 'seq', axis=0, tiled=True)  80.2 us
    all_gather x1, waiting for transfers between devices, shards(): value_all = lax.all_gather(value_rows, 'seq', axis=0, tiled=True)  79.9 us
    all_gather x1, waiting for transfers between devices, shards(): segment = lax.all_gather(visual_part, 'seq', axis=0, tiled=True)  56.8 us
    all_gather x1, waiting for transfers between devices, shards(): whole_pictures = lax.all_gather(merge_input, 'tp', axis=1, tiled=True)  41 us
    all_gather x1, waiting for transfers between devices, shards(): lax.all_gather(patch_normed, 'tp', axis=1, tiled=True)  36.6 us
    all_gather x1, blocking collectives, shards(): lax.all_gather(arrived, 'tp', axis=0, tiled=True)  24.1 us
  transfers between devices with their start and end apart: 9, of which 9 were waited for; matrix products, arithmetic and copies ran while one was open for 1% of the time, Pallas kernels for 0%

profile of v1, /device:TPU:223, one launch (start us, length us, event | category | flops | bytes accessed | tf_op | source)
XLA Modules:
  0.0 642.8 jit_solution(7804748584833806054)
XLA Ops:
  7.2 1.2 convert_reduce_fusion
  8.4 1.1 fusion.20
  9.6 1.8 fusion.22
  11.4 0.7 dynamic_slice.9
  12.2 36.6 %all-gather.7.cloned.1.call-done = bf16[2,256,1664]{2,1,0:T(8,128)(2,1)} async-done(((bf16[2,32,1664]{2,1,0:T(8,128)(2,1)}), bf16[2,256,1664]{2,1,0:T(8,128)(2,1)}) %all-gather.7.cloned.1.call-update) | async-done | bytes 1703952 | tf_op jit(solution)/shard_map/all_gather | solution.py:172
  48.9 3.4 convolution_convert_fusion.2
  52.4 0.6 fusion.59
  52.9 1.3 fusion.12
  54.3 1.9 fusion.14
  56.2 0.2 copy.39
  56.4 0.2 reshape.234
  56.7 3.5 fusion.60
  60.2 51.3 %reduce-scatter.4.cloned.1.call-done = f32[64,1664]{1,0:T(8,128)} async-done(((f32[512,1664]{1,0:T(8,128)}), f32[64,1664]{1,0:T(8,128)}) %reduce-scatter.4.cloned.1.call-update) | async-done | bytes 426000 | tf_op jit(solution)/shard_map/reduce_scatter | solution.py:49
  111.5 1.3 reshape.235
  112.7 0.1 convert_reduce_fusion.1
  112.9 0.2 fusion.23
  113.1 0.8 fusion.25
  114.0 41.0 %all-gather.9.cloned.1.call-done = bf16[2,256,1664]{2,1,0:T(8,128)(2,1)} async-done(((bf16[2,32,1664]{2,1,0:T(8,128)(2,1)}), bf16[2,256,1664]{2,1,0:T(8,128)(2,1)}) %all-gather.9.cloned.1.call-update) | async-done | bytes 1703952 | tf_op jit(solution)/shard_map/all_gather | solution.py:220
  155.0 3.9 reshape.236
  158.9 2.6 fusion.30
  161.5 39.9 %reduce-scatter.6.cloned.1.call-done = f32[16,1664]{1,0:T(8,128)} async-done(((f32[128,1664]{1,0:T(8,128)}), f32[16,1664]{1,0:T(8,128)}) %reduce-scatter.6.cloned.1.call-update) | async-done | bytes 106512 | tf_op jit(solution)/shard_map/reduce_scatter | solution.py:49
  201.5 1.5 convert_element_type.75
  203.1 0.5 all-gather.13.cloned.1.call-update
  203.6 0.1 reshape.228
  203.8 0.1 reshape.227
  203.9 0.1 fusion.41
  204.4 0.1 fusion.35
  204.5 0.1 fusion.29
  204.6 0.5 multiply_cosine_fusion
  205.1 56.8 %all-gather.11.cloned.1.call-done = bf16[512,1664]{1,0:T(8,128)(2,1)} async-done(((bf16[16,1664]{1,0:T(8,128)(2,1)}), bf16[512,1664]{1,0:T(8,128)(2,1)}) %all-gather.11.cloned.1.call-update) | async-done | bytes 1703952 | tf_op jit(solution)/shard_map/all_gather | solution.py:240
  261.9 1.8 convolution_convert_fusion.1
  263.7 24.1 %all_gather.24 = bf16[128,1664]{1,0:T(8,128)(2,1)S(1)} all-gather(bf16[16,1664]{1,0:T(8,128)(2,1)S(1)} %convolution_convert_fusion.1), channel_id=1, replica_groups=mesh['seq'=32,'tp'=8] {'tp'}, dimensions={0}, use_global_device_ids=true | all-gather | bytes 479232 | tf_op jit(solution)/shard_map/all_gather | solution.py:255
  287.7 13.2 %all-gather.13.cloned.1.call-done = bf16[512,1664]{1,0:T(8,128)(2,1)} async-done(((bf16[64,1664]{1,0:T(8,128)(2,1)}), bf16[512,1664]{1,0:T(8,128)(2,1)}) %all-gather.13.cloned.1.call-update) | async-done | bytes 1703952 | tf_op jit(solution)/shard_map/all_gather | solution.py:254
  301.0 2.4 fusion.1
  303.4 1.5 fusion.5
  305.0 0.2 subtract_convert_fusion
  305.2 0.8 copy-done.2
  306.1 0.8 copy.41
  307.0 1.0 slice.60
  308.0 0.8 copy.46
  308.9 0.2 reduce-scatter.8.cloned.1.call-start
  309.1 0.8 copy.43.q_ref
  309.9 80.2 %all-gather.15.cloned.1.call-done.k_ref = bf16[16384,208]{1,0:T(8,128)(2,1)} async-done(((bf16[512,208]{1,0:T(8,128)(2,1)}), bf16[16384,208]{1,0:T(8,128)(2,1)}) %all-gather.15.cloned.1.call-update) | async-done | bytes 6815760 | tf_op jit(solution)/shard_map/all_gather | solution.py:289
  390.1 79.9 %all-gather.17.cloned.1.call-done.v_ref = bf16[16384,208]{1,0:T(8,128)(2,1)} async-done(((bf16[512,208]{1,0:T(8,128)(2,1)}), bf16[16384,208]{1,0:T(8,128)(2,1)}) %all-gather.17.cloned.1.call-update) | async-done | bytes 6815760 | tf_op jit(solution)/shard_map/all_gather | solution.py:290
  470.1 116.5 %shard_map.148 = bf16[512,208]{1,0:T(8,128)(2,1)} custom-call(s32[1]{0:T(128)} %bitcast.10.meta_ref, s32[32]{0:T(128)} %lengths_ref.1, bf16[512,208]{1,0:T(8,128)(2,1)} %copy.43.q_ref, bf16[16384,208]{1,0:T(8,128)(2,1)} %all-gather.15.cloned.1.call-done.k_ref, bf16[16384,208]{1,0:T(8,128)(2,1)} %all-gather.17.cloned.1.call-done.v_ref), custom_call_target="tpu_custom_call" | custom-call | flops 13958643712 | bytes 14057472 | tf_op jit(solution)/shard_map/pallas_call | solution.py:132
  586.6 3.5 fusion.61
  590.2 44.3 %reduce-scatter.8.cloned.1.call-done = f32[64,1664]{1,0:T(8,128)} async-done(((f32[512,1664]{1,0:T(8,128)}), f32[64,1664]{1,0:T(8,128)}) %reduce-scatter.8.cloned.1.call-update) | async-done | bytes 426000 | tf_op jit(solution)/shard_map/reduce_scatter | solution.py:49
  634.5 1.8 add_convert_fusion
  (56 shorter events, 1.1 us)
Async XLA Ops:
  7.2 151.7 %copy-start = (bf16[832,1664]{1,0:T(8,128)(2,1)S(1)}, bf16[832,1664]{1,0:T(8,128)(2,1)}, u32[]{:S(2)}) copy-start(bf16[832,1664]{1,0:T(8,128)(2,1)} %param.22) | copy-start | bytes 8306692
  7.2 41.7 %all-gather.7.cloned.1.call-start = ((), (), s32[]{:S(2)}) async-start(), calls=%async_computation.3 | async-start | bytes 1916928 | tf_op jit(solution)/shard_map/all_gather | solution.py:172
  11.4 100.1 %reduce-scatter.4.cloned.1.call-start = ((), (), s32[]{:S(2)}) async-start(), calls=%async_computation.4 | async-start | bytes 3833856 | tf_op jit(solution)/shard_map/reduce_scatter | solution.py:49
  60.1 52.6 %copy-start.1 = (bf16[2,32,1664]{2,1,0:T(8,128)(2,1)S(1)}, bf16[2,32,1664]{2,1,0:T(8,128)(2,1)}, u32[]{:S(2)}) copy-start(bf16[2,32,1664]{2,1,0:T(8,128)(2,1)} %param.13) | copy-start | bytes 638980
  60.1 53.0 %copy-start.6 = (f32[1664]{0:T(1024)S(1)}, f32[1664]{0:T(1024)}, u32[]{:S(2)}) copy-start(f32[1664]{0:T(1024)} %param.21) | copy-start | bytes 19972
  60.1 94.9 %all-gather.9.cloned.1.call-start = ((), (), s32[]{:S(2)}) async-start(), calls=%async_computation.5 | async-start | bytes 1916928 | tf_op jit(solution)/shard_map/all_gather | solution.py:220
  114.0 87.5 %reduce-scatter.6.cloned.1.call-start = ((), (), s32[]{:S(2)}) async-start(), calls=%async_computation.6 | async-start | bytes 958464 | tf_op jit(solution)/shard_map/reduce_scatter | solution.py:49
  158.9 44.8 %copy-start.7 = (s32[64]{0:T(128)S(1)}, s32[64]{0:T(128)}, u32[]{:S(2)}) copy-start(s32[64]{0:T(128)} %param.15) | copy-start | bytes 772
  158.9 44.9 %copy-start.8 = (s32[64]{0:T(128)S(1)}, s32[64]{0:T(128)}, u32[]{:S(2)}) copy-start(s32[64]{0:T(128)} %param.16) | copy-start | bytes 772
  161.5 100.4 %all-gather.11.cloned.1.call-start = ((), (), s32[]{:S(2)}) async-start(), calls=%async_computation.7 | async-start | bytes 1757184 | tf_op jit(solution)/shard_map/all_gather | solution.py:240
  203.0 97.9 %all-gather.13.cloned.1.call-start = ((), (), s32[]{:S(2)}) async-start(), calls=%async_computation.8 | async-start | bytes 1916928 | tf_op jit(solution)/shard_map/all_gather | solution.py:254
  203.6 186.5 %all-gather.15.cloned.1.call-start = ((), (), s32[]{:S(2)}) async-start(), calls=%async_computation.9 | async-start | bytes 8650752 | tf_op jit(solution)/shard_map/all_gather | solution.py:289
  287.7 15.7 %copy-start.10 = (f32[1664]{0:T(1024)S(1)}, f32[1664]{0:T(1024)}, u32[]{:S(2)}) copy-start(f32[1664]{0:T(1024)} %param.23) | copy-start | bytes 19972
  300.9 2.5 copy-start.9
  303.4 1.5 copy-start.5
  304.9 1.2 copy-start.2
  306.1 280.5 %copy-start.3 = (bf16[512,2,104]{0,2,1:T(8,128)(2,1)}, bf16[512,2,104]{0,2,1:T(8,128)(2,1)S(1)}, u32[]{:S(2)}) copy-start(bf16[512,2,104]{0,2,1:T(8,128)(2,1)S(1)} %get-tuple-element.36) | copy-start | bytes 638980
  306.9 163.1 %all-gather.17.cloned.1.call-start = ((), (), s32[]{:S(2)}) async-start(), calls=%async_computation.10 | async-start | bytes 8650752 | tf_op jit(solution)/shard_map/all_gather | solution.py:290
  308.0 278.6 %copy-start.4 = (bf16[512,208]{0,1:T(8,128)(2,1)}, bf16[512,208]{0,1:T(8,128)(2,1)S(1)}, u32[]{:S(2)}) copy-start(bf16[512,208]{0,1:T(8,128)(2,1)S(1)} %slice.60) | copy-start | bytes 638980
  308.9 325.6 %reduce-scatter.8.cloned.1.call-start = ((), (), s32[]{:S(2)}) async-start(), calls=%async_computation.11 | async-start | bytes 3833856 | tf_op jit(solution)/shard_map/reduce_scatter | solution.py:49
Sparse Core Ops, SparseCore 0:
  11.5 37.3 all-gather.6
  60.3 51.1 reduce-scatter.3
  114.1 40.8 all-gather.8
  161.6 39.8 reduce-scatter.5
  204.8 57.0 all-gather.10
  263.7 37.2 all-gather.12
  307.0 83.0 all-gather.14
  393.0 77.0 all-gather.16
  590.3 44.1 reduce-scatter.7

commit v2 on v1

--- a/solution.py
+++ b/solution.py
@@ -68,15 +68,17 @@
         l_sc[...] = jnp.zeros(l_sc.shape, jnp.float32)
         acc_sc[...] = jnp.zeros(acc_sc.shape, jnp.float32)
 
-    @pl.when(step <= seq)
-    def _():
+    def update(diagonal):
         q = q_ref[...]
         k = k_ref[...]
         v = v_ref[...]
         column = lax.broadcasted_iota(jnp.int32, (rows, width), 1)
-        query_pos = seq * rows + lax.broadcasted_iota(jnp.int32, (rows, span), 0)
-        key_index = lax.broadcasted_iota(jnp.int32, (rows, span), 1)
-        allowed = (step * span + key_index <= query_pos) & (key_index < lengths_ref[step])
+        key_index = lax.broadcasted_iota(jnp.int32, (1, span), 1)
+        bias = jnp.where(key_index < lengths_ref[step], 0.0, MASKED_SCORE).astype(jnp.float32)
+        if diagonal:
+            causal = lax.broadcasted_iota(jnp.int32, (rows, span), 1) <= lax.broadcasted_iota(
+                jnp.int32, (rows, span), 0
+            )
         for h in range(heads):
             in_head = (column >= h * HEAD) & (column < (h + 1) * HEAD)
             q_head = jnp.where(in_head, q, jnp.zeros_like(q))
@@ -85,17 +87,27 @@
                     q_head, k, (((1,), (1,)), ((), ())), preferred_element_type=jnp.float32
                 )
                 * score_scale
+                + bias
             )
-            scores = jnp.where(allowed, scores, MASKED_SCORE)
+            if diagonal:
+                scores = jnp.where(causal, scores, MASKED_SCORE)
             m_prev = m_sc[h][:, :1]
             m_new = jnp.maximum(m_prev, jnp.max(scores, axis=1, keepdims=True))
-            weights = jnp.where(allowed, jnp.exp(scores - m_new), 0.0)
+            weights = jnp.exp(scores - m_new)
             alpha = jnp.exp(m_prev - m_new)
             l_new = alpha * l_sc[h][:, :1] + jnp.sum(weights, axis=1, keepdims=True)
             mixed = jnp.dot(weights.astype(jnp.bfloat16), v, preferred_element_type=jnp.float32)
             acc_sc[h] = acc_sc[h] * alpha + mixed
             m_sc[h] = jnp.broadcast_to(m_new, m_sc.shape[1:])
             l_sc[h] = jnp.broadcast_to(l_new, l_sc.shape[1:])
+
+    @pl.when(step < seq)
+    def _():
+        update(False)
+
+    @pl.when(step == seq)
+    def _():
+        update(True)
 
     @pl.when(step == pl.num_programs(0) - 1)
     def _():
@@ -107,10 +119,10 @@
         o_ref[...] = result.astype(o_ref.dtype)
 
 
-def causal_attention(query_flat, key_all, value_all, seq_index, block_lengths, rows_per_block):
+def causal_attention(query_flat, key_value_all, seq_index, block_lengths, rows_per_block):
     rows, width = query_flat.shape
     span = rows_per_block
-    steps = key_all.shape[0] // span
+    steps = key_value_all.shape[0] // (2 * span)
     heads = width // HEAD
     meta = jnp.reshape(seq_index, (1,)).astype(jnp.int32)
     grid_spec = pltpu.PrefetchScalarGridSpec(
@@ -118,8 +130,8 @@
         grid=(steps,),
         in_specs=[
             pl.BlockSpec((rows, width), lambda i, m, n: (0, 0)),
-            pl.BlockSpec((span, width), lambda i, m, n: (jnp.minimum(i, m[0]), 0)),
-            pl.BlockSpec((span, width), lambda i, m, n: (jnp.minimum(i, m[0]), 0)),
+            pl.BlockSpec((span, width), lambda i, m, n: (2 * jnp.minimum(i, m[0]), 0)),
+            pl.BlockSpec((span, width), lambda i, m, n: (2 * jnp.minimum(i, m[0]) + 1, 0)),
         ],
         out_specs=pl.BlockSpec((rows, width), lambda i, m, n: (0, 0)),
         scratch_shapes=[
@@ -128,18 +140,18 @@
             pltpu.VMEM((heads, rows, width), jnp.float32),
         ],
     )
-    flops = 4 * heads * rows * key_all.shape[0] * width
+    keys_total = steps * span
     return pl.pallas_call(
         attention_kernel,
         grid_spec=grid_spec,
         out_shape=jax.ShapeDtypeStruct((rows, width), jnp.bfloat16),
         compiler_params=pltpu.CompilerParams(dimension_semantics=("arbitrary",)),
         cost_estimate=pl.CostEstimate(
-            flops=flops,
-            transcendentals=heads * rows * key_all.shape[0],
-            bytes_accessed=2 * key_all.size * 2 + 2 * query_flat.size * 2,
+            flops=4 * heads * rows * keys_total * width,
+            transcendentals=heads * rows * keys_total,
+            bytes_accessed=key_value_all.size * 2 + 2 * query_flat.size * 2,
         ),
-    )(meta, block_lengths, query_flat, key_all, value_all)
+    )(meta, block_lengths, query_flat, key_value_all, key_value_all)
 
 
 def shards(
@@ -286,12 +298,12 @@
     ).astype(jnp.bfloat16)
     value_rows = text_heads[:, 2 * local_width :].astype(jnp.bfloat16)
     key_flat = key_rows.reshape(rows_per_block, local_width)
-    key_all = lax.all_gather(key_flat, "seq", axis=0, tiled=True)
-    value_all = lax.all_gather(value_rows, "seq", axis=0, tiled=True)
+    key_value_all = lax.all_gather(
+        jnp.concatenate([key_flat, value_rows], 0), "seq", axis=0, tiled=True
+    )
     attended_rows = causal_attention(
         query_rows.reshape(rows_per_block, local_width),
-        key_all,
-        value_all,
+        key_value_all,
         seq_index,
         block_lengths,
         rows_per_block,

time: 651 us -> 612 us (0.940)
  waiting for transfers between devices: 444 us -> 404 us
    all_gather x2 -> x1, waiting for transfers between devices: 160 us -> 121 us  [shards(): lax.all_gather(jnp.concatenate([key_flat, value_rows], 0), 'seq', axis=0,...]
  transfers between devices with their start and end apart: 9 -> 8, of which waited for: 9 -> 8; matrix products, arithmetic and copies ran while one was open for 1% -> 1% of each run, Pallas kernels for 0% -> 0%
where the time goes in v2:
time: 612 us; the launch traced here: 604 us
  waiting for transfers between devices  404 us (66%)
  Pallas kernels  116 us (19%)
  blocking collectives  24.1 us (4%)
  matrix products  22.5 us (4%)
  between operations  14.4 us (2%)
  other arithmetic  11.5 us (2%)
  local copies, waits for them, and re-layouts  10.5 us (2%)
    reduce_scatter x3, waiting for transfers between devices, summed_rows(): lax.psum_scatter(term_task(jnp.int32(0), own_rows * lax.axis_size('tp')),...  136 us
    all_gather x1, waiting for transfers between devices, shards(): lax.all_gather(jnp.concatenate([key_flat, value_rows], 0), 'seq', axis=0,...  121 us
    pallas_call x1, Pallas kernels, causal_attention(): pl.pallas_call(attention_kernel, grid_spec=grid_spec, out_shape=jax.Shape...  116 us
    all_gather x1, waiting for transfers between devices, shards(): segment = lax.all_gather(visual_part, 'seq', axis=0, tiled=True)  56.5 us
    all_gather x1, waiting for transfers between devices, shards(): whole_pictures = lax.all_gather(merge_input, 'tp', axis=1, tiled=True)  41 us
    all_gather x1, waiting for transfers between devices, shards(): lax.all_gather(patch_normed, 'tp', axis=1, tiled=True)  36.6 us
    all_gather x1, blocking collectives, shards(): lax.all_gather(arrived, 'tp', axis=0, tiled=True)  24.1 us
    all_gather x1, waiting for transfers between devices, shards(): lax.all_gather(text_rows, 'tp', axis=0, tiled=True)  13.2 us
  transfers between devices with their start and end apart: 8, of which 8 were waited for; matrix products, arithmetic and copies ran while one was open for 1% of the time, Pallas kernels for 0%

profile of v2, /device:TPU:223, one launch (start us, length us, event | category | flops | bytes accessed | tf_op | source)
XLA Modules:
  0.0 603.6 jit_solution(2063546958312632550)
XLA Ops:
  7.2 1.2 convert_reduce_fusion
  8.4 1.1 fusion.20
  9.6 1.8 fusion.22
  11.4 0.7 dynamic_slice.9
  12.2 36.6 %all-gather.6.cloned.1.call-done = bf16[2,256,1664]{2,1,0:T(8,128)(2,1)} async-done(((bf16[2,32,1664]{2,1,0:T(8,128)(2,1)}), bf16[2,256,1664]{2,1,0:T(8,128)(2,1)}) %all-gather.6.cloned.1.call-update) | async-done | bytes 1703952 | tf_op jit(solution)/shard_map/all_gather | solution.py:184
  48.9 3.4 convolution_convert_fusion.2
  52.4 1.3 fusion.12
  53.7 0.6 fusion.59
  54.3 1.9 fusion.14
  56.2 0.2 copy.39
  56.4 0.2 reshape.234
  56.7 3.5 fusion.60
  60.2 51.3 %reduce-scatter.4.cloned.1.call-done = f32[64,1664]{1,0:T(8,128)} async-done(((f32[512,1664]{1,0:T(8,128)}), f32[64,1664]{1,0:T(8,128)}) %reduce-scatter.4.cloned.1.call-update) | async-done | bytes 426000 | tf_op jit(solution)/shard_map/reduce_scatter | solution.py:49
  111.5 1.3 reshape.235
  112.7 0.1 convert_reduce_fusion.1
  112.9 0.2 fusion.23
  113.1 0.8 fusion.25
  114.0 41.0 %all-gather.8.cloned.1.call-done = bf16[2,256,1664]{2,1,0:T(8,128)(2,1)} async-done(((bf16[2,32,1664]{2,1,0:T(8,128)(2,1)}), bf16[2,256,1664]{2,1,0:T(8,128)(2,1)}) %all-gather.8.cloned.1.call-update) | async-done | bytes 1703952 | tf_op jit(solution)/shard_map/all_gather | solution.py:232
  155.0 3.9 reshape.236
  158.9 2.6 fusion.30
  161.6 40.2 %reduce-scatter.6.cloned.1.call-done = f32[16,1664]{1,0:T(8,128)} async-done(((f32[128,1664]{1,0:T(8,128)}), f32[16,1664]{1,0:T(8,128)}) %reduce-scatter.6.cloned.1.call-update) | async-done | bytes 106512 | tf_op jit(solution)/shard_map/reduce_scatter | solution.py:49
  201.7 1.5 convert_element_type.75
  203.3 0.5 all-gather.12.cloned.1.call-update
  203.9 0.1 reshape.228
  204.1 0.1 reshape.227
  204.2 0.1 fusion.41
  204.7 0.1 fusion.35
  204.8 0.1 fusion.29
  204.9 0.5 multiply_cosine_fusion
  205.4 56.5 %all-gather.10.cloned.1.call-done = bf16[512,1664]{1,0:T(8,128)(2,1)} async-done(((bf16[16,1664]{1,0:T(8,128)(2,1)}), bf16[512,1664]{1,0:T(8,128)(2,1)}) %all-gather.10.cloned.1.call-update) | async-done | bytes 1703952 | tf_op jit(solution)/shard_map/all_gather | solution.py:252
  261.9 1.8 convolution_convert_fusion.1
  263.7 24.1 %all_gather.21 = bf16[128,1664]{1,0:T(8,128)(2,1)S(1)} all-gather(bf16[16,1664]{1,0:T(8,128)(2,1)S(1)} %convolution_convert_fusion.1), channel_id=1, replica_groups=mesh['seq'=32,'tp'=8] {'tp'}, dimensions={0}, use_global_device_ids=true | all-gather | bytes 479232 | tf_op jit(solution)/shard_map/all_gather | solution.py:267
  287.8 13.2 %all-gather.12.cloned.1.call-done = bf16[512,1664]{1,0:T(8,128)(2,1)} async-done(((bf16[64,1664]{1,0:T(8,128)(2,1)}), bf16[512,1664]{1,0:T(8,128)(2,1)}) %all-gather.12.cloned.1.call-update) | async-done | bytes 1703952 | tf_op jit(solution)/shard_map/all_gather | solution.py:266
  301.0 2.4 fusion.1
  303.4 1.5 fusion.5
  305.0 0.7 slice.60
  305.7 0.2 subtract_convert_fusion
  305.9 0.7 pad_maximum_fusion.1
  306.6 0.1 copy.42
  306.7 1.1 copy.46
  307.8 0.9 pad_maximum_fusion
  308.7 0.2 reduce-scatter.8.cloned.1.call-start
  309.0 1.8 copy.43.q_ref
  310.7 120.8 %all-gather.14.cloned.1.call-done.k_ref.v_ref = bf16[32768,208]{1,0:T(8,128)(2,1)} async-done(((bf16[1024,208]{1,0:T(8,128)(2,1)}), bf16[32768,208]{1,0:T(8,128)(2,1)}) %all-gather.14.cloned.1.call-update) | async-done | bytes 13631504 | tf_op jit(solution)/shard_map/all_gather | solution.py:301
  431.5 115.7 %shard_map.148 = bf16[512,208]{1,0:T(8,128)(2,1)} custom-call(s32[1]{0:T(128)} %bitcast.10.meta_ref, s32[32]{0:T(128)} %lengths_ref.1, bf16[512,208]{1,0:T(8,128)(2,1)} %copy.43.q_ref, bf16[32768,208]{1,0:T(8,128)(2,1)} %all-gather.14.cloned.1.call-done.k_ref.v_ref, bf16[32768,208]{1,0:T(8,128)(2,1)} %all-gather.14.cloned.1.call-done.k_ref.v_ref), custom_call_target="tpu_custom_call" | custom-call | flops 13958643712 | bytes 14057472 | tf_op jit(solution)/shard_map/pallas_call | solution.py:144
  547.2 3.5 fusion.61
  550.8 44.2 %reduce-scatter.8.cloned.1.call-done = f32[64,1664]{1,0:T(8,128)} async-done(((f32[512,1664]{1,0:T(8,128)}), f32[64,1664]{1,0:T(8,128)}) %reduce-scatter.8.cloned.1.call-update) | async-done | bytes 426000 | tf_op jit(solution)/shard_map/reduce_scatter | solution.py:49
  594.9 1.8 add_convert_fusion
  (50 shorter events, 1.0 us)
Async XLA Ops:
  7.2 151.8 %copy-start = (bf16[832,1664]{1,0:T(8,128)(2,1)S(1)}, bf16[832,1664]{1,0:T(8,128)(2,1)}, u32[]{:S(2)}) copy-start(bf16[832,1664]{1,0:T(8,128)(2,1)} %param.22) | copy-start | bytes 8306692
  7.2 41.7 %all-gather.6.cloned.1.call-start = ((), (), s32[]{:S(2)}) async-start(), calls=%async_computation.3 | async-start | bytes 1916928 | tf_op jit(solution)/shard_map/all_gather | solution.py:184
  11.4 100.1 %reduce-scatter.4.cloned.1.call-start = ((), (), s32[]{:S(2)}) async-start(), calls=%async_computation.4 | async-start | bytes 3833856 | tf_op jit(solution)/shard_map/reduce_scatter | solution.py:49
  60.1 52.6 %copy-start.1 = (bf16[2,32,1664]{2,1,0:T(8,128)(2,1)S(1)}, bf16[2,32,1664]{2,1,0:T(8,128)(2,1)}, u32[]{:S(2)}) copy-start(bf16[2,32,1664]{2,1,0:T(8,128)(2,1)} %param.13) | copy-start | bytes 638980
  60.1 53.0 %copy-start.4 = (f32[1664]{0:T(1024)S(1)}, f32[1664]{0:T(1024)}, u32[]{:S(2)}) copy-start(f32[1664]{0:T(1024)} %param.21) | copy-start | bytes 19972
  60.1 94.9 %all-gather.8.cloned.1.call-start = ((), (), s32[]{:S(2)}) async-start(), calls=%async_computation.5 | async-start | bytes 1916928 | tf_op jit(solution)/shard_map/all_gather | solution.py:232
  114.0 87.8 %reduce-scatter.6.cloned.1.call-start = ((), (), s32[]{:S(2)}) async-start(), calls=%async_computation.6 | async-start | bytes 958464 | tf_op jit(solution)/shard_map/reduce_scatter | solution.py:49
  158.9 45.0 %copy-start.5 = (s32[64]{0:T(128)S(1)}, s32[64]{0:T(128)}, u32[]{:S(2)}) copy-start(s32[64]{0:T(128)} %param.15) | copy-start | bytes 772
  158.9 45.1 %copy-start.6 = (s32[64]{0:T(128)S(1)}, s32[64]{0:T(128)}, u32[]{:S(2)}) copy-start(s32[64]{0:T(128)} %param.16) | copy-start | bytes 772
  161.5 100.4 %all-gather.10.cloned.1.call-start = ((), (), s32[]{:S(2)}) async-start(), calls=%async_computation.7 | async-start | bytes 1757184 | tf_op jit(solution)/shard_map/all_gather | solution.py:252
  203.3 97.7 %all-gather.12.cloned.1.call-start = ((), (), s32[]{:S(2)}) async-start(), calls=%async_computation.8 | async-start | bytes 1916928 | tf_op jit(solution)/shard_map/all_gather | solution.py:266
  203.9 227.7 %all-gather.14.cloned.1.call-start = ((), (), s32[]{:S(2)}) async-start(), calls=%async_computation.9 | async-start | bytes 17301504 | tf_op jit(solution)/shard_map/all_gather | solution.py:301
  287.8 15.7 %copy-start.8 = (f32[1664]{0:T(1024)S(1)}, f32[1664]{0:T(1024)}, u32[]{:S(2)}) copy-start(f32[1664]{0:T(1024)} %param.23) | copy-start | bytes 19972
  301.0 2.5 copy-start.7
  303.4 1.5 copy-start.3
  306.6 240.6 %copy-start.2 = (bf16[512,2,104]{0,2,1:T(8,128)(2,1)}, bf16[512,2,104]{0,2,1:T(8,128)(2,1)S(1)}, u32[]{:S(2)}) copy-start(bf16[512,2,104]{0,2,1:T(8,128)(2,1)S(1)} %get-tuple-element.36) | copy-start | bytes 638980
  308.7 286.2 %reduce-scatter.8.cloned.1.call-start = ((), (), s32[]{:S(2)}) async-start(), calls=%async_computation.10 | async-start | bytes 3833856 | tf_op jit(solution)/shard_map/reduce_scatter | solution.py:49
Sparse Core Ops, SparseCore 0:
  11.5 37.3 all-gather.5
  60.3 51.1 reduce-scatter.3
  114.1 40.8 all-gather.7
  161.6 40.0 reduce-scatter.5
  205.1 56.7 all-gather.9
  263.7 37.2 all-gather.11
  308.8 122.6 all-gather.13
  550.9 44.0 reduce-scatter.7

commit v3 on v2

--- a/solution.py
+++ b/solution.py
@@ -54,10 +54,10 @@
     )
 
 
-def attention_kernel(meta_ref, lengths_ref, q_ref, k_ref, v_ref, o_ref, m_sc, l_sc, acc_sc):
+def attention_kernel(meta_ref, lengths_ref, qt_ref, k_ref, v_ref, o_ref, m_sc, l_sc, acc_sc):
     step = pl.program_id(0)
     seq = meta_ref[0]
-    rows, width = q_ref.shape
+    width, rows = qt_ref.shape
     span = k_ref.shape[0]
     heads = width // HEAD
     score_scale = 1.0 / math.sqrt(HEAD)
@@ -69,37 +69,35 @@
         acc_sc[...] = jnp.zeros(acc_sc.shape, jnp.float32)
 
     def update(diagonal):
-        q = q_ref[...]
+        qt = qt_ref[...]
         k = k_ref[...]
         v = v_ref[...]
-        column = lax.broadcasted_iota(jnp.int32, (rows, width), 1)
-        key_index = lax.broadcasted_iota(jnp.int32, (1, span), 1)
+        feature = lax.broadcasted_iota(jnp.int32, (width, rows), 0)
+        key_index = lax.broadcasted_iota(jnp.int32, (span, 1), 0)
         bias = jnp.where(key_index < lengths_ref[step], 0.0, MASKED_SCORE).astype(jnp.float32)
         if diagonal:
-            causal = lax.broadcasted_iota(jnp.int32, (rows, span), 1) <= lax.broadcasted_iota(
-                jnp.int32, (rows, span), 0
+            causal = lax.broadcasted_iota(jnp.int32, (span, rows), 0) <= lax.broadcasted_iota(
+                jnp.int32, (span, rows), 1
             )
         for h in range(heads):
-            in_head = (column >= h * HEAD) & (column < (h + 1) * HEAD)
-            q_head = jnp.where(in_head, q, jnp.zeros_like(q))
-            scores = (
-                lax.dot_general(
-                    q_head, k, (((1,), (1,)), ((), ())), preferred_element_type=jnp.float32
-                )
-                * score_scale
-                + bias
-            )
+            in_head = (feature >= h * HEAD) & (feature < (h + 1) * HEAD)
+            qt_head = jnp.where(in_head, qt, jnp.zeros_like(qt))
+            scores = jnp.dot(k, qt_head, preferred_element_type=jnp.float32) * score_scale + bias
             if diagonal:
                 scores = jnp.where(causal, scores, MASKED_SCORE)
-            m_prev = m_sc[h][:, :1]
-            m_new = jnp.maximum(m_prev, jnp.max(scores, axis=1, keepdims=True))
+            m_prev = m_sc[h]
+            m_new = jnp.maximum(m_prev, jnp.max(scores, axis=0, keepdims=True))
             weights = jnp.exp(scores - m_new)
             alpha = jnp.exp(m_prev - m_new)
-            l_new = alpha * l_sc[h][:, :1] + jnp.sum(weights, axis=1, keepdims=True)
-            mixed = jnp.dot(weights.astype(jnp.bfloat16), v, preferred_element_type=jnp.float32)
+            l_sc[h] = alpha * l_sc[h] + jnp.sum(weights, axis=0, keepdims=True)
+            mixed = lax.dot_general(
+                v,
+                weights.astype(jnp.bfloat16),
+                (((0,), (0,)), ((), ())),
+                preferred_element_type=jnp.float32,
+            )
             acc_sc[h] = acc_sc[h] * alpha + mixed
-            m_sc[h] = jnp.broadcast_to(m_new, m_sc.shape[1:])
-            l_sc[h] = jnp.broadcast_to(l_new, l_sc.shape[1:])
+            m_sc[h] = m_new
 
     @pl.when(step < seq)
     def _():
@@ -111,12 +109,12 @@
 
     @pl.when(step == pl.num_programs(0) - 1)
     def _():
-        column = lax.broadcasted_iota(jnp.int32, (rows, width), 1)
-        result = jnp.zeros((rows, width), jnp.float32)
+        feature = lax.broadcasted_iota(jnp.int32, (width, rows), 0)
+        result = jnp.zeros((width, rows), jnp.float32)
         for h in range(heads):
-            in_head = (column >= h * HEAD) & (column < (h + 1) * HEAD)
-            result = jnp.where(in_head, acc_sc[h] / l_sc[h][:, :1], result)
-        o_ref[...] = result.astype(o_ref.dtype)
+            in_head = (feature >= h * HEAD) & (feature < (h + 1) * HEAD)
+            result = jnp.where(in_head, acc_sc[h] / l_sc[h], result)
+        o_ref[...] = result
 
 
 def causal_attention(query_flat, key_value_all, seq_index, block_lengths, rows_per_block):
@@ -129,29 +127,30 @@
         num_scalar_prefetch=2,
         grid=(steps,),
         in_specs=[
-            pl.BlockSpec((rows, width), lambda i, m, n: (0, 0)),
+            pl.BlockSpec((width, rows), lambda i, m, n: (0, 0)),
             pl.BlockSpec((span, width), lambda i, m, n: (2 * jnp.minimum(i, m[0]), 0)),
             pl.BlockSpec((span, width), lambda i, m, n: (2 * jnp.minimum(i, m[0]) + 1, 0)),
         ],
-        out_specs=pl.BlockSpec((rows, width), lambda i, m, n: (0, 0)),
+        out_specs=pl.BlockSpec((width, rows), lambda i, m, n: (0, 0)),
         scratch_shapes=[
-            pltpu.VMEM((heads, rows, 128), jnp.float32),
-            pltpu.VMEM((heads, rows, 128), jnp.float32),
-            pltpu.VMEM((heads, rows, width), jnp.float32),
+            pltpu.VMEM((heads, 1, rows), jnp.float32),
+            pltpu.VMEM((heads, 1, rows), jnp.float32),
+            pltpu.VMEM((heads, width, rows), jnp.float32),
         ],
     )
     keys_total = steps * span
-    return pl.pallas_call(
+    result = pl.pallas_call(
         attention_kernel,
         grid_spec=grid_spec,
-        out_shape=jax.ShapeDtypeStruct((rows, width), jnp.bfloat16),
+        out_shape=jax.ShapeDtypeStruct((width, rows), jnp.float32),
         compiler_params=pltpu.CompilerParams(dimension_semantics=("arbitrary",)),
         cost_estimate=pl.CostEstimate(
             flops=4 * heads * rows * keys_total * width,
             transcendentals=heads * rows * keys_total,
-            bytes_accessed=key_value_all.size * 2 + 2 * query_flat.size * 2,
+            bytes_accessed=key_value_all.size * 2 + 3 * query_flat.size * 2,
         ),
-    )(meta, block_lengths, query_flat, key_value_all, key_value_all)
+    )(meta, block_lengths, jnp.transpose(query_flat), key_value_all, key_value_all)
+    return jnp.transpose(result).astype(jnp.bfloat16)
 
 
 def shards(

time: 612 us -> 541 us (0.88)
  Pallas kernels: 116 us -> 44.8 us
    pallas_call x1, Pallas kernels: 116 us -> 44.8 us  [causal_attention(): pl.pallas_call(attention_kernel, grid_spec=grid_spec, out_shape=jax.Shape...]
where the time goes in v3:
time: 541 us; the launch traced here: 533 us
  waiting for transfers between devices  405 us (75%)
  Pallas kernels  44.8 us (8%)
  blocking collectives  24.1 us (4%)
  matrix products  22.6 us (4%)
  between operations  14.4 us (3%)
  other arithmetic  13.2 us (2%)
  local copies, waits for them, and re-layouts  8.72 us (2%)
    reduce_scatter x3, waiting for transfers between devices, summed_rows(): lax.psum_scatter(term_task(jnp.int32(0), own_rows * lax.axis_size('tp')),...  136 us
    all_gather x1, waiting for transfers between devices, shards(): lax.all_gather(jnp.concatenate([key_flat, value_rows], 0), 'seq', axis=0,...  121 us
    all_gather x1, waiting for transfers between devices, shards(): segment = lax.all_gather(visual_part, 'seq', axis=0, tiled=True)  56.5 us
    pallas_call x1, Pallas kernels, causal_attention(): pl.pallas_call(attention_kernel, grid_spec=grid_spec, out_shape=jax.Shape...  44.8 us
    all_gather x1, waiting for transfers between devices, shards(): whole_pictures = lax.all_gather(merge_input, 'tp', axis=1, tiled=True)  41.1 us
    all_gather x1, waiting for transfers between devices, shards(): lax.all_gather(patch_normed, 'tp', axis=1, tiled=True)  36.6 us
    all_gather x1, blocking collectives, shards(): lax.all_gather(arrived, 'tp', axis=0, tiled=True)  24.1 us
    all_gather x1, waiting for transfers between devices, shards(): lax.all_gather(text_rows, 'tp', axis=0, tiled=True)  13.2 us
  transfers between devices with their start and end apart: 8, of which 8 were waited for; matrix products, arithmetic and copies ran while one was open for 1% of the time, Pallas kernels for 0%

profile of v3, /device:TPU:223, one launch (start us, length us, event | category | flops | bytes accessed | tf_op | source)
XLA Modules:
  0.0 533.2 jit_solution(866227254736673469)
XLA Ops:
  7.2 1.2 convert_reduce_fusion
  8.4 1.1 fusion.20
  9.6 1.8 fusion.22
  11.4 0.7 dynamic_slice.9
  12.2 36.6 %all-gather.6.cloned.1.call-done = bf16[2,256,1664]{2,1,0:T(8,128)(2,1)} async-done(((bf16[2,32,1664]{2,1,0:T(8,128)(2,1)}), bf16[2,256,1664]{2,1,0:T(8,128)(2,1)}) %all-gather.6.cloned.1.call-update) | async-done | bytes 1703952 | tf_op jit(solution)/shard_map/all_gather | solution.py:183
  48.9 3.4 convolution_convert_fusion.2
  52.4 0.6 fusion.61
  52.9 1.3 fusion.12
  54.3 1.9 fusion.14
  56.2 0.2 copy.38
  56.4 0.2 reshape.234
  56.7 3.5 fusion.62
  60.2 51.2 %reduce-scatter.4.cloned.1.call-done = f32[64,1664]{1,0:T(8,128)} async-done(((f32[512,1664]{1,0:T(8,128)}), f32[64,1664]{1,0:T(8,128)}) %reduce-scatter.4.cloned.1.call-update) | async-done | bytes 426000 | tf_op jit(solution)/shard_map/reduce_scatter | solution.py:49
  111.4 1.3 reshape.235
  112.6 0.1 convert_reduce_fusion.1
  112.8 0.2 fusion.23
  113.0 0.8 fusion.25
  113.9 41.1 %all-gather.8.cloned.1.call-done = bf16[2,256,1664]{2,1,0:T(8,128)(2,1)} async-done(((bf16[2,32,1664]{2,1,0:T(8,128)(2,1)}), bf16[2,256,1664]{2,1,0:T(8,128)(2,1)}) %all-gather.8.cloned.1.call-update) | async-done | bytes 1703952 | tf_op jit(solution)/shard_map/all_gather | solution.py:231
  155.0 3.9 reshape.236
  159.0 2.6 fusion.30
  161.6 40.2 %reduce-scatter.6.cloned.1.call-done = f32[16,1664]{1,0:T(8,128)} async-done(((f32[128,1664]{1,0:T(8,128)}), f32[16,1664]{1,0:T(8,128)}) %reduce-scatter.6.cloned.1.call-update) | async-done | bytes 106512 | tf_op jit(solution)/shard_map/reduce_scatter | solution.py:49
  201.8 1.5 convert_element_type.79
  203.4 0.5 all-gather.12.cloned.1.call-update
  204.0 0.1 reshape.228
  204.1 0.1 reshape.227
  204.2 0.1 fusion.43
  204.4 0.1 lt.52
  204.6 0.1 add.107
  204.7 0.1 fusion.37
  204.8 0.1 fusion.29
  205.0 0.5 multiply_cosine_fusion
  205.5 56.5 %all-gather.10.cloned.1.call-done = bf16[512,1664]{1,0:T(8,128)(2,1)} async-done(((bf16[16,1664]{1,0:T(8,128)(2,1)}), bf16[512,1664]{1,0:T(8,128)(2,1)}) %all-gather.10.cloned.1.call-update) | async-done | bytes 1703952 | tf_op jit(solution)/shard_map/all_gather | solution.py:251
  262.0 1.8 convolution_convert_fusion.1
  263.7 24.1 %all_gather.21 = bf16[128,1664]{1,0:T(8,128)(2,1)S(1)} all-gather(bf16[16,1664]{1,0:T(8,128)(2,1)S(1)} %convolution_convert_fusion.1), channel_id=1, replica_groups=mesh['seq'=32,'tp'=8] {'tp'}, dimensions={0}, use_global_device_ids=true | all-gather | bytes 479232 | tf_op jit(solution)/shard_map/all_gather | solution.py:266
  287.8 13.2 %all-gather.12.cloned.1.call-done = bf16[512,1664]{1,0:T(8,128)(2,1)} async-done(((bf16[64,1664]{1,0:T(8,128)(2,1)}), bf16[512,1664]{1,0:T(8,128)(2,1)}) %all-gather.12.cloned.1.call-update) | async-done | bytes 1703952 | tf_op jit(solution)/shard_map/all_gather | solution.py:265
  301.0 2.4 fusion.1
  303.5 1.5 fusion.5
  304.9 0.7 slice.60
  305.7 0.8 subtract_convert_fusion
  306.6 0.1 copy.41
  306.7 1.1 copy.44
  307.8 0.9 pad_maximum_fusion
  308.8 1.7 pad_maximum_fusion.1
  310.5 121.1 %all-gather.14.cloned.1.call-done.k_ref.v_ref = bf16[32768,208]{1,0:T(8,128)(2,1)} async-done(((bf16[1024,208]{1,0:T(8,128)(2,1)}), bf16[32768,208]{1,0:T(8,128)(2,1)}) %all-gather.14.cloned.1.call-update) | async-done | bytes 13631504 | tf_op jit(solution)/shard_map/all_gather | solution.py:300
  431.5 44.8 %shard_map.148 = f32[208,512]{1,0:T(8,128)} custom-call(s32[1]{0:T(128)} %bitcast.10.meta_ref, s32[32]{0:T(128)} %lengths_ref.1, bf16[208,512]{1,0:T(8,128)(2,1)} %bitcast.51, bf16[32768,208]{1,0:T(8,128)(2,1)} %all-gather.14.cloned.1.call-done.k_ref.v_ref, bf16[32768,208]{1,0:T(8,128)(2,1)} %all-gather.14.cloned.1.call-done.k_ref.v_ref), custom_call_target="tpu_custom_call" | custom-call | flops 13958643712 | bytes 14270464 | tf_op jit(solution)/shard_map/pallas_call | solution.py:142
  476.4 3.6 fusion.32
  480.0 44.5 %reduce-scatter.8.cloned.1.call-done = f32[64,1664]{1,0:T(8,128)} async-done(((f32[512,1664]{1,0:T(8,128)}), f32[64,1664]{1,0:T(8,128)}) %reduce-scatter.8.cloned.1.call-update) | async-done | bytes 426000 | tf_op jit(solution)/shard_map/reduce_scatter | solution.py:49
  524.5 1.8 add_convert_fusion
  (50 shorter events, 0.9 us)
Async XLA Ops:
  7.2 151.8 %copy-start = (bf16[832,1664]{1,0:T(8,128)(2,1)S(1)}, bf16[832,1664]{1,0:T(8,128)(2,1)}, u32[]{:S(2)}) copy-start(bf16[832,1664]{1,0:T(8,128)(2,1)} %param.22) | copy-start | bytes 8306692
  7.2 41.7 %all-gather.6.cloned.1.call-start = ((), (), s32[]{:S(2)}) async-start(), calls=%async_computation.3 | async-start | bytes 1916928 | tf_op jit(solution)/shard_map/all_gather | solution.py:183
  11.4 100.0 %reduce-scatter.4.cloned.1.call-start = ((), (), s32[]{:S(2)}) async-start(), calls=%async_computation.4 | async-start | bytes 3833856 | tf_op jit(solution)/shard_map/reduce_scatter | solution.py:49
  60.1 52.5 %copy-start.1 = (bf16[2,32,1664]{2,1,0:T(8,128)(2,1)S(1)}, bf16[2,32,1664]{2,1,0:T(8,128)(2,1)}, u32[]{:S(2)}) copy-start(bf16[2,32,1664]{2,1,0:T(8,128)(2,1)} %param.13) | copy-start | bytes 638980
  60.1 52.9 %copy-start.4 = (f32[1664]{0:T(1024)S(1)}, f32[1664]{0:T(1024)}, u32[]{:S(2)}) copy-start(f32[1664]{0:T(1024)} %param.21) | copy-start | bytes 19972
  60.1 94.9 %all-gather.8.cloned.1.call-start = ((), (), s32[]{:S(2)}) async-start(), calls=%async_computation.5 | async-start | bytes 1916928 | tf_op jit(solution)/shard_map/all_gather | solution.py:231
  113.9 87.9 %reduce-scatter.6.cloned.1.call-start = ((), (), s32[]{:S(2)}) async-start(), calls=%async_computation.6 | async-start | bytes 958464 | tf_op jit(solution)/shard_map/reduce_scatter | solution.py:49
  158.9 45.0 %copy-start.5 = (s32[64]{0:T(128)S(1)}, s32[64]{0:T(128)}, u32[]{:S(2)}) copy-start(s32[64]{0:T(128)} %param.15) | copy-start | bytes 772
  158.9 45.1 %copy-start.6 = (s32[64]{0:T(128)S(1)}, s32[64]{0:T(128)}, u32[]{:S(2)}) copy-start(s32[64]{0:T(128)} %param.16) | copy-start | bytes 772
  161.5 100.4 %all-gather.10.cloned.1.call-start = ((), (), s32[]{:S(2)}) async-start(), calls=%async_computation.7 | async-start | bytes 1757184 | tf_op jit(solution)/shard_map/all_gather | solution.py:251
  203.3 97.6 %all-gather.12.cloned.1.call-start = ((), (), s32[]{:S(2)}) async-start(), calls=%async_computation.8 | async-start | bytes 1916928 | tf_op jit(solution)/shard_map/all_gather | solution.py:265
  203.9 227.6 %all-gather.14.cloned.1.call-start = ((), (), s32[]{:S(2)}) async-start(), calls=%async_computation.9 | async-start | bytes 17301504 | tf_op jit(solution)/shard_map/all_gather | solution.py:300
  287.8 15.7 %copy-start.8 = (f32[1664]{0:T(1024)S(1)}, f32[1664]{0:T(1024)}, u32[]{:S(2)}) copy-start(f32[1664]{0:T(1024)} %param.23) | copy-start | bytes 19972
  301.0 2.5 copy-start.7
  303.4 1.5 copy-start.3
  306.6 169.8 %copy-start.2 = (bf16[512,2,104]{0,2,1:T(8,128)(2,1)}, bf16[512,2,104]{0,2,1:T(8,128)(2,1)S(1)}, u32[]{:S(2)}) copy-start(bf16[512,2,104]{0,2,1:T(8,128)(2,1)S(1)} %pad_maximum_fusion.2) | copy-start | bytes 638980
  308.7 215.8 %reduce-scatter.8.cloned.1.call-start = ((), (), s32[]{:S(2)}) async-start(), calls=%async_computation.10 | async-start | bytes 3833856 | tf_op jit(solution)/shard_map/reduce_scatter | solution.py:49
Sparse Core Ops, SparseCore 0:
  11.5 37.3 all-gather.5
  60.3 51.0 reduce-scatter.3
  114.0 41.0 all-gather.7
  161.6 40.0 reduce-scatter.5
  205.2 56.7 all-gather.9
  263.7 37.2 all-gather.11
  308.8 122.6 all-gather.13
  480.1 44.3 reduce-scatter.7

commit v4 on v3

--- a/solution.py
+++ b/solution.py
@@ -1,3 +1,4 @@
+import functools
 import math
 
 import jax
@@ -45,12 +46,76 @@
     )
 
 
-def summed_rows(term_task, own_rows):
-    return lax.psum_scatter(
-        term_task(jnp.int32(0), own_rows * lax.axis_size("tp")),
-        "tp",
-        scatter_dimension=0,
-        tiled=True,
+MESH_IDS = pl.DeviceIdType.MESH
+
+
+def exchange_kernel(ways, gather, x_ref, y_ref, send_sem, recv_sem, local_sem):
+    me = lax.axis_index("tp")
+    row = lax.axis_index("seq")
+    barrier = pltpu.get_barrier_semaphore()
+    for shift in range(1, ways):
+        peer = lax.rem(me + shift, ways)
+        pl.semaphore_signal(barrier, inc=1, device_id=(row, peer), device_id_type=MESH_IDS)
+    pl.semaphore_wait(barrier, ways - 1)
+    sends = []
+    for shift in range(1, ways):
+        peer = lax.rem(me + shift, ways)
+        copy = pltpu.make_async_remote_copy(
+            src_ref=x_ref if gather else x_ref.at[peer],
+            dst_ref=y_ref.at[me],
+            send_sem=send_sem.at[shift],
+            recv_sem=recv_sem.at[shift],
+            device_id=(row, peer),
+            device_id_type=MESH_IDS,
+        )
+        copy.start()
+        sends.append(copy)
+    local = pltpu.make_async_copy(x_ref if gather else x_ref.at[me], y_ref.at[me], local_sem)
+    local.start()
+    for copy in sends:
+        copy.wait_send()
+    for shift in range(1, ways):
+        source = lax.rem(me + ways - shift, ways)
+        arriving = pltpu.make_async_remote_copy(
+            src_ref=x_ref if gather else x_ref.at[source],
+            dst_ref=y_ref.at[source],
+            send_sem=send_sem.at[shift],
+            recv_sem=recv_sem.at[shift],
+            device_id=(row, source),
+            device_id_type=MESH_IDS,
+        )
+        arriving.wait_recv()
+    local.wait()
+
+
+def tp_exchange(x, ways, gather, collective_id):
+    piece = x.shape if gather else x.shape[1:]
+    return pl.pallas_call(
+        functools.partial(exchange_kernel, ways, gather),
+        out_shape=jax.ShapeDtypeStruct((ways,) + tuple(piece), x.dtype),
+        in_specs=[pl.BlockSpec(memory_space=pl.ANY)],
+        out_specs=pl.BlockSpec(memory_space=pl.ANY),
+        scratch_shapes=[
+            pltpu.SemaphoreType.DMA((ways,)),
+            pltpu.SemaphoreType.DMA((ways,)),
+            pltpu.SemaphoreType.DMA(()),
+        ],
+        compiler_params=pltpu.CompilerParams(collective_id=collective_id, has_side_effects=True),
+    )(x)
+
+
+def summed_rows(term_task, own_rows, collective_id):
+    ways = lax.axis_size("tp")
+    partial = term_task(jnp.int32(0), own_rows * ways)
+    pieces = partial.reshape((ways, own_rows) + partial.shape[1:])
+    return jnp.sum(tp_exchange(pieces, ways, False, collective_id), 0)
+
+
+def gathered_patches(piece, collective_id):
+    ways = lax.axis_size("tp")
+    whole = tp_exchange(piece, ways, True, collective_id)
+    return jnp.transpose(whole, (1, 0, 2, 3)).reshape(
+        (piece.shape[0], ways * piece.shape[1]) + piece.shape[2:]
     )
 
 
@@ -180,7 +245,7 @@
     packed_project = vision_project.reshape(model_width, 3 * local_width)
     projected = jnp.einsum(
         "npd,de->npe",
-        lax.all_gather(patch_normed, "tp", axis=1, tiled=True),
+        gathered_patches(patch_normed, 0),
         packed_project,
         preferred_element_type=jnp.float32,
     ).astype(jnp.bfloat16)
@@ -220,7 +285,7 @@
     def vision_term(offset, row_count):
         return jnp.dot(patch_major, vision_output, preferred_element_type=jnp.float32)
 
-    vision_sum = summed_rows(vision_term, local_patches * picture_total)
+    vision_sum = summed_rows(vision_term, local_patches * picture_total, 2)
     vision_sum = jnp.transpose(
         vision_sum.reshape(local_patches, picture_total, model_width), (1, 0, 2)
     )
@@ -228,7 +293,7 @@
     merge_input = layer_normed(vision_rows, merge_gain).astype(jnp.bfloat16)
     merged_total = patch_total // 4
     input_share = merge_weight.shape[0]
-    whole_pictures = lax.all_gather(merge_input, "tp", axis=1, tiled=True)
+    whole_pictures = gathered_patches(merge_input, 1)
     merged_rows = whole_pictures.reshape(picture_total * merged_total, 4 * model_width)
     owned_inputs = lax.dynamic_slice_in_dim(merged_rows, tp_index * input_share, input_share, 1)
 
@@ -236,7 +301,7 @@
         return jnp.dot(owned_inputs, merge_weight, preferred_element_type=jnp.float32)
 
     part_rows = picture_total * merged_total // tp_ways
-    visual_part = summed_rows(merge_term, part_rows).astype(jnp.bfloat16)
+    visual_part = summed_rows(merge_term, part_rows, 3).astype(jnp.bfloat16)
     rows_per_block = text_rows.shape[0] * tp_ways
     start_table = picture_starts.reshape(seq_ways, picture_total)
     dest_table = start_table // rows_per_block
@@ -261,10 +326,9 @@
     arrived = jnp.dot(
         selector.astype(jnp.bfloat16), segment, preferred_element_type=jnp.float32
     ).astype(jnp.bfloat16)
-    text_block, visual_block = (
-        lax.all_gather(text_rows, "tp", axis=0, tiled=True),
-        lax.all_gather(arrived, "tp", axis=0, tiled=True),
-    )
+    both_blocks = tp_exchange(jnp.concatenate([text_rows, arrived], 0), tp_ways, True, 5)
+    text_block = both_blocks[:, : text_rows.shape[0]].reshape(-1, model_width)
+    visual_block = both_blocks[:, text_rows.shape[0] :].reshape(-1, model_width)
     landed = dest_table == seq_index
     local_starts = jnp.sum(jnp.where(landed, start_table - seq_index * rows_per_block, 0), 0)
     live_groups = jnp.sum(
@@ -312,7 +376,7 @@
     def text_term(offset, row_count):
         return jnp.dot(attended_rows, text_output, preferred_element_type=jnp.float32)
 
-    text_sum = summed_rows(text_term, own_rows)
+    text_sum = summed_rows(text_term, own_rows, 4)
     residual = lax.dynamic_slice_in_dim(embedded, tp_index * own_rows, own_rows, 0)
     hidden = (residual.astype(jnp.float32) + text_sum).astype(jnp.bfloat16)
     return (hidden, key_flat, value_rows)

time: 541 us -> 480 us (0.89); the launches traced: 533 us -> 479 us
  waiting for transfers between devices: 405 us -> 174 us
  Pallas kernels: 44.8 us -> 240 us
  blocking collectives: 24.1 us -> 0 us
  local copies, waits for them, and re-layouts: 8.72 us -> 14.7 us
    pallas_call x0 -> x6, Pallas kernels: none -> 195 us  [tp_exchange(): pl.pallas_call(functools.partial(exchange_kernel, ways, gather), out_shap...]
    reduce_scatter x3 -> x0, waiting for transfers between devices: 136 us -> none  [summed_rows(): lax.psum_scatter(term_task(jnp.int32(0), own_rows * lax.axis_size('tp')),...]
    all_gather x3 -> x0, waiting for transfers between devices: 91 us -> none  [the longest x1 41.1 us: shards(): whole_pictures = lax.all_gather(merge_input, 'tp', axis=1, tiled=True)]
    all_gather x1 -> x0, blocking collectives: 24.1 us -> none  [shards(): lax.all_gather(arrived, 'tp', axis=0, tiled=True)]
    reduce_sum x0 -> x3, other arithmetic: none -> 7.02 us  [summed_rows(): return jnp.sum(tp_exchange(pieces, ways, False, collective_id), 0)]
  transfers between devices with their start and end apart: 8 -> 2, of which waited for: 8 -> 2; matrix products, arithmetic and copies ran while one was open for 1% -> 0% of each run, Pallas kernels for 0% -> 0%
where the time goes in v4:
time: 480 us; the launch traced here: 479 us
  Pallas kernels  240 us (50%)
  waiting for transfers between devices  174 us (36%)
  matrix products  18.7 us (4%)
  other arithmetic  17.5 us (4%)
  local copies, waits for them, and re-layouts  14.7 us (3%)
  between operations  14.4 us (3%)
    pallas_call x6, Pallas kernels, tp_exchange(): pl.pallas_call(functools.partial(exchange_kernel, ways, gather), out_shap...  195 us
    all_gather x1, waiting for transfers between devices, shards(): lax.all_gather(jnp.concatenate([key_flat, value_rows], 0), 'seq', axis=0,...  117 us
    all_gather x1, waiting for transfers between devices, shards(): segment = lax.all_gather(visual_part, 'seq', axis=0, tiled=True)  56.3 us
    pallas_call x1, Pallas kernels, causal_attention(): pl.pallas_call(attention_kernel, grid_spec=grid_spec, out_shape=jax.Shape...  44.9 us
  transfers between devices with their start and end apart: 2, of which 2 were waited for; matrix products, arithmetic and copies ran while one was open for 0% of the time, Pallas kernels for 0%

profile of v4, /device:TPU:223, one launch (start us, length us, event | category | flops | bytes accessed | tf_op | source)
XLA Modules:
  0.0 479.4 jit_solution(7473254056802309102)
XLA Ops:
  7.2 0.9 dynamic_slice.9
  8.2 1.0 convert_reduce_fusion
  9.2 1.1 fusion.22
  10.4 1.8 fusion.24.x_ref
  12.2 26.1 %shard_map.148 = bf16[8,2,32,1664]{3,2,1,0:T(8,128)(2,1)} custom-call(bf16[2,32,1664]{2,1,0:T(8,128)(2,1)} %fusion.24.x_ref), custom_call_target="tpu_custom_call" | custom-call | tf_op jit(solution)/shard_map/pallas_call | solution.py:93
  38.3 1.7 copy.42
  40.0 0.3 copy-done.11
  40.4 1.3 convolution_convert_fusion.2
  41.8 0.6 fusion.63
  42.4 1.3 fusion.12
  43.7 1.9 fusion.14
  45.6 0.2 copy.44
  45.8 0.2 dot_general.32
  46.1 3.5 fusion.15.x_ref
  49.6 46.4 %shard_map.149 = f32[8,64,1664]{2,1,0:T(8,128)} custom-call(f32[8,64,1664]{2,1,0:T(8,128)} %fusion.15.x_ref), custom_call_target="tpu_custom_call" | custom-call | tf_op jit(solution)/shard_map/pallas_call | solution.py:93
  96.0 3.0 reduce_sum.114
  99.0 1.3 reshape.248
  100.4 0.2 fusion.25
  100.7 0.8 fusion.27.x_ref
  101.5 19.9 %shard_map.150 = bf16[8,2,32,1664]{3,2,1,0:T(8,128)(2,1)} custom-call(bf16[2,32,1664]{2,1,0:T(8,128)(2,1)} %fusion.27.x_ref), custom_call_target="tpu_custom_call" | custom-call | tf_op jit(solution)/shard_map/pallas_call | solution.py:93
  121.4 2.8 copy.46
  124.2 3.9 reshape_reshape.3
  128.1 2.5 fusion.32
  130.6 11.6 %shard_map.151 = f32[8,16,1664]{2,1,0:T(8,128)} custom-call(f32[8,16,1664]{2,1,0:T(8,128)} %bitcast.57), custom_call_target="tpu_custom_call" | custom-call | tf_op jit(solution)/shard_map/pallas_call | solution.py:93
  142.3 1.8 reduce_sum.117
  144.1 0.2 all-gather.5.cloned.1.call-start
  144.6 0.1 fusion.45
  145.2 0.1 fusion.31
  145.4 0.5 multiply_cosine_fusion
  145.9 56.3 %all-gather.3.cloned.1.call-done = bf16[512,1664]{1,0:T(8,128)(2,1)} async-done(((bf16[16,1664]{1,0:T(8,128)(2,1)}), bf16[512,1664]{1,0:T(8,128)(2,1)}) %all-gather.3.cloned.1.call-update) | async-done | bytes 1703952 | tf_op jit(solution)/shard_map/all_gather | solution.py:316
  202.2 1.8 convolution_convert_fusion.1
  204.0 0.8 pad_maximum_fusion.1.x_ref
  204.8 35.3 %shard_map.152 = bf16[8,80,1664]{2,1,0:T(8,128)(2,1)} custom-call(bf16[80,1664]{1,0:T(8,128)(2,1)} %pad_maximum_fusion.1.x_ref), custom_call_target="tpu_custom_call" | custom-call | tf_op jit(solution)/shard_map/pallas_call | solution.py:93
  240.1 1.0 slice-done
  241.1 0.6 slice-done.1
  241.7 0.8 fusion.1
  242.6 0.7 copy-done.12
  243.3 1.5 fusion.5
  244.9 0.2 subtract_convert_fusion
  245.2 0.2 copy-done.4
  245.6 0.9 pad_maximum_fusion
  246.5 0.7 pad_maximum_fusion.2
  247.2 117.3 %all-gather.5.cloned.1.call-done.k_ref.v_ref = bf16[32768,208]{1,0:T(8,128)(2,1)} async-done(((bf16[1024,208]{1,0:T(8,128)(2,1)}), bf16[32768,208]{1,0:T(8,128)(2,1)}) %all-gather.5.cloned.1.call-update) | async-done | bytes 13631504 | tf_op jit(solution)/shard_map/all_gather | solution.py:364
  364.5 44.9 %shard_map.153 = f32[208,512]{1,0:T(8,128)} custom-call(s32[1]{0:T(128)} %bitcast.17.meta_ref, s32[32]{0:T(128)} %lengths_ref.1, bf16[208,512]{1,0:T(8,128)(2,1)} %bitcast.69, bf16[32768,208]{1,0:T(8,128)(2,1)} %all-gather.5.cloned.1.call-done.k_ref.v_ref, bf16[32768,208]{1,0:T(8,128)(2,1)} %all-gather.5.cloned.1.call-done.k_ref.v_ref), custom_call_target="tpu_custom_call" | custom-call | flops 13958643712 | bytes 14270464 | tf_op jit(solution)/shard_map/pallas_call | solution.py:207
  409.5 3.4 fusion.34
  412.9 55.8 %shard_map.154 = f32[8,64,1664]{2,1,0:T(8,128)} custom-call(f32[8,64,1664]{2,1,0:T(8,128)} %bitcast.52), custom_call_target="tpu_custom_call" | custom-call | tf_op jit(solution)/shard_map/pallas_call | solution.py:93
  468.7 2.2 reduce_sum.119
  470.9 1.7 add_convert_fusion
  (56 shorter events, 1.4 us)
Async XLA Ops:
  7.2 120.9 %copy-start = (bf16[832,1664]{1,0:T(8,128)(2,1)S(1)}, bf16[832,1664]{1,0:T(8,128)(2,1)}, u32[]{:S(2)}) copy-start(bf16[832,1664]{1,0:T(8,128)(2,1)} %param.22) | copy-start | bytes 8306692
  7.2 195.0 %all-gather.3.cloned.1.call-start = ((), (), s32[]{:S(2)}) async-start(), calls=%async_computation | async-start | bytes 1757184 | tf_op jit(solution)/shard_map/all_gather | solution.py:316
  38.3 2.1 copy-start.11
  96.0 4.3 copy-start.2
  96.0 4.6 copy-start.8
  130.6 13.8 %copy-start.9 = (s32[64]{0:T(128)S(1)}, s32[64]{0:T(128)}, u32[]{:S(2)}) copy-start(s32[64]{0:T(128)} %param.15) | copy-start | bytes 772
  130.6 13.9 %copy-start.10 = (s32[64]{0:T(128)S(1)}, s32[64]{0:T(128)}, u32[]{:S(2)}) copy-start(s32[64]{0:T(128)} %param.16) | copy-start | bytes 772
  130.6 73.4 %copy-start.6 = (bf16[64,1664]{1,0:T(8,128)(2,1)S(1)}, bf16[64,1664]{1,0:T(8,128)(2,1)}, u32[]{:S(2)}) copy-start(bf16[64,1664]{1,0:T(8,128)(2,1)} %param.14) | copy-start | bytes 638980
  144.1 220.4 %all-gather.5.cloned.1.call-start = ((), (), s32[]{:S(2)}) async-start(), calls=%async_computation.1 | async-start | bytes 17301504 | tf_op jit(solution)/shard_map/all_gather | solution.py:364
  240.1 1.0 slice-start
  240.1 1.6 slice-start.1
  241.7 1.6 copy-start.12
  241.7 1.6 copy-start.13
  242.5 2.2 copy-start.7
  244.8 0.7 copy-start.4
  245.1 164.4 %copy-start.3 = (bf16[512,2,104]{0,2,1:T(8,128)(2,1)}, bf16[512,2,104]{0,2,1:T(8,128)(2,1)S(1)}, u32[]{:S(2)}) copy-start(bf16[512,2,104]{0,2,1:T(8,128)(2,1)S(1)} %pad_maximum_fusion.3) | copy-start | bytes 638980
  364.5 44.9 %copy-start.5 = (bf16[208,1664]{1,0:T(8,128)(2,1)S(1)}, bf16[208,1664]{1,0:T(8,128)(2,1)}, u32[]{:S(2)}) copy-start(bf16[208,1664]{1,0:T(8,128)(2,1)} %param.25) | copy-start | bytes 2076676
  412.9 59.7 %copy-start.1 = (bf16[832,1664]{1,0:T(8,128)(2,1)S(1)}, bf16[832,1664]{1,0:T(8,128)(2,1)}, u32[]{:S(2)}) copy-start(bf16[832,1664]{1,0:T(8,128)(2,1)} %param.22) | copy-start | bytes 8306692
Sparse Core Ops, SparseCore 0:
  144.3 57.9 all-gather.2
  246.6 117.8 all-gather.4

commit v5 on v4

--- a/solution.py
+++ b/solution.py
@@ -107,8 +107,9 @@
 def summed_rows(term_task, own_rows, collective_id):
     ways = lax.axis_size("tp")
     partial = term_task(jnp.int32(0), own_rows * ways)
-    pieces = partial.reshape((ways, own_rows) + partial.shape[1:])
-    return jnp.sum(tp_exchange(pieces, ways, False, collective_id), 0)
+    pieces = partial.reshape((ways, own_rows) + partial.shape[1:]).astype(jnp.bfloat16)
+    arrived = tp_exchange(pieces, ways, False, collective_id)
+    return jnp.sum(arrived.astype(jnp.float32), 0)
 
 
 def gathered_patches(piece, collective_id):

time: 480 us -> 426 us (0.89)
  Pallas kernels: 240 us -> 186 us
    pallas_call x6, Pallas kernels: 195 us -> 142 us  [tp_exchange(): pl.pallas_call(functools.partial(exchange_kernel, ways, gather), out_shap...]
  transfers between devices with their start and end apart: 2 -> 2, of which waited for: 2 -> 2; matrix products, arithmetic and copies ran while one was open for 0% -> 1% of each run, Pallas kernels for 0% -> 0%
where the time goes in v5:
time: 426 us; the launch traced here: 425 us
  Pallas kernels  186 us (44%)
  waiting for transfers between devices  171 us (40%)
  matrix products  18.4 us (4%)
  other arithmetic  18.1 us (4%)
  local copies, waits for them, and re-layouts  16.9 us (4%)
  between operations  14.4 us (3%)
    pallas_call x6, Pallas kernels, tp_exchange(): pl.pallas_call(functools.partial(exchange_kernel, ways, gather), out_shap...  142 us
    all_gather x1, waiting for transfers between devices, shards(): lax.all_gather(jnp.concatenate([key_flat, value_rows], 0), 'seq', axis=0,...  116 us
    all_gather x1, waiting for transfers between devices, shards(): segment = lax.all_gather(visual_part, 'seq', axis=0, tiled=True)  54.4 us
    pallas_call x1, Pallas kernels, causal_attention(): pl.pallas_call(attention_kernel, grid_spec=grid_spec, out_shape=jax.Shape...  44.8 us
  transfers between devices with their start and end apart: 2, of which 2 were waited for; matrix products, arithmetic and copies ran while one was open for 1% of the time, Pallas kernels for 0%

profile of v5, /device:TPU:223, one launch (start us, length us, event | category | flops | bytes accessed | tf_op | source)
XLA Modules:
  0.0 425.3 jit_solution(8663801365507071848)
XLA Ops:
  7.2 0.9 dynamic_slice.9
  8.2 1.0 convert_reduce_fusion.2
  9.2 1.1 fusion.21
  10.4 1.8 fusion.23.x_ref
  12.2 26.1 %shard_map.148 = bf16[8,2,32,1664]{3,2,1,0:T(8,128)(2,1)} custom-call(bf16[2,32,1664]{2,1,0:T(8,128)(2,1)} %fusion.23.x_ref), custom_call_target="tpu_custom_call" | custom-call | tf_op jit(solution)/shard_map/pallas_call | solution.py:93
  38.3 1.7 copy.42
  40.0 0.3 copy-done.8
  40.4 1.3 convolution_convert_fusion.5
  41.8 0.6 fusion.60
  42.4 1.3 fusion.12
  43.7 2.6 fusion.14
  46.3 1.1 copy.44
  47.4 0.2 dot_general.32
  47.7 2.9 convolution_convert_fusion.2.x_ref
  50.6 20.5 %shard_map.149 = bf16[8,64,1664]{2,1,0:T(8,128)(2,1)} custom-call(bf16[8,64,1664]{2,1,0:T(8,128)(2,1)} %convolution_convert_fusion.2.x_ref), custom_call_target="tpu_custom_call" | custom-call | tf_op jit(solution)/shard_map/pallas_call | solution.py:93
  71.1 2.5 convert_reduce_fusion.1
  73.6 1.3 reshape.246
  75.1 0.2 fusion.24
  75.3 0.8 fusion.26.x_ref
  76.1 21.0 %shard_map.150 = bf16[8,2,32,1664]{3,2,1,0:T(8,128)(2,1)} custom-call(bf16[2,32,1664]{2,1,0:T(8,128)(2,1)} %fusion.26.x_ref), custom_call_target="tpu_custom_call" | custom-call | tf_op jit(solution)/shard_map/pallas_call | solution.py:93
  97.2 2.8 copy.46
  100.0 3.9 reshape_reshape.3
  103.9 2.4 convolution_convert_fusion.3
  106.3 9.4 %shard_map.151 = bf16[8,16,1664]{2,1,0:T(8,128)(2,1)} custom-call(bf16[8,16,1664]{2,1,0:T(8,128)(2,1)} %bitcast.60), custom_call_target="tpu_custom_call" | custom-call | tf_op jit(solution)/shard_map/pallas_call | solution.py:93
  115.7 1.7 reduce_sum.120
  117.4 0.2 all-gather.5.cloned.1.call-start
  118.5 0.1 fusion.30
  118.7 0.5 multiply_cosine_fusion
  119.1 54.4 %all-gather.3.cloned.1.call-done = bf16[512,1664]{1,0:T(8,128)(2,1)} async-done(((bf16[16,1664]{1,0:T(8,128)(2,1)}), bf16[512,1664]{1,0:T(8,128)(2,1)}) %all-gather.3.cloned.1.call-update) | async-done | bytes 1703952 | tf_op jit(solution)/shard_map/all_gather | solution.py:317
  173.6 1.8 convolution_convert_fusion.4
  175.4 0.8 pad_maximum_fusion.1.x_ref
  176.1 35.3 %shard_map.152 = bf16[8,80,1664]{2,1,0:T(8,128)(2,1)} custom-call(bf16[80,1664]{1,0:T(8,128)(2,1)} %pad_maximum_fusion.1.x_ref), custom_call_target="tpu_custom_call" | custom-call | tf_op jit(solution)/shard_map/pallas_call | solution.py:93
  211.5 1.0 slice-done
  212.5 0.6 slice-done.1
  213.1 0.9 fusion.1
  214.0 0.7 copy-done.9
  214.6 1.5 fusion.5
  216.1 0.7 slice.68
  216.9 0.8 subtract_convert_fusion
  217.9 1.1 copy.51
  219.0 0.9 pad_maximum_fusion
  219.9 1.7 pad_maximum_fusion.2
  221.6 116.3 %all-gather.5.cloned.1.call-done.k_ref.v_ref = bf16[32768,208]{1,0:T(8,128)(2,1)} async-done(((bf16[1024,208]{1,0:T(8,128)(2,1)}), bf16[32768,208]{1,0:T(8,128)(2,1)}) %all-gather.5.cloned.1.call-update) | async-done | bytes 13631504 | tf_op jit(solution)/shard_map/all_gather | solution.py:365
  337.9 44.8 %shard_map.153 = f32[208,512]{1,0:T(8,128)} custom-call(s32[1]{0:T(128)} %bitcast.17.meta_ref, s32[32]{0:T(128)} %lengths_ref.1, bf16[208,512]{1,0:T(8,128)(2,1)} %bitcast.69, bf16[32768,208]{1,0:T(8,128)(2,1)} %all-gather.5.cloned.1.call-done.k_ref.v_ref, bf16[32768,208]{1,0:T(8,128)(2,1)} %all-gather.5.cloned.1.call-done.k_ref.v_ref), custom_call_target="tpu_custom_call" | custom-call | flops 13958643712 | bytes 14270464 | tf_op jit(solution)/shard_map/pallas_call | solution.py:208
  382.7 3.1 convolution_convert_fusion
  385.8 29.2 %shard_map.154 = bf16[8,64,1664]{2,1,0:T(8,128)(2,1)} custom-call(bf16[8,64,1664]{2,1,0:T(8,128)(2,1)} %bitcast.56), custom_call_target="tpu_custom_call" | custom-call | tf_op jit(solution)/shard_map/pallas_call | solution.py:93
  415.0 1.7 convert_reduce_fusion
  416.8 1.7 add_convert_fusion
  (50 shorter events, 1.4 us)
Async XLA Ops:
  7.2 96.7 %copy-start = (bf16[832,1664]{1,0:T(8,128)(2,1)S(1)}, bf16[832,1664]{1,0:T(8,128)(2,1)}, u32[]{:S(2)}) copy-start(bf16[832,1664]{1,0:T(8,128)(2,1)} %param.22) | copy-start | bytes 8306692
  7.2 166.4 %all-gather.3.cloned.1.call-start = ((), (), s32[]{:S(2)}) async-start(), calls=%async_computation | async-start | bytes 1757184 | tf_op jit(solution)/shard_map/all_gather | solution.py:317
  38.3 2.1 copy-start.8
  71.1 3.8 copy-start.1
  71.1 4.2 copy-start.5
  103.9 13.8 %copy-start.6 = (s32[64]{0:T(128)S(1)}, s32[64]{0:T(128)}, u32[]{:S(2)}) copy-start(s32[64]{0:T(128)} %param.15) | copy-start | bytes 772
  103.9 13.9 %copy-start.7 = (s32[64]{0:T(128)S(1)}, s32[64]{0:T(128)}, u32[]{:S(2)}) copy-start(s32[64]{0:T(128)} %param.16) | copy-start | bytes 772
  106.3 69.1 %copy-start.3 = (bf16[64,1664]{1,0:T(8,128)(2,1)S(1)}, bf16[64,1664]{1,0:T(8,128)(2,1)}, u32[]{:S(2)}) copy-start(bf16[64,1664]{1,0:T(8,128)(2,1)} %param.14) | copy-start | bytes 638980
  117.4 220.5 %all-gather.5.cloned.1.call-start = ((), (), s32[]{:S(2)}) async-start(), calls=%async_computation.1 | async-start | bytes 17301504 | tf_op jit(solution)/shard_map/all_gather | solution.py:365
  211.5 1.0 slice-start
  211.5 1.6 slice-start.1
  213.1 1.6 copy-start.9
  213.1 1.6 copy-start.10
  214.0 2.1 copy-start.4
  217.8 165.0 %copy-start.2 = (bf16[512,2,104]{0,2,1:T(8,128)(2,1)}, bf16[512,2,104]{0,2,1:T(8,128)(2,1)S(1)}, u32[]{:S(2)}) copy-start(bf16[512,2,104]{0,2,1:T(8,128)(2,1)S(1)} %pad_maximum_fusion.3) | copy-start | bytes 638980
Sparse Core Ops, SparseCore 0:
  117.5 56.0 all-gather.2
  220.0 117.8 all-gather.4

commit v6 on v5

--- a/solution.py
+++ b/solution.py
@@ -49,13 +49,17 @@
 MESH_IDS = pl.DeviceIdType.MESH
 
 
-def exchange_kernel(ways, gather, x_ref, y_ref, send_sem, recv_sem, local_sem):
-    me = lax.axis_index("tp")
-    row = lax.axis_index("seq")
+def exchange_kernel(axis, ways, gather, x_ref, y_ref, send_sem, recv_sem, local_sem):
+    me = lax.axis_index(axis)
+    other = lax.axis_index("seq" if axis == "tp" else "tp")
+
+    def device(peer):
+        return (other, peer) if axis == "tp" else (peer, other)
+
     barrier = pltpu.get_barrier_semaphore()
     for shift in range(1, ways):
         peer = lax.rem(me + shift, ways)
-        pl.semaphore_signal(barrier, inc=1, device_id=(row, peer), device_id_type=MESH_IDS)
+        pl.semaphore_signal(barrier, inc=1, device_id=device(peer), device_id_type=MESH_IDS)
     pl.semaphore_wait(barrier, ways - 1)
     sends = []
     for shift in range(1, ways):
@@ -65,7 +69,7 @@
             dst_ref=y_ref.at[me],
             send_sem=send_sem.at[shift],
             recv_sem=recv_sem.at[shift],
-            device_id=(row, peer),
+            device_id=device(peer),
             device_id_type=MESH_IDS,
         )
         copy.start()
@@ -81,17 +85,17 @@
             dst_ref=y_ref.at[source],
             send_sem=send_sem.at[shift],
             recv_sem=recv_sem.at[shift],
-            device_id=(row, source),
+            device_id=device(source),
             device_id_type=MESH_IDS,
         )
         arriving.wait_recv()
     local.wait()
 
 
-def tp_exchange(x, ways, gather, collective_id):
+def tp_exchange(x, ways, gather, collective_id, axis="tp"):
     piece = x.shape if gather else x.shape[1:]
     return pl.pallas_call(
-        functools.partial(exchange_kernel, ways, gather),
+        functools.partial(exchange_kernel, axis, ways, gather),
         out_shape=jax.ShapeDtypeStruct((ways,) + tuple(piece), x.dtype),
         in_specs=[pl.BlockSpec(memory_space=pl.ANY)],
         out_specs=pl.BlockSpec(memory_space=pl.ANY),
@@ -314,7 +318,7 @@
         1,
     )
     senders = rank_dest == seq_index
-    segment = lax.all_gather(visual_part, "seq", axis=0, tiled=True)
+    segment = tp_exchange(visual_part, seq_ways, True, 6, "seq").reshape(-1, model_width)
     row_count = segment.shape[0]
     sources = jnp.arange(row_count, dtype=jnp.int32) // part_rows
     wanted = jnp.any(

time: 426 us -> 430 us (level)
  Pallas kernels: 186 us -> 244 us
  waiting for transfers between devices: 171 us -> 115 us
    pallas_call x6 -> x7, Pallas kernels: 142 us -> 199 us  [tp_exchange(): pl.pallas_call(functools.partial(exchange_kernel, axis, ways, gather), ou...]
    all_gather x1 -> x0, waiting for transfers between devices: 54.4 us -> none  [shards(): segment = lax.all_gather(visual_part, 'seq', axis=0, tiled=True)]
  transfers between devices with their start and end apart: 2 -> 1, of which waited for: 2 -> 1; matrix products, arithmetic and copies ran while one was open for 1% -> 0% of each run, Pallas kernels for 0% -> 0%
where the time goes in v6:
time: 430 us; the launch traced here: 429 us
  Pallas kernels  244 us (57%)
  waiting for transfers between devices  115 us (27%)
  matrix products  20 us (5%)
  local copies, waits for them, and re-layouts  18.2 us (4%)
  other arithmetic  18.1 us (4%)
  between operations  14.4 us (3%)
    pallas_call x7, Pallas kernels, tp_exchange(): pl.pallas_call(functools.partial(exchange_kernel, axis, ways, gather), ou...  199 us
    all_gather x1, waiting for transfers between devices, shards(): lax.all_gather(jnp.concatenate([key_flat, value_rows], 0), 'seq', axis=0,...  115 us
    pallas_call x1, Pallas kernels, causal_attention(): pl.pallas_call(attention_kernel, grid_spec=grid_spec, out_shape=jax.Shape...  44.8 us
  transfers between devices with their start and end apart: 1, of which 1 were waited for; matrix products, arithmetic and copies ran while one was open for 0% of the time, Pallas kernels for 0%

profile of v6, /device:TPU:223, one launch (start us, length us, event | category | flops | bytes accessed | tf_op | source)
XLA Modules:
  0.0 429.2 jit_solution(1995888345935299296)
XLA Ops:
  7.3 0.9 reshape.242
  8.2 0.7 dynamic_slice.9
  9.0 1.0 convert_reduce_fusion.2
  10.0 1.1 fusion.21
  11.2 1.8 fusion.23.x_ref
  13.0 26.1 %shard_map.148 = bf16[8,2,32,1664]{3,2,1,0:T(8,128)(2,1)} custom-call(bf16[2,32,1664]{2,1,0:T(8,128)(2,1)} %fusion.23.x_ref), custom_call_target="tpu_custom_call" | custom-call | tf_op jit(solution)/shard_map/pallas_call | solution.py:97
  39.1 1.7 copy.42
  40.9 0.3 copy-done.7
  41.2 1.3 convolution_convert_fusion.5
  42.6 0.6 fusion.60
  43.2 1.3 fusion.12
  44.7 0.1 fusion.42
  44.8 2.6 fusion.14
  47.4 1.1 copy.44
  48.5 0.2 dot_general.32
  48.8 2.9 convolution_convert_fusion.2.x_ref
  51.7 20.5 %shard_map.149 = bf16[8,64,1664]{2,1,0:T(8,128)(2,1)} custom-call(bf16[8,64,1664]{2,1,0:T(8,128)(2,1)} %convolution_convert_fusion.2.x_ref), custom_call_target="tpu_custom_call" | custom-call | tf_op jit(solution)/shard_map/pallas_call | solution.py:97
  72.2 2.5 convert_reduce_fusion.1
  74.7 1.3 reshape.249
  76.1 0.2 fusion.24
  76.4 0.8 fusion.26.x_ref
  77.2 21.0 %shard_map.150 = bf16[8,2,32,1664]{3,2,1,0:T(8,128)(2,1)} custom-call(bf16[2,32,1664]{2,1,0:T(8,128)(2,1)} %fusion.26.x_ref), custom_call_target="tpu_custom_call" | custom-call | tf_op jit(solution)/shard_map/pallas_call | solution.py:97
  98.2 2.8 copy.46
  101.0 3.9 reshape_reshape.3
  104.9 2.4 convolution_convert_fusion.3
  107.3 9.4 %shard_map.151 = bf16[8,16,1664]{2,1,0:T(8,128)(2,1)} custom-call(bf16[8,16,1664]{2,1,0:T(8,128)(2,1)} %bitcast.62), custom_call_target="tpu_custom_call" | custom-call | tf_op jit(solution)/shard_map/pallas_call | solution.py:97
  116.7 1.7 reduce_sum.120.x_ref
  118.5 56.1 %shard_map.152 = bf16[32,16,1664]{2,1,0:T(8,128)(2,1)} custom-call(bf16[16,1664]{1,0:T(8,128)(2,1)} %reduce_sum.120.x_ref), custom_call_target="tpu_custom_call" | custom-call | tf_op jit(solution)/shard_map/pallas_call | solution.py:97
  174.7 1.8 convolution_convert_fusion.4
  176.5 0.8 pad_maximum_fusion.1.x_ref
  177.2 36.5 %shard_map.153 = bf16[8,80,1664]{2,1,0:T(8,128)(2,1)} custom-call(bf16[80,1664]{1,0:T(8,128)(2,1)} %pad_maximum_fusion.1.x_ref), custom_call_target="tpu_custom_call" | custom-call | tf_op jit(solution)/shard_map/pallas_call | solution.py:97
  213.8 2.8 slice.41
  216.9 0.2 fusion.30
  217.1 2.4 fusion.1
  219.6 1.5 fusion.5
  221.1 0.7 slice.68
  221.8 0.5 multiply_cosine_fusion
  222.3 0.8 subtract_convert_fusion
  223.2 0.1 copy.48
  223.4 1.1 copy.51
  224.4 0.9 pad_maximum_fusion
  225.3 1.7 pad_maximum_fusion.2
  227.0 114.8 %all-gather.2.cloned.1.call-done.k_ref.v_ref = bf16[32768,208]{1,0:T(8,128)(2,1)} async-done(((bf16[1024,208]{1,0:T(8,128)(2,1)}), bf16[32768,208]{1,0:T(8,128)(2,1)}) %all-gather.2.cloned.1.call-update) | async-done | bytes 13631504 | tf_op jit(solution)/shard_map/all_gather | solution.py:369
  341.8 44.8 %shard_map.154 = f32[208,512]{1,0:T(8,128)} custom-call(s32[1]{0:T(128)} %bitcast.18.meta_ref, s32[32]{0:T(128)} %lengths_ref.1, bf16[208,512]{1,0:T(8,128)(2,1)} %bitcast.71, bf16[32768,208]{1,0:T(8,128)(2,1)} %all-gather.2.cloned.1.call-done.k_ref.v_ref, bf16[32768,208]{1,0:T(8,128)(2,1)} %all-gather.2.cloned.1.call-done.k_ref.v_ref), custom_call_target="tpu_custom_call" | custom-call | flops 13958643712 | bytes 14270464 | tf_op jit(solution)/shard_map/pallas_call | solution.py:212
  386.7 3.1 convolution_convert_fusion
  389.8 29.2 %shard_map.155 = bf16[8,64,1664]{2,1,0:T(8,128)(2,1)} custom-call(bf16[8,64,1664]{2,1,0:T(8,128)(2,1)} %bitcast.57), custom_call_target="tpu_custom_call" | custom-call | tf_op jit(solution)/shard_map/pallas_call | solution.py:97
  419.0 1.7 convert_reduce_fusion
  420.7 1.7 add_convert_fusion
  (45 shorter events, 1.0 us)
Async XLA Ops:
  7.2 97.8 %copy-start = (bf16[832,1664]{1,0:T(8,128)(2,1)S(1)}, bf16[832,1664]{1,0:T(8,128)(2,1)}, u32[]{:S(2)}) copy-start(bf16[832,1664]{1,0:T(8,128)(2,1)} %param.22) | copy-start | bytes 8306692
  7.2 334.7 %all-gather.2.cloned.1.call-start = ((), (), s32[]{:S(2)}) async-start(), calls=%async_computation | async-start | bytes 17301504 | tf_op jit(solution)/shard_map/all_gather | solution.py:369
  39.1 2.1 copy-start.7
  42.6 1.9 copy-start.6
  72.2 3.8 copy-start.1
  72.2 4.2 copy-start.5
  118.4 58.0 %copy-start.3 = (bf16[64,1664]{1,0:T(8,128)(2,1)S(1)}, bf16[64,1664]{1,0:T(8,128)(2,1)}, u32[]{:S(2)}) copy-start(bf16[64,1664]{1,0:T(8,128)(2,1)} %param.14) | copy-start | bytes 638980
  213.8 3.3 slice-start
  217.1 2.5 copy-start.8
  217.1 2.5 copy-start.9
  219.6 1.5 copy-start.4
  223.2 163.4 %copy-start.2 = (bf16[512,2,104]{0,2,1:T(8,128)(2,1)}, bf16[512,2,104]{0,2,1:T(8,128)(2,1)S(1)}, u32[]{:S(2)}) copy-start(bf16[512,2,104]{0,2,1:T(8,128)(2,1)S(1)} %pad_maximum_fusion.3) | copy-start | bytes 638980
Sparse Core Ops, SparseCore 0:
  225.5 116.3 all-gather.1

commit v7 on v5

--- a/solution.py
+++ b/solution.py
@@ -242,6 +242,30 @@
     patch_total = local_patches * tp_ways
     local_width = vision_project.shape[2]
     head_count = local_width // HEAD
+    model_width = pixels.shape[2]
+    rows_per_block = text_rows.shape[0] * tp_ways
+    text_block = lax.all_gather(text_rows, "tp", axis=0, tiled=True)
+    packed_text = text_project.reshape(model_width, 3 * local_width)
+    positions = seq_index * rows_per_block + jnp.arange(rows_per_block, dtype=jnp.int32)
+
+    def block_heads(rows_in):
+        normed = rms_normed(rows_in, text_gain).astype(jnp.bfloat16)
+        return jnp.dot(normed, packed_text, preferred_element_type=jnp.float32)
+
+    def keys_and_values(heads_in):
+        keys = rotary(
+            heads_in[:, local_width : 2 * local_width].reshape(rows_per_block, head_count, HEAD),
+            positions,
+        ).astype(jnp.bfloat16)
+        return keys.reshape(rows_per_block, local_width), heads_in[:, 2 * local_width :].astype(
+            jnp.bfloat16
+        )
+
+    early_key, early_value = keys_and_values(block_heads(text_block))
+    early_operand, pixels = lax.optimization_barrier(
+        (jnp.concatenate([early_key, early_value], 0), pixels)
+    )
+    early_all = lax.all_gather(early_operand, "seq", axis=0, tiled=True)
     patch_normed = layer_normed(pixels, vision_gain).astype(jnp.bfloat16)
     packed_project = vision_project.reshape(model_width, 3 * local_width)
     projected = jnp.einsum(
@@ -303,6 +327,7 @@
 
     part_rows = picture_total * merged_total // tp_ways
     visual_part = summed_rows(merge_term, part_rows, 3).astype(jnp.bfloat16)
+    early_all, visual_part = lax.optimization_barrier((early_all, visual_part))
     rows_per_block = text_rows.shape[0] * tp_ways
     start_table = picture_starts.reshape(seq_ways, picture_total)
     dest_table = start_table // rows_per_block
@@ -327,9 +352,7 @@
     arrived = jnp.dot(
         selector.astype(jnp.bfloat16), segment, preferred_element_type=jnp.float32
     ).astype(jnp.bfloat16)
-    both_blocks = tp_exchange(jnp.concatenate([text_rows, arrived], 0), tp_ways, True, 5)
-    text_block = both_blocks[:, : text_rows.shape[0]].reshape(-1, model_width)
-    visual_block = both_blocks[:, text_rows.shape[0] :].reshape(-1, model_width)
+    visual_block = tp_exchange(arrived, tp_ways, True, 5).reshape(-1, model_width)
     landed = dest_table == seq_index
     local_starts = jnp.sum(jnp.where(landed, start_table - seq_index * rows_per_block, 0), 0)
     live_groups = jnp.sum(
@@ -338,33 +361,52 @@
     slot_index = jnp.arange(merged_total, dtype=jnp.int32)
     targets = (local_starts[:, None] + slot_index[None, :]).reshape(-1)
     in_use = (slot_index[None, :] < live_groups[:, None]).reshape(-1)
-    placement = (jnp.arange(rows_per_block, dtype=jnp.int32)[:, None] == targets[None, :]) & in_use[
-        None, :
-    ]
+    row_index = jnp.arange(rows_per_block, dtype=jnp.int32)
+    placement = (row_index[:, None] == targets[None, :]) & in_use[None, :]
     covered = jnp.any(placement, 1)
     placed = jnp.dot(
         placement.astype(jnp.bfloat16), visual_block, preferred_element_type=jnp.float32
     ).astype(jnp.bfloat16)
     embedded = jnp.where(covered[:, None], placed, text_block)
-    text_normed = rms_normed(embedded, text_gain).astype(jnp.bfloat16)
-    text_heads = jnp.dot(
-        text_normed,
-        text_project.reshape(model_width, 3 * local_width),
-        preferred_element_type=jnp.float32,
-    )
-    positions = seq_index * rows_per_block + jnp.arange(rows_per_block, dtype=jnp.int32)
+    text_heads = block_heads(embedded)
     query_rows = rotary(
         text_heads[:, :local_width].reshape(rows_per_block, head_count, HEAD), positions
     ).astype(jnp.bfloat16)
-    key_rows = rotary(
-        text_heads[:, local_width : 2 * local_width].reshape(rows_per_block, head_count, HEAD),
-        positions,
-    ).astype(jnp.bfloat16)
-    value_rows = text_heads[:, 2 * local_width :].astype(jnp.bfloat16)
-    key_flat = key_rows.reshape(rows_per_block, local_width)
-    key_value_all = lax.all_gather(
-        jnp.concatenate([key_flat, value_rows], 0), "seq", axis=0, tiled=True
-    )
+    key_flat, value_rows = keys_and_values(text_heads)
+    pick = (targets[:, None] == row_index[None, :]).astype(jnp.bfloat16)
+    picture_kv = jnp.concatenate(
+        [
+            jnp.dot(pick, key_flat, preferred_element_type=jnp.float32),
+            jnp.dot(pick, value_rows, preferred_element_type=jnp.float32),
+        ],
+        0,
+    ).astype(jnp.bfloat16)
+    picture_all = lax.all_gather(picture_kv, "seq", axis=0, tiled=True).reshape(
+        seq_ways, 2, picture_total * merged_total, local_width
+    )
+    block_ids = jnp.arange(seq_ways, dtype=jnp.int32)
+    landed_all = dest_table[None, :, :] == block_ids[:, None, None]
+    starts_all = jnp.sum(
+        jnp.where(landed_all, start_table[None] - block_ids[:, None, None] * rows_per_block, 0), 1
+    )
+    live_all = jnp.sum(
+        jnp.where(landed_all, patch_counts.reshape(seq_ways, picture_total)[None] // 4, 0), 1
+    )
+    targets_all = (starts_all[:, :, None] + slot_index[None, None, :]).reshape(seq_ways, -1)
+    in_use_all = (slot_index[None, None, :] < live_all[:, :, None]).reshape(seq_ways, -1)
+    placement_all = (row_index[None, :, None] == targets_all[:, None, :]) & in_use_all[:, None, :]
+    covered_all = jnp.any(placement_all, 2)
+    patched = jnp.einsum(
+        "brs,bksd->bkrd",
+        placement_all.astype(jnp.bfloat16),
+        picture_all,
+        preferred_element_type=jnp.float32,
+    ).astype(jnp.bfloat16)
+    key_value_all = jnp.where(
+        covered_all[:, None, :, None],
+        patched,
+        early_all.reshape(seq_ways, 2, rows_per_block, local_width),
+    ).reshape(-1, local_width)
     attended_rows = causal_attention(
         query_rows.reshape(rows_per_block, local_width),
         key_value_all,

time: 426 us -> 518 us (1.22); the launches traced: 425 us -> 510 us
  matrix products: 18.4 us -> 70.5 us
  local copies, waits for them, and re-layouts: 16.9 us -> 65.4 us
  waiting for transfers between devices: 171 us -> 146 us
  Pallas kernels: 186 us -> 195 us
    dot_general x1 -> x5, matrix products: 1.45 us -> 52.5 us  [the longest x1 47 us: shards(): jnp.einsum('brs,bksd->bkrd', placement_all.astype(jnp.bfloat16), picture_...]
    all_gather x1 -> x3, waiting for transfers between devices: 116 us -> 72 us  [the longest x1 38.6 us: shards(): text_block = lax.all_gather(text_rows, 'tp', axis=0, tiled=True)]
    reshape x0 -> x2, local copies, waits for them, and re-layouts: none -> 31.7 us  [the longest x1 22.8 us: shards(): early_all.reshape(seq_ways, 2, rows_per_block, local_width)]
    select_n x0 -> x3, local copies, waits for them, and re-layouts: none -> 20.1 us  [the longest x1 20 us: shards(): jnp.where(covered_all[:, None, :, None], patched, early_all.reshape(seq_w...]
    all_gather x1, waiting for transfers between devices: 54.4 us -> 73.2 us  [shards(): segment = lax.all_gather(visual_part, 'seq', axis=0, tiled=True)]
    pallas_call x6, Pallas kernels: 142 us -> 150 us  [tp_exchange(): pl.pallas_call(functools.partial(exchange_kernel, ways, gather), out_shap...]
  transfers between devices with their start and end apart: 2 -> 4, of which waited for: 2 -> 3; matrix products, arithmetic and copies ran while one was open for 1% -> 11% of each run, Pallas kernels for 0% -> 22%
where the time goes in v7:
time: 518 us; the launch traced here: 510 us
  Pallas kernels  195 us (38%)
  waiting for transfers between devices  146 us (28%)
  matrix products  70.5 us (14%)
  local copies, waits for them, and re-layouts  65.4 us (13%)
  other arithmetic  17.8 us (3%)
  between operations  14.5 us (3%)
    pallas_call x6, Pallas kernels, tp_exchange(): pl.pallas_call(functools.partial(exchange_kernel, ways, gather), out_shap...  150 us
    all_gather x1, waiting for transfers between devices, shards(): segment = lax.all_gather(visual_part, 'seq', axis=0, tiled=True)  73.2 us
    dot_general x1, matrix products, shards(): jnp.einsum('brs,bksd->bkrd', placement_all.astype(jnp.bfloat16), picture_...  47 us
    pallas_call x1, Pallas kernels, causal_attention(): pl.pallas_call(attention_kernel, grid_spec=grid_spec, out_shape=jax.Shape...  45 us
    all_gather x1, waiting for transfers between devices, shards(): text_block = lax.all_gather(text_rows, 'tp', axis=0, tiled=True)  38.6 us
    all_gather x1, waiting for transfers between devices, shards(): lax.all_gather(picture_kv, 'seq', axis=0, tiled=True)  33.3 us
    reshape x1, local copies, waits for them, and re-layouts, shards(): early_all.reshape(seq_ways, 2, rows_per_block, local_width)  22.8 us
    select_n x1, local copies, waits for them, and re-layouts, shards(): jnp.where(covered_all[:, None, :, None], patched, early_all.reshape(seq_w...  20 us
  transfers between devices with their start and end apart: 4, of which 3 were waited for; matrix products, arithmetic and copies ran while one was open for 11% of the time, Pallas kernels for 22%

profile of v7, /device:TPU:223, one launch (start us, length us, event | category | flops | bytes accessed | tf_op | source)
XLA Modules:
  0.0 509.7 jit_solution(16021803089387421628)
XLA Ops:
  7.2 0.7 all-gather.5.cloned.1.call-update
  8.0 0.5 multiply_cosine_fusion
  8.5 38.6 %all-gather.5.cloned.1.call-done = bf16[512,1664]{1,0:T(8,128)(2,1)} async-done(((bf16[64,1664]{1,0:T(8,128)(2,1)}), bf16[512,1664]{1,0:T(8,128)(2,1)}) %all-gather.5.cloned.1.call-update) | async-done | bytes 1703952 | tf_op jit(solution)/shard_map/all_gather | solution.py:247
  47.1 1.9 fusion.7
  49.0 3.5 fusion.17
  52.8 0.8 pad_maximum_fusion
  54.3 0.8 fusion.37.x_ref
  55.1 20.8 %shard_map.148 = bf16[8,2,32,1664]{3,2,1,0:T(8,128)(2,1)} custom-call(bf16[2,32,1664]{2,1,0:T(8,128)(2,1)} %fusion.37.x_ref), custom_call_target="tpu_custom_call" | custom-call | tf_op jit(solution)/shard_map/pallas_call | solution.py:93
  75.9 1.7 copy.29
  77.6 0.3 copy-done.16
  78.0 1.3 convolution_convert_fusion.5
  79.3 0.7 fusion.73
  80.0 0.6 fusion.74
  80.6 1.3 fusion.26
  81.9 2.0 fusion.28
  84.4 3.0 convolution_convert_fusion.2.x_ref
  87.4 17.7 %shard_map.149 = bf16[8,64,1664]{2,1,0:T(8,128)(2,1)} custom-call(bf16[8,64,1664]{2,1,0:T(8,128)(2,1)} %convolution_convert_fusion.2.x_ref), custom_call_target="tpu_custom_call" | custom-call | tf_op jit(solution)/shard_map/pallas_call | solution.py:93
  105.1 2.5 convert_reduce_fusion.1
  107.6 1.3 reshape.403
  109.2 0.8 fusion.40.x_ref
  110.1 60.6 %shard_map.150 = bf16[8,2,32,1664]{3,2,1,0:T(8,128)(2,1)} custom-call(bf16[2,32,1664]{2,1,0:T(8,128)(2,1)} %fusion.40.x_ref), custom_call_target="tpu_custom_call" | custom-call | tf_op jit(solution)/shard_map/pallas_call | solution.py:93
  170.7 2.8 copy.33
  173.5 3.9 reshape_reshape.3
  177.4 2.4 convolution_convert_fusion.3
  179.8 12.6 %shard_map.151 = bf16[8,16,1664]{2,1,0:T(8,128)(2,1)} custom-call(bf16[8,16,1664]{2,1,0:T(8,128)(2,1)} %bitcast.77), custom_call_target="tpu_custom_call" | custom-call | tf_op jit(solution)/shard_map/pallas_call | solution.py:93
  192.4 1.7 reduce_sum.148
  194.1 0.4 all-gather.11.cloned.1.call-start
  195.6 73.2 %all-gather.9.cloned.1.call-done = bf16[512,1664]{1,0:T(8,128)(2,1)} async-done(((bf16[16,1664]{1,0:T(8,128)(2,1)}), bf16[512,1664]{1,0:T(8,128)(2,1)}) %all-gather.9.cloned.1.call-update) | async-done | bytes 1703952 | tf_op jit(solution)/shard_map/all_gather | solution.py:342
  268.9 2.4 convolution_convert_fusion.4.x_ref
  271.3 9.3 %shard_map.152 = bf16[8,16,1664]{2,1,0:T(8,128)(2,1)} custom-call(bf16[16,1664]{1,0:T(8,128)(2,1)} %convolution_convert_fusion.4.x_ref), custom_call_target="tpu_custom_call" | custom-call | tf_op jit(solution)/shard_map/pallas_call | solution.py:93
  280.6 2.0 fusion.10
  282.6 1.5 fusion.15
  284.2 0.8 copy-done.5
  285.3 0.3 convolution_convert_fusion.7
  285.6 0.3 convolution_convert_fusion.6
  285.9 0.7 pad_maximum_fusion.4
  287.6 2.2 fusion.3
  289.9 22.8 %reshape.409 = bf16[32,2,512,208]{2,1,0,3:T(2,128)(2,1)} reshape(bf16[32768,208]{0,1:T(8,128)(2,1)} %all-gather.7.cloned.1.call-done) | data formatting | bytes 27262976 | tf_op jit(solution)/shard_map/reshape | solution.py:408
  312.7 0.7 pad_maximum_fusion.2
  313.4 33.3 %all-gather.11.cloned.1.call-done = bf16[8192,208]{0,1:T(8,128)(2,1)} async-done(((bf16[256,208]{0,1:T(8,128)(2,1)}), bf16[8192,208]{0,1:T(8,128)(2,1)}) %all-gather.11.cloned.1.call-update) | async-done | bytes 3407888 | tf_op jit(solution)/shard_map/all_gather | solution.py:384
  346.7 8.9 %reshape.408 = bf16[32,2,128,208]{2,1,0,3:T(2,128)(2,1)} reshape(bf16[8192,208]{0,1:T(8,128)(2,1)} %all-gather.11.cloned.1.call-done) | data formatting | bytes 6815744 | tf_op jit(solution)/shard_map/reshape | solution.py:384
  355.6 47.0 %bitcast_select_fusion = bf16[32,2,512,208]{2,3,1,0:T(8,128)(2,1)} fusion(bf16[32,2,512,208]{2,1,0,3:T(2,128)(2,1)} %reshape.409, pred[32,512]{1,0:T(8,128)(4,1)S(1)} %fusion.3, s32[32,128]{1,0:T(8,128)S(1)} %broadcast_add_fusion, pred[32,128]{1,0:T(8,128)(4,1)S(1)} %broadcast_compare_fusion, bf16[32,2,128,208]{2,1,0,3:T(2,128)(2,1)} %reshape.408), kind=kOutput, calls=%fused_computation.1 | convolution fusion | flops 1762656256 | bytes 30707712 | tf_op jit(solution)/shard_map/brs,bksd->bkrd/dot_general | solution.py:399
  402.6 20.0 %copy.41 = bf16[32,2,512,208]{3,2,1,0:T(8,128)(2,1)} copy(bf16[32,2,512,208]{2,3,1,0:T(8,128)(2,1)} %bitcast_select_fusion) | data formatting | bytes 27262976 | tf_op jit(solution)/shard_map/jit(_where)/select_n | solution.py:405
  422.6 45.0 %shard_map.153 = f32[208,512]{1,0:T(8,128)} custom-call(s32[1]{0:T(128)} %bitcast.19.meta_ref, s32[32]{0:T(128)} %lengths_ref.1, bf16[208,512]{1,0:T(8,128)(2,1)} %bitcast.88, bf16[32768,208]{1,0:T(8,128)(2,1)} %bitcast.68, bf16[32768,208]{1,0:T(8,128)(2,1)} %bitcast.69), custom_call_target="tpu_custom_call" | custom-call | flops 13958643712 | bytes 14270464 | tf_op jit(solution)/shard_map/pallas_call | solution.py:208
  467.5 2.9 convolution_convert_fusion
  470.4 29.1 %shard_map.154 = bf16[8,64,1664]{2,1,0:T(8,128)(2,1)} custom-call(bf16[8,64,1664]{2,1,0:T(8,128)(2,1)} %bitcast.72), custom_call_target="tpu_custom_call" | custom-call | tf_op jit(solution)/shard_map/pallas_call | solution.py:93
  499.5 1.7 convert_reduce_fusion
  501.3 1.7 add_convert_fusion
  (98 shorter events, 4.1 us)
Async XLA Ops:
  7.2 170.2 %copy-start = (bf16[832,1664]{1,0:T(8,128)(2,1)S(1)}, bf16[832,1664]{1,0:T(8,128)(2,1)}, u32[]{:S(2)}) copy-start(bf16[832,1664]{1,0:T(8,128)(2,1)} %param.22) | copy-start | bytes 8306692
  7.2 41.8 %copy-start.18 = (f32[1664]{0:T(1024)S(1)}, f32[1664]{0:T(1024)}, u32[]{:S(2)}) copy-start(f32[1664]{0:T(1024)} %param.23) | copy-start | bytes 19972
  7.2 40.0 %all-gather.5.cloned.1.call-start = ((), (), s32[]{:S(2)}) async-start(), calls=%async_computation | async-start | bytes 1916928 | tf_op jit(solution)/shard_map/all_gather | solution.py:247
  7.9 186.2 %all-gather.7.cloned.1.call-start = ((), (), s32[]{:S(2)}) async-start(), calls=%async_computation.1 | async-start | bytes 14057472 | tf_op jit(solution)/shard_map/all_gather | solution.py:268
  8.5 44.2 %copy-start.4 = (f32[512,52]{0,1:T(8,128)}, f32[512,52]{0,1:T(8,128)S(1)}, u32[]{:S(2)}) copy-start(f32[512,52]{0,1:T(8,128)S(1)} %get-tuple-element.33) | copy-start | bytes 319492
  8.5 44.2 %copy-start.6 = (f32[512,52]{0,1:T(8,128)}, f32[512,52]{0,1:T(8,128)S(1)}, u32[]{:S(2)}) copy-start(f32[512,52]{0,1:T(8,128)S(1)} %get-tuple-element.34) | copy-start | bytes 319492
  52.6 1.2 copy-start.14
  52.6 1.3 copy-start.2
  52.6 1.6 copy-start.12
  53.7 215.2 %all-gather.9.cloned.1.call-start = ((), (), s32[]{:S(2)}) async-start(), calls=%async_computation.2 | async-start | bytes 1757184 | tf_op jit(solution)/shard_map/all_gather | solution.py:342
  75.9 2.1 copy-start.16
  105.1 4.1 copy-start.13
  177.3 17.4 %copy-start.15 = (s32[64]{0:T(128)S(1)}, s32[64]{0:T(128)}, u32[]{:S(2)}) copy-start(s32[64]{0:T(128)} %param.16) | copy-start | bytes 772
  179.8 100.8 %copy-start.3 = (bf16[512,1664]{1,0:T(8,128)(2,1)S(1)}, bf16[512,1664]{1,0:T(8,128)(2,1)}, u32[]{:S(2)}) copy-start(bf16[512,1664]{1,0:T(8,128)(2,1)} %all-gather.5.cloned.1.call-done) | copy-start | bytes 5111812
  194.1 152.6 %all-gather.11.cloned.1.call-start = ((), (), s32[]{:S(2)}) async-start(), calls=%async_computation.3 | async-start | bytes 3514368 | tf_op jit(solution)/shard_map/all_gather | solution.py:384
  280.6 2.0 copy-start.17
  282.6 1.5 copy-start.11
  284.1 0.9 copy-start.5
  284.1 1.0 copy-start.7
  284.1 1.8 copy-start.10
  285.3 27.4 %copy-start.9 = (bf16[512,2,104]{0,2,1:T(8,128)(2,1)}, bf16[512,2,104]{0,2,1:T(8,128)(2,1)S(1)}, u32[]{:S(2)}) copy-start(bf16[512,2,104]{0,2,1:T(8,128)(2,1)S(1)} %pad_maximum_fusion.3) | copy-start | bytes 638980
  422.6 45.0 %copy-start.8 = (bf16[208,1664]{1,0:T(8,128)(2,1)S(1)}, bf16[208,1664]{1,0:T(8,128)(2,1)}, u32[]{:S(2)}) copy-start(bf16[208,1664]{1,0:T(8,128)(2,1)} %param.25) | copy-start | bytes 2076676
  470.4 32.5 %copy-start.1 = (bf16[832,1664]{1,0:T(8,128)(2,1)S(1)}, bf16[832,1664]{1,0:T(8,128)(2,1)}, u32[]{:S(2)}) copy-start(bf16[832,1664]{1,0:T(8,128)(2,1)} %param.22) | copy-start | bytes 8306692
Sparse Core Ops, SparseCore 0:
  9.8 37.2 all-gather.4
  53.8 128.1 all-gather.6
  194.2 74.5 all-gather.8
  286.7 59.9 all-gather.10

commit v8 on v6

--- a/solution.py
+++ b/solution.py
@@ -49,12 +49,15 @@
 MESH_IDS = pl.DeviceIdType.MESH
 
 
-def exchange_kernel(axis, ways, gather, x_ref, y_ref, send_sem, recv_sem, local_sem):
-    me = lax.axis_index(axis)
+def exchange_kernel(axis, ways, stride, gather, x_ref, y_ref, send_sem, recv_sem, local_sem):
+    position = lax.axis_index(axis)
+    me = lax.rem(lax.div(position, stride), ways)
+    base = position - me * stride
     other = lax.axis_index("seq" if axis == "tp" else "tp")
 
-    def device(peer):
-        return (other, peer) if axis == "tp" else (peer, other)
+    def device(member):
+        index = base + member * stride
+        return (other, index) if axis == "tp" else (index, other)
 
     barrier = pltpu.get_barrier_semaphore()
     for shift in range(1, ways):
@@ -92,10 +95,10 @@
     local.wait()
 
 
-def tp_exchange(x, ways, gather, collective_id, axis="tp"):
+def tp_exchange(x, ways, gather, collective_id, axis="tp", stride=1):
     piece = x.shape if gather else x.shape[1:]
     return pl.pallas_call(
-        functools.partial(exchange_kernel, axis, ways, gather),
+        functools.partial(exchange_kernel, axis, ways, stride, gather),
         out_shape=jax.ShapeDtypeStruct((ways,) + tuple(piece), x.dtype),
         in_specs=[pl.BlockSpec(memory_space=pl.ANY)],
         out_specs=pl.BlockSpec(memory_space=pl.ANY),
@@ -106,6 +109,15 @@
         ],
         compiler_params=pltpu.CompilerParams(collective_id=collective_id, has_side_effects=True),
     )(x)
+
+
+def seq_gathered(piece, seq_ways, collective_ids):
+    inner = math.gcd(seq_ways, 8)
+    near = tp_exchange(piece, inner, True, collective_ids[0], "seq", 1)
+    if seq_ways == inner:
+        return near
+    far = tp_exchange(near, seq_ways // inner, True, collective_ids[1], "seq", inner)
+    return far.reshape((seq_ways,) + piece.shape)
 
 
 def summed_rows(term_task, own_rows, collective_id):
@@ -318,7 +330,7 @@
         1,
     )
     senders = rank_dest == seq_index
-    segment = tp_exchange(visual_part, seq_ways, True, 6, "seq").reshape(-1, model_width)
+    segment = seq_gathered(visual_part, seq_ways, (6, 7)).reshape(-1, model_width)
     row_count = segment.shape[0]
     sources = jnp.arange(row_count, dtype=jnp.int32) // part_rows
     wanted = jnp.any(
@@ -331,9 +343,8 @@
     arrived = jnp.dot(
         selector.astype(jnp.bfloat16), segment, preferred_element_type=jnp.float32
     ).astype(jnp.bfloat16)
-    both_blocks = tp_exchange(jnp.concatenate([text_rows, arrived], 0), tp_ways, True, 5)
-    text_block = both_blocks[:, : text_rows.shape[0]].reshape(-1, model_width)
-    visual_block = both_blocks[:, text_rows.shape[0] :].reshape(-1, model_width)
+    text_block = lax.all_gather(text_rows, "tp", axis=0, tiled=True)
+    visual_block = tp_exchange(arrived, tp_ways, True, 5).reshape(-1, model_width)
     landed = dest_table == seq_index
     local_starts = jnp.sum(jnp.where(landed, start_table - seq_index * rows_per_block, 0), 0)
     live_groups = jnp.sum(

time: 430 us -> 412 us (0.958)
  Pallas kernels: 244 us -> 226 us
    pallas_call x7 -> x8, Pallas kernels: 199 us -> 181 us  [tp_exchange(): pl.pallas_call(functools.partial(exchange_kernel, axis, ways, stride, gat...]
  transfers between devices with their start and end apart: 1 -> 2, of which waited for: 1 -> 1; matrix products, arithmetic and copies ran while one was open for 0% -> 9% of each run, Pallas kernels for 0% -> 37%
where the time goes in v8:
time: 412 us; the launch traced here: 411 us
  Pallas kernels  226 us (55%)
  waiting for transfers between devices  117 us (28%)
  matrix products  20.8 us (5%)
  other arithmetic  17.4 us (4%)
  local copies, waits for them, and re-layouts  15.2 us (4%)
  between operations  14.4 us (3%)
    pallas_call x8, Pallas kernels, tp_exchange(): pl.pallas_call(functools.partial(exchange_kernel, axis, ways, stride, gat...  181 us
    all_gather x1, waiting for transfers between devices, shards(): lax.all_gather(jnp.concatenate([key_flat, value_rows], 0), 'seq', axis=0,...  116 us
    pallas_call x1, Pallas kernels, causal_attention(): pl.pallas_call(attention_kernel, grid_spec=grid_spec, out_shape=jax.Shape...  44.8 us
  transfers between devices with their start and end apart: 2, of which 1 were waited for; matrix products, arithmetic and copies ran while one was open for 9% of the time, Pallas kernels for 37%

profile of v8, /device:TPU:223, one launch (start us, length us, event | category | flops | bytes accessed | tf_op | source)
XLA Modules:
  0.0 410.9 jit_solution(13101377275490685370)
XLA Ops:
  7.2 0.7 all-gather.3.cloned.1.call-update
  8.0 0.8 reshape.236
  8.8 0.7 dynamic_slice.9
  9.6 1.0 convert_reduce_fusion.2
  10.6 1.1 fusion.21
  11.8 1.8 fusion.23.x_ref
  13.5 34.5 %shard_map.148 = bf16[8,2,32,1664]{3,2,1,0:T(8,128)(2,1)} custom-call(bf16[2,32,1664]{2,1,0:T(8,128)(2,1)} %fusion.23.x_ref), custom_call_target="tpu_custom_call" | custom-call | tf_op jit(solution)/shard_map/pallas_call | solution.py:100
  48.0 1.8 copy.42
  49.8 0.3 copy-done.6
  50.1 1.3 convolution_convert_fusion.5
  51.6 0.6 fusion.60
  52.1 1.3 fusion.12
  54.0 2.6 fusion.14
  56.6 1.1 copy.44
  57.8 0.2 dot_general.32
  58.0 3.0 convolution_convert_fusion.2.x_ref
  61.0 19.8 %shard_map.149 = bf16[8,64,1664]{2,1,0:T(8,128)(2,1)} custom-call(bf16[8,64,1664]{2,1,0:T(8,128)(2,1)} %convolution_convert_fusion.2.x_ref), custom_call_target="tpu_custom_call" | custom-call | tf_op jit(solution)/shard_map/pallas_call | solution.py:100
  80.8 2.6 convert_reduce_fusion.1
  83.3 1.3 reshape.243
  84.6 0.1 convert_reduce_fusion.3
  84.7 0.2 fusion.24
  85.0 0.8 fusion.26.x_ref
  85.8 22.6 %shard_map.150 = bf16[8,2,32,1664]{3,2,1,0:T(8,128)(2,1)} custom-call(bf16[2,32,1664]{2,1,0:T(8,128)(2,1)} %fusion.26.x_ref), custom_call_target="tpu_custom_call" | custom-call | tf_op jit(solution)/shard_map/pallas_call | solution.py:100
  108.4 2.8 copy.46
  111.2 3.9 reshape_reshape.6
  115.1 2.4 convolution_convert_fusion.3
  117.5 9.5 %shard_map.151 = bf16[8,16,1664]{2,1,0:T(8,128)(2,1)} custom-call(bf16[8,16,1664]{2,1,0:T(8,128)(2,1)} %bitcast.59), custom_call_target="tpu_custom_call" | custom-call | tf_op jit(solution)/shard_map/pallas_call | solution.py:100
  127.0 1.7 reduce_sum.120.x_ref
  128.7 13.2 %shard_map.152.x_ref = bf16[8,16,1664]{2,1,0:T(8,128)(2,1)} custom-call(bf16[16,1664]{1,0:T(8,128)(2,1)} %reduce_sum.120.x_ref), custom_call_target="tpu_custom_call" | custom-call | tf_op jit(solution)/shard_map/pallas_call | solution.py:100
  142.0 43.5 %shard_map.153 = bf16[4,8,16,1664]{3,2,1,0:T(8,128)(2,1)} custom-call(bf16[8,16,1664]{2,1,0:T(8,128)(2,1)} %shard_map.152.x_ref), custom_call_target="tpu_custom_call" | custom-call | tf_op jit(solution)/shard_map/pallas_call | solution.py:100
  185.6 2.4 convolution_convert_fusion.4.x_ref
  188.0 8.9 %shard_map.154 = bf16[8,16,1664]{2,1,0:T(8,128)(2,1)} custom-call(bf16[16,1664]{1,0:T(8,128)(2,1)} %convolution_convert_fusion.4.x_ref), custom_call_target="tpu_custom_call" | custom-call | tf_op jit(solution)/shard_map/pallas_call | solution.py:100
  196.9 0.2 fusion.30
  197.1 0.5 multiply_cosine_fusion
  197.6 2.6 fusion.1
  200.2 1.5 fusion.5
  201.7 0.7 slice.60
  202.5 0.8 subtract_convert_fusion
  203.4 0.1 copy.48
  203.5 1.1 copy.51
  204.6 0.9 pad_maximum_fusion
  205.5 1.7 pad_maximum_fusion.1
  207.2 116.3 %all-gather.5.cloned.1.call-done.k_ref.v_ref = bf16[32768,208]{1,0:T(8,128)(2,1)} async-done(((bf16[1024,208]{1,0:T(8,128)(2,1)}), bf16[32768,208]{1,0:T(8,128)(2,1)}) %all-gather.5.cloned.1.call-update) | async-done | bytes 13631504 | tf_op jit(solution)/shard_map/all_gather | solution.py:380
  323.5 44.8 %shard_map.155 = f32[208,512]{1,0:T(8,128)} custom-call(s32[1]{0:T(128)} %bitcast.17.meta_ref, s32[32]{0:T(128)} %lengths_ref.1, bf16[208,512]{1,0:T(8,128)(2,1)} %bitcast.69, bf16[32768,208]{1,0:T(8,128)(2,1)} %all-gather.5.cloned.1.call-done.k_ref.v_ref, bf16[32768,208]{1,0:T(8,128)(2,1)} %all-gather.5.cloned.1.call-done.k_ref.v_ref), custom_call_target="tpu_custom_call" | custom-call | flops 13958643712 | bytes 14270464 | tf_op jit(solution)/shard_map/pallas_call | solution.py:224
  368.3 3.1 convolution_convert_fusion
  371.4 29.2 %shard_map.156 = bf16[8,64,1664]{2,1,0:T(8,128)(2,1)} custom-call(bf16[8,64,1664]{2,1,0:T(8,128)(2,1)} %bitcast.55), custom_call_target="tpu_custom_call" | custom-call | tf_op jit(solution)/shard_map/pallas_call | solution.py:100
  400.6 1.7 convert_reduce_fusion
  402.4 1.7 add_convert_fusion
  (43 shorter events, 1.1 us)
Async XLA Ops:
  7.2 107.9 %copy-start = (bf16[832,1664]{1,0:T(8,128)(2,1)S(1)}, bf16[832,1664]{1,0:T(8,128)(2,1)}, u32[]{:S(2)}) copy-start(bf16[832,1664]{1,0:T(8,128)(2,1)} %param.22) | copy-start | bytes 8306692
  7.2 190.4 %all-gather.3.cloned.1.call-start = ((), (), s32[]{:S(2)}) async-start(), calls=%async_computation | async-start | bytes 1916928 | tf_op jit(solution)/shard_map/all_gather | solution.py:346
  7.9 315.6 %all-gather.5.cloned.1.call-start = ((), (), s32[]{:S(2)}) async-start(), calls=%async_computation.1 | async-start | bytes 17301504 | tf_op jit(solution)/shard_map/all_gather | solution.py:380
  48.0 2.1 copy-start.6
  51.5 1.9 copy-start.5
  80.7 3.8 copy-start.1
  80.8 4.2 %copy-start.4 = (f32[1664]{0:T(1024)S(1)}, f32[1664]{0:T(1024)}, u32[]{:S(2)}) copy-start(f32[1664]{0:T(1024)} %param.21) | copy-start | bytes 19972
  197.6 2.6 copy-start.7
  197.6 2.6 copy-start.8
  200.2 1.5 copy-start.3
  203.4 165.0 %copy-start.2 = (bf16[512,2,104]{0,2,1:T(8,128)(2,1)}, bf16[512,2,104]{0,2,1:T(8,128)(2,1)S(1)}, u32[]{:S(2)}) copy-start(bf16[512,2,104]{0,2,1:T(8,128)(2,1)S(1)} %pad_maximum_fusion.2) | copy-start | bytes 638980
Sparse Core Ops, SparseCore 0:
  9.8 49.0 all-gather.2
  205.6 117.8 all-gather.4

commit v9 on v8

--- a/solution.py
+++ b/solution.py
@@ -113,11 +113,11 @@
 
 def seq_gathered(piece, seq_ways, collective_ids):
     inner = math.gcd(seq_ways, 8)
-    near = tp_exchange(piece, inner, True, collective_ids[0], "seq", 1)
     if seq_ways == inner:
-        return near
-    far = tp_exchange(near, seq_ways // inner, True, collective_ids[1], "seq", inner)
-    return far.reshape((seq_ways,) + piece.shape)
+        return tp_exchange(piece, inner, True, collective_ids[0], "seq", 1)
+    far = tp_exchange(piece, seq_ways // inner, True, collective_ids[1], "seq", inner)
+    near = tp_exchange(far, inner, True, collective_ids[0], "seq", 1)
+    return jnp.swapaxes(near, 0, 1).reshape((seq_ways,) + piece.shape)
 
 
 def summed_rows(term_task, own_rows, collective_id):

time: 412 us -> 391 us (0.949)
  Pallas kernels: 226 us -> 206 us
    pallas_call x8, Pallas kernels: 181 us -> 161 us  [tp_exchange(): pl.pallas_call(functools.partial(exchange_kernel, axis, ways, stride, gat...]
  transfers between devices with their start and end apart: 2 -> 2, of which waited for: 1 -> 1; matrix products, arithmetic and copies ran while one was open for 9% -> 10% of each run, Pallas kernels for 37% -> 34%
where the time goes in v9:
time: 391 us
  Pallas kernels  206 us (53%)
  waiting for transfers between devices  117 us (30%)
  matrix products  19.3 us (5%)
  other arithmetic  17.4 us (4%)
  local copies, waits for them, and re-layouts  16.8 us (4%)
  between operations  14.4 us (4%)
    pallas_call x8, Pallas kernels, tp_exchange(): pl.pallas_call(functools.partial(exchange_kernel, axis, ways, stride, gat...  161 us
    all_gather x1, waiting for transfers between devices, shards(): lax.all_gather(jnp.concatenate([key_flat, value_rows], 0), 'seq', axis=0,...  116 us
    pallas_call x1, Pallas kernels, causal_attention(): pl.pallas_call(attention_kernel, grid_spec=grid_spec, out_shape=jax.Shape...  44.8 us
  transfers between devices with their start and end apart: 2, of which 1 were waited for; matrix products, arithmetic and copies ran while one was open for 10% of the time, Pallas kernels for 34%

profile of v9, /device:TPU:223, one launch (start us, length us, event | category | flops | bytes accessed | tf_op | source)
XLA Modules:
  0.0 390.5 jit_solution(4037875201726332012)
XLA Ops:
  7.2 0.7 all-gather.3.cloned.1.call-update
  8.0 0.8 reshape.236
  8.8 0.7 dynamic_slice.9
  9.6 1.0 convert_reduce_fusion.2
  10.6 1.1 fusion.21
  11.8 1.8 fusion.23.x_ref
  13.5 34.5 %shard_map.148 = bf16[8,2,32,1664]{3,2,1,0:T(8,128)(2,1)} custom-call(bf16[2,32,1664]{2,1,0:T(8,128)(2,1)} %fusion.23.x_ref), custom_call_target="tpu_custom_call" | custom-call | tf_op jit(solution)/shard_map/pallas_call | solution.py:100
  48.0 1.8 copy.44
  49.8 0.3 copy-done.6
  50.1 1.3 convolution_convert_fusion.5
  51.6 0.6 fusion.60
  52.1 1.3 fusion.12
  54.0 2.6 fusion.14
  56.6 1.1 copy.46
  57.8 0.2 dot_general.32
  58.0 3.0 convolution_convert_fusion.2.x_ref
  61.0 19.8 %shard_map.149 = bf16[8,64,1664]{2,1,0:T(8,128)(2,1)} custom-call(bf16[8,64,1664]{2,1,0:T(8,128)(2,1)} %convolution_convert_fusion.2.x_ref), custom_call_target="tpu_custom_call" | custom-call | tf_op jit(solution)/shard_map/pallas_call | solution.py:100
  80.8 2.6 convert_reduce_fusion.1
  83.3 1.3 reshape.243
  84.7 0.2 fusion.24
  85.0 0.8 fusion.26.x_ref
  85.8 22.6 %shard_map.150 = bf16[8,2,32,1664]{3,2,1,0:T(8,128)(2,1)} custom-call(bf16[2,32,1664]{2,1,0:T(8,128)(2,1)} %fusion.26.x_ref), custom_call_target="tpu_custom_call" | custom-call | tf_op jit(solution)/shard_map/pallas_call | solution.py:100
  108.4 2.8 copy.48
  111.2 3.9 reshape_reshape.6
  115.1 2.4 convolution_convert_fusion.3
  117.5 9.5 %shard_map.151 = bf16[8,16,1664]{2,1,0:T(8,128)(2,1)} custom-call(bf16[8,16,1664]{2,1,0:T(8,128)(2,1)} %bitcast.61), custom_call_target="tpu_custom_call" | custom-call | tf_op jit(solution)/shard_map/pallas_call | solution.py:100
  127.0 1.7 reduce_sum.120.x_ref
  128.7 8.5 %shard_map.152.x_ref = bf16[4,16,1664]{2,1,0:T(8,128)(2,1)} custom-call(bf16[16,1664]{1,0:T(8,128)(2,1)} %reduce_sum.120.x_ref), custom_call_target="tpu_custom_call" | custom-call | tf_op jit(solution)/shard_map/pallas_call | solution.py:100
  137.2 28.2 %shard_map.153 = bf16[8,4,16,1664]{3,2,1,0:T(8,128)(2,1)} custom-call(bf16[4,16,1664]{2,1,0:T(8,128)(2,1)} %shard_map.152.x_ref), custom_call_target="tpu_custom_call" | custom-call | tf_op jit(solution)/shard_map/pallas_call | solution.py:100
  165.4 1.6 copy.49
  167.2 1.0 convolution_convert_fusion.4.x_ref
  168.1 8.7 %shard_map.154 = bf16[8,16,1664]{2,1,0:T(8,128)(2,1)} custom-call(bf16[16,1664]{1,0:T(8,128)(2,1)} %convolution_convert_fusion.4.x_ref), custom_call_target="tpu_custom_call" | custom-call | tf_op jit(solution)/shard_map/pallas_call | solution.py:100
  176.8 0.2 fusion.30
  177.0 0.5 multiply_cosine_fusion
  177.5 2.6 fusion.1
  180.1 1.5 fusion.5
  181.6 0.7 slice.60
  182.4 0.8 subtract_convert_fusion
  183.3 0.1 copy.51
  183.4 1.1 copy.54
  184.5 0.9 pad_maximum_fusion
  185.4 1.7 pad_maximum_fusion.1
  187.1 116.1 %all-gather.5.cloned.1.call-done.k_ref.v_ref = bf16[32768,208]{1,0:T(8,128)(2,1)} async-done(((bf16[1024,208]{1,0:T(8,128)(2,1)}), bf16[32768,208]{1,0:T(8,128)(2,1)}) %all-gather.5.cloned.1.call-update) | async-done | bytes 13631504 | tf_op jit(solution)/shard_map/all_gather | solution.py:380
  303.2 44.8 %shard_map.155 = f32[208,512]{1,0:T(8,128)} custom-call(s32[1]{0:T(128)} %bitcast.18.meta_ref, s32[32]{0:T(128)} %lengths_ref.1, bf16[208,512]{1,0:T(8,128)(2,1)} %bitcast.71, bf16[32768,208]{1,0:T(8,128)(2,1)} %all-gather.5.cloned.1.call-done.k_ref.v_ref, bf16[32768,208]{1,0:T(8,128)(2,1)} %all-gather.5.cloned.1.call-done.k_ref.v_ref), custom_call_target="tpu_custom_call" | custom-call | flops 13958643712 | bytes 14270464 | tf_op jit(solution)/shard_map/pallas_call | solution.py:224
  348.0 3.1 convolution_convert_fusion
  351.1 29.1 %shard_map.156 = bf16[8,64,1664]{2,1,0:T(8,128)(2,1)} custom-call(bf16[8,64,1664]{2,1,0:T(8,128)(2,1)} %bitcast.57), custom_call_target="tpu_custom_call" | custom-call | tf_op jit(solution)/shard_map/pallas_call | solution.py:100
  380.3 1.7 convert_reduce_fusion
  382.0 1.7 add_convert_fusion
  (44 shorter events, 1.2 us)
Async XLA Ops:
  7.2 107.9 %copy-start = (bf16[832,1664]{1,0:T(8,128)(2,1)S(1)}, bf16[832,1664]{1,0:T(8,128)(2,1)}, u32[]{:S(2)}) copy-start(bf16[832,1664]{1,0:T(8,128)(2,1)} %param.22) | copy-start | bytes 8306692
  7.2 170.3 %all-gather.3.cloned.1.call-start = ((), (), s32[]{:S(2)}) async-start(), calls=%async_computation | async-start | bytes 1916928 | tf_op jit(solution)/shard_map/all_gather | solution.py:346
  7.9 295.3 %all-gather.5.cloned.1.call-start = ((), (), s32[]{:S(2)}) async-start(), calls=%async_computation.1 | async-start | bytes 17301504 | tf_op jit(solution)/shard_map/all_gather | solution.py:380
  48.0 2.1 copy-start.6
  51.5 1.9 copy-start.5
  80.7 3.8 copy-start.1
  80.8 4.2 %copy-start.4 = (f32[1664]{0:T(1024)S(1)}, f32[1664]{0:T(1024)}, u32[]{:S(2)}) copy-start(f32[1664]{0:T(1024)} %param.21) | copy-start | bytes 19972
  177.5 2.6 copy-start.7
  177.5 2.6 copy-start.8
  180.1 1.5 copy-start.3
  183.3 164.8 %copy-start.2 = (bf16[512,2,104]{0,2,1:T(8,128)(2,1)}, bf16[512,2,104]{0,2,1:T(8,128)(2,1)S(1)}, u32[]{:S(2)}) copy-start(bf16[512,2,104]{0,2,1:T(8,128)(2,1)S(1)} %pad_maximum_fusion.2) | copy-start | bytes 638980
Sparse Core Ops, SparseCore 0:
  9.8 49.0 all-gather.2
  185.5 117.6 all-gather.4

commit v10 on v9

--- a/solution.py
+++ b/solution.py
@@ -140,7 +140,7 @@
     step = pl.program_id(0)
     seq = meta_ref[0]
     width, rows = qt_ref.shape
-    span = k_ref.shape[0]
+    span = k_ref.shape[1]
     heads = width // HEAD
     score_scale = 1.0 / math.sqrt(HEAD)
 
@@ -164,7 +164,13 @@
         for h in range(heads):
             in_head = (feature >= h * HEAD) & (feature < (h + 1) * HEAD)
             qt_head = jnp.where(in_head, qt, jnp.zeros_like(qt))
-            scores = jnp.dot(k, qt_head, preferred_element_type=jnp.float32) * score_scale + bias
+            scores = (
+                lax.dot_general(
+                    k, qt_head, (((0,), (0,)), ((), ())), preferred_element_type=jnp.float32
+                )
+                * score_scale
+                + bias
+            )
             if diagonal:
                 scores = jnp.where(causal, scores, MASKED_SCORE)
             m_prev = m_sc[h]
@@ -172,12 +178,7 @@
             weights = jnp.exp(scores - m_new)
             alpha = jnp.exp(m_prev - m_new)
             l_sc[h] = alpha * l_sc[h] + jnp.sum(weights, axis=0, keepdims=True)
-            mixed = lax.dot_general(
-                v,
-                weights.astype(jnp.bfloat16),
-                (((0,), (0,)), ((), ())),
-                preferred_element_type=jnp.float32,
-            )
+            mixed = jnp.dot(v, weights.astype(jnp.bfloat16), preferred_element_type=jnp.float32)
             acc_sc[h] = acc_sc[h] * alpha + mixed
             m_sc[h] = m_new
 
@@ -202,7 +203,7 @@
 def causal_attention(query_flat, key_value_all, seq_index, block_lengths, rows_per_block):
     rows, width = query_flat.shape
     span = rows_per_block
-    steps = key_value_all.shape[0] // (2 * span)
+    steps = key_value_all.shape[0] // (2 * width)
     heads = width // HEAD
     meta = jnp.reshape(seq_index, (1,)).astype(jnp.int32)
     grid_spec = pltpu.PrefetchScalarGridSpec(
@@ -210,8 +211,8 @@
         grid=(steps,),
         in_specs=[
             pl.BlockSpec((width, rows), lambda i, m, n: (0, 0)),
-            pl.BlockSpec((span, width), lambda i, m, n: (2 * jnp.minimum(i, m[0]), 0)),
-            pl.BlockSpec((span, width), lambda i, m, n: (2 * jnp.minimum(i, m[0]) + 1, 0)),
+            pl.BlockSpec((width, span), lambda i, m, n: (2 * jnp.minimum(i, m[0]), 0)),
+            pl.BlockSpec((width, span), lambda i, m, n: (2 * jnp.minimum(i, m[0]) + 1, 0)),
         ],
         out_specs=pl.BlockSpec((width, rows), lambda i, m, n: (0, 0)),
         scratch_shapes=[
@@ -378,7 +379,10 @@
     value_rows = text_heads[:, 2 * local_width :].astype(jnp.bfloat16)
     key_flat = key_rows.reshape(rows_per_block, local_width)
     key_value_all = lax.all_gather(
-        jnp.concatenate([key_flat, value_rows], 0), "seq", axis=0, tiled=True
+        jnp.concatenate([jnp.transpose(key_flat), jnp.transpose(value_rows)], 0),
+        "seq",
+        axis=0,
+        tiled=True,
     )
     attended_rows = causal_attention(
         query_rows.reshape(rows_per_block, local_width),

time: 391 us -> 376 us (0.962)
  waiting for transfers between devices: 117 us -> 101 us
    all_gather x1, waiting for transfers between devices: 116 us -> 100 us  [shards(): lax.all_gather(jnp.concatenate([jnp.transpose(key_flat), jnp.transpose(va...]
  transfers between devices with their start and end apart: 2 -> 2, of which waited for: 1 -> 1; matrix products, arithmetic and copies ran while one was open for 10% -> 11% of each run, Pallas kernels for 34% -> 35%
where the time goes in v10:
time: 376 us; the launch traced here: 375 us
  Pallas kernels  207 us (55%)
  waiting for transfers between devices  101 us (27%)
  matrix products  19.3 us (5%)
  local copies, waits for them, and re-layouts  17.4 us (5%)
  other arithmetic  15.7 us (4%)
  between operations  14.4 us (4%)
    pallas_call x8, Pallas kernels, tp_exchange(): pl.pallas_call(functools.partial(exchange_kernel, axis, ways, stride, gat...  161 us
    all_gather x1, waiting for transfers between devices, shards(): lax.all_gather(jnp.concatenate([jnp.transpose(key_flat), jnp.transpose(va...  100 us
    pallas_call x1, Pallas kernels, causal_attention(): pl.pallas_call(attention_kernel, grid_spec=grid_spec, out_shape=jax.Shape...  45.9 us
  transfers between devices with their start and end apart: 2, of which 1 were waited for; matrix products, arithmetic and copies ran while one was open for 11% of the time, Pallas kernels for 35%

profile of v10, /device:TPU:223, one launch (start us, length us, event | category | flops | bytes accessed | tf_op | source)
XLA Modules:
  0.0 374.8 jit_solution(494842327745901744)
XLA Ops:
  7.2 0.7 all-gather.3.cloned.1.call-update
  8.0 0.8 reshape.236
  8.8 0.7 dynamic_slice.9
  9.6 1.0 convert_reduce_fusion.2
  10.6 1.1 fusion.21
  11.8 1.8 fusion.23.x_ref
  13.5 34.5 %shard_map.148 = bf16[8,2,32,1664]{3,2,1,0:T(8,128)(2,1)} custom-call(bf16[2,32,1664]{2,1,0:T(8,128)(2,1)} %fusion.23.x_ref), custom_call_target="tpu_custom_call" | custom-call | tf_op jit(solution)/shard_map/pallas_call | solution.py:100
  48.0 1.8 copy.24
  49.8 0.3 copy-done.7
  50.1 1.3 convolution_convert_fusion.5
  51.6 0.6 fusion.60
  52.1 1.3 fusion.12
  54.0 2.6 fusion.14
  56.6 1.1 copy.26
  57.8 0.2 dot_general.32
  58.0 3.0 convolution_convert_fusion.2.x_ref
  61.0 19.8 %shard_map.149 = bf16[8,64,1664]{2,1,0:T(8,128)(2,1)} custom-call(bf16[8,64,1664]{2,1,0:T(8,128)(2,1)} %convolution_convert_fusion.2.x_ref), custom_call_target="tpu_custom_call" | custom-call | tf_op jit(solution)/shard_map/pallas_call | solution.py:100
  80.8 2.6 convert_reduce_fusion.1
  83.3 1.3 reshape.243
  84.6 0.1 convert_reduce_fusion.3
  84.7 0.2 fusion.24
  85.0 0.8 fusion.26.x_ref
  85.8 22.6 %shard_map.150 = bf16[8,2,32,1664]{3,2,1,0:T(8,128)(2,1)} custom-call(bf16[2,32,1664]{2,1,0:T(8,128)(2,1)} %fusion.26.x_ref), custom_call_target="tpu_custom_call" | custom-call | tf_op jit(solution)/shard_map/pallas_call | solution.py:100
  108.4 2.8 copy.28
  111.2 3.9 %reshape_reshape.6 = bf16[128,6656]{1,0:T(8,128)(2,1)} reshape(bf16[2,8,32,1664]{3,2,1,0:T(8,128)(2,1)} %copy.28) | data formatting | bytes 3407872 | tf_op jit(solution)/shard_map/reshape;reshape | solution.py:315
  115.1 2.4 convolution_convert_fusion.3
  117.5 9.5 %shard_map.151 = bf16[8,16,1664]{2,1,0:T(8,128)(2,1)} custom-call(bf16[8,16,1664]{2,1,0:T(8,128)(2,1)} %bitcast.65), custom_call_target="tpu_custom_call" | custom-call | tf_op jit(solution)/shard_map/pallas_call | solution.py:100
  127.0 1.7 reduce_sum.120.x_ref
  128.7 8.5 %shard_map.152.x_ref = bf16[4,16,1664]{2,1,0:T(8,128)(2,1)} custom-call(bf16[16,1664]{1,0:T(8,128)(2,1)} %reduce_sum.120.x_ref), custom_call_target="tpu_custom_call" | custom-call | tf_op jit(solution)/shard_map/pallas_call | solution.py:100
  137.2 28.2 %shard_map.153 = bf16[8,4,16,1664]{3,2,1,0:T(8,128)(2,1)} custom-call(bf16[4,16,1664]{2,1,0:T(8,128)(2,1)} %shard_map.152.x_ref), custom_call_target="tpu_custom_call" | custom-call | tf_op jit(solution)/shard_map/pallas_call | solution.py:100
  165.4 1.6 copy.29
  167.2 1.0 convolution_convert_fusion.4.x_ref
  168.1 8.7 %shard_map.154 = bf16[8,16,1664]{2,1,0:T(8,128)(2,1)} custom-call(bf16[16,1664]{1,0:T(8,128)(2,1)} %convolution_convert_fusion.4.x_ref), custom_call_target="tpu_custom_call" | custom-call | tf_op jit(solution)/shard_map/pallas_call | solution.py:100
  176.8 0.2 fusion.30
  177.0 0.5 multiply_cosine_fusion
  177.5 2.6 fusion.1
  180.1 1.5 fusion.5
  181.7 0.2 subtract_convert_fusion
  181.9 0.8 copy-done.2
  182.7 0.8 pad_maximum_fusion
  183.6 1.7 slice.60
  185.3 0.7 pad_maximum_fusion.1
  186.0 100.4 %all-gather.5.cloned.1.call-done.k_ref.v_ref = bf16[13312,512]{1,0:T(8,128)(2,1)} async-done(((bf16[416,512]{1,0:T(8,128)(2,1)}), bf16[13312,512]{1,0:T(8,128)(2,1)}) %all-gather.5.cloned.1.call-update) | async-done | bytes 13631504 | tf_op jit(solution)/shard_map/all_gather | solution.py:381
  286.4 45.9 %shard_map.155 = f32[208,512]{1,0:T(8,128)} custom-call(s32[1]{0:T(128)} %bitcast.18.meta_ref, s32[32]{0:T(128)} %lengths_ref.1, bf16[208,512]{1,0:T(8,128)(2,1)} %bitcast.75, bf16[13312,512]{1,0:T(8,128)(2,1)} %all-gather.5.cloned.1.call-done.k_ref.v_ref, bf16[13312,512]{1,0:T(8,128)(2,1)} %all-gather.5.cloned.1.call-done.k_ref.v_ref), custom_call_target="tpu_custom_call" | custom-call | flops 13958643712 | bytes 14270464 | tf_op jit(solution)/shard_map/pallas_call | solution.py:225
  332.4 3.1 convolution_convert_fusion
  335.5 29.1 %shard_map.156 = bf16[8,64,1664]{2,1,0:T(8,128)(2,1)} custom-call(bf16[8,64,1664]{2,1,0:T(8,128)(2,1)} %bitcast.61), custom_call_target="tpu_custom_call" | custom-call | tf_op jit(solution)/shard_map/pallas_call | solution.py:100
  364.6 1.7 convert_reduce_fusion
  366.3 1.7 add_convert_fusion
  (45 shorter events, 1.1 us)
Async XLA Ops:
  7.2 107.9 %copy-start = (bf16[832,1664]{1,0:T(8,128)(2,1)S(1)}, bf16[832,1664]{1,0:T(8,128)(2,1)}, u32[]{:S(2)}) copy-start(bf16[832,1664]{1,0:T(8,128)(2,1)} %param.22) | copy-start | bytes 8306692
  7.2 170.3 %all-gather.3.cloned.1.call-start = ((), (), s32[]{:S(2)}) async-start(), calls=%async_computation | async-start | bytes 1916928 | tf_op jit(solution)/shard_map/all_gather | solution.py:347
  7.9 278.5 %all-gather.5.cloned.1.call-start = ((), (), s32[]{:S(2)}) async-start(), calls=%async_computation.1 | async-start | bytes 14057472 | tf_op jit(solution)/shard_map/all_gather | solution.py:381
  48.0 2.1 copy-start.7
  51.5 1.9 copy-start.6
  80.7 3.8 %copy-start.1 = (bf16[2,32,1664]{2,1,0:T(8,128)(2,1)S(1)}, bf16[2,32,1664]{2,1,0:T(8,128)(2,1)}, u32[]{:S(2)}) copy-start(bf16[2,32,1664]{2,1,0:T(8,128)(2,1)} %param.13) | copy-start | bytes 638980
  80.8 4.2 %copy-start.5 = (f32[1664]{0:T(1024)S(1)}, f32[1664]{0:T(1024)}, u32[]{:S(2)}) copy-start(f32[1664]{0:T(1024)} %param.21) | copy-start | bytes 19972
  177.5 2.6 copy-start.8
  177.5 2.6 copy-start.9
  180.1 1.5 copy-start.4
  181.6 1.1 copy-start.2
  182.7 149.6 %copy-start.3 = (bf16[512,2,104]{0,2,1:T(8,128)(2,1)}, bf16[512,2,104]{0,2,1:T(8,128)(2,1)S(1)}, u32[]{:S(2)}) copy-start(bf16[512,2,104]{0,2,1:T(8,128)(2,1)S(1)} %pad_maximum_fusion.2) | copy-start | bytes 638980
Sparse Core Ops, SparseCore 0:
  9.8 49.0 all-gather.2
  183.7 102.6 all-gather.4

commit v11 on v10

--- a/solution.py
+++ b/solution.py
@@ -311,9 +311,18 @@
     merge_input = layer_normed(vision_rows, merge_gain).astype(jnp.bfloat16)
     merged_total = patch_total // 4
     input_share = merge_weight.shape[0]
-    whole_pictures = gathered_patches(merge_input, 1)
-    merged_rows = whole_pictures.reshape(picture_total * merged_total, 4 * model_width)
-    owned_inputs = lax.dynamic_slice_in_dim(merged_rows, tp_index * input_share, input_share, 1)
+    groups = input_share * tp_ways // model_width
+    halves = tp_ways // groups
+    outgoing = merge_input.reshape(
+        picture_total, local_patches // groups, groups, halves, input_share
+    )
+    outgoing = jnp.transpose(outgoing, (2, 3, 0, 1, 4)).reshape(
+        tp_ways, picture_total, local_patches // groups, input_share
+    )
+    incoming = tp_exchange(outgoing, tp_ways, False, 1)
+    owned_inputs = jnp.transpose(incoming, (1, 0, 2, 3)).reshape(
+        picture_total * merged_total, input_share
+    )
 
     def merge_term(offset, row_count):
         return jnp.dot(owned_inputs, merge_weight, preferred_element_type=jnp.float32)

time: 376 us -> 358 us (0.952)
  Pallas kernels: 207 us -> 196 us
  local copies, waits for them, and re-layouts: 17.4 us -> 12.7 us
    pallas_call x8, Pallas kernels: 161 us -> 149 us  [tp_exchange(): pl.pallas_call(functools.partial(exchange_kernel, axis, ways, stride, gat...]
    another operation x1 -> x0, local copies, waits for them, and re-layouts: 3.89 us -> none  [shards(): whole_pictures.reshape(picture_total * merged_total, 4 * model_width)]
  transfers between devices with their start and end apart: 2 -> 2, of which waited for: 1 -> 1; matrix products, arithmetic and copies ran while one was open for 11% -> 9% of each run, Pallas kernels for 35% -> 34%
where the time goes in v11:
time: 358 us; the launch traced here: 357 us
  Pallas kernels  196 us (55%)
  waiting for transfers between devices  101 us (28%)
  matrix products  18.3 us (5%)
  other arithmetic  15 us (4%)
  between operations  14.4 us (4%)
  local copies, waits for them, and re-layouts  12.7 us (4%)
    pallas_call x8, Pallas kernels, tp_exchange(): pl.pallas_call(functools.partial(exchange_kernel, axis, ways, stride, gat...  149 us
    all_gather x1, waiting for transfers between devices, shards(): lax.all_gather(jnp.concatenate([jnp.transpose(key_flat), jnp.transpose(va...  100 us
    pallas_call x1, Pallas kernels, causal_attention(): pl.pallas_call(attention_kernel, grid_spec=grid_spec, out_shape=jax.Shape...  46.2 us
  transfers between devices with their start and end apart: 2, of which 1 were waited for; matrix products, arithmetic and copies ran while one was open for 9% of the time, Pallas kernels for 34%

profile of v11, /device:TPU:223, one launch (start us, length us, event | category | flops | bytes accessed | tf_op | source)
XLA Modules:
  0.0 357.2 jit_solution(13350743007427677404)
XLA Ops:
  7.2 0.7 all-gather.3.cloned.1.call-update
  8.0 0.8 reshape.244
  8.8 0.7 dynamic_slice.6
  9.6 1.0 convert_reduce_fusion.2
  10.6 1.1 fusion.26
  11.8 1.8 fusion.28.x_ref
  13.5 34.5 %shard_map.148 = bf16[8,2,32,1664]{3,2,1,0:T(8,128)(2,1)} custom-call(bf16[2,32,1664]{2,1,0:T(8,128)(2,1)} %fusion.28.x_ref), custom_call_target="tpu_custom_call" | custom-call | tf_op jit(solution)/shard_map/pallas_call | solution.py:100
  48.0 1.8 copy.26
  49.8 0.3 copy-done.7
  50.1 1.3 convolution_convert_fusion.4
  51.6 0.6 fusion.63
  52.1 1.3 fusion.17
  54.0 2.6 fusion.19
  56.6 1.1 copy.28
  57.8 0.2 dot_general.34
  58.0 3.0 convolution_convert_fusion.2.x_ref
  61.0 19.8 %shard_map.149 = bf16[8,64,1664]{2,1,0:T(8,128)(2,1)} custom-call(bf16[8,64,1664]{2,1,0:T(8,128)(2,1)} %convolution_convert_fusion.2.x_ref), custom_call_target="tpu_custom_call" | custom-call | tf_op jit(solution)/shard_map/pallas_call | solution.py:100
  80.8 2.6 convert_reduce_fusion.1
  83.3 1.3 reshape.251
  84.7 0.2 fusion.29
  85.0 0.1 fusion.31
  85.1 0.2 reshape.252
  85.3 0.7 copy.30
  86.1 7.6 %shard_map.150 = bf16[8,2,8,832]{3,2,1,0:T(8,128)(2,1)} custom-call(bf16[8,2,8,832]{3,2,1,0:T(8,128)(2,1)} %bitcast.71), custom_call_target="tpu_custom_call" | custom-call | tf_op jit(solution)/shard_map/pallas_call | solution.py:100
  93.6 1.0 copy.31
  94.6 1.4 fusion.7.x_ref
  96.0 7.9 %shard_map.151 = bf16[8,16,1664]{2,1,0:T(8,128)(2,1)} custom-call(bf16[8,16,1664]{2,1,0:T(8,128)(2,1)} %fusion.7.x_ref), custom_call_target="tpu_custom_call" | custom-call | tf_op jit(solution)/shard_map/pallas_call | solution.py:100
  103.9 1.7 reduce_sum.120.x_ref
  105.6 9.0 %shard_map.152.x_ref = bf16[4,16,1664]{2,1,0:T(8,128)(2,1)} custom-call(bf16[16,1664]{1,0:T(8,128)(2,1)} %reduce_sum.120.x_ref), custom_call_target="tpu_custom_call" | custom-call | tf_op jit(solution)/shard_map/pallas_call | solution.py:100
  114.6 32.9 %shard_map.153 = bf16[8,4,16,1664]{3,2,1,0:T(8,128)(2,1)} custom-call(bf16[4,16,1664]{2,1,0:T(8,128)(2,1)} %shard_map.152.x_ref), custom_call_target="tpu_custom_call" | custom-call | tf_op jit(solution)/shard_map/pallas_call | solution.py:100
  147.5 1.6 copy.32
  149.2 1.0 convolution_convert_fusion.3.x_ref
  150.2 8.8 %shard_map.154 = bf16[8,16,1664]{2,1,0:T(8,128)(2,1)} custom-call(bf16[16,1664]{1,0:T(8,128)(2,1)} %convolution_convert_fusion.3.x_ref), custom_call_target="tpu_custom_call" | custom-call | tf_op jit(solution)/shard_map/pallas_call | solution.py:100
  159.0 0.2 fusion.35
  159.2 0.5 multiply_cosine_fusion
  159.7 2.6 fusion.1
  162.3 1.5 fusion.10
  163.9 0.2 subtract_convert_fusion
  164.1 0.8 copy-done.2
  164.9 0.8 pad_maximum_fusion
  165.8 1.7 slice.60
  167.5 0.7 pad_maximum_fusion.1
  168.2 100.4 %all-gather.5.cloned.1.call-done.k_ref.v_ref = bf16[13312,512]{1,0:T(8,128)(2,1)} async-done(((bf16[416,512]{1,0:T(8,128)(2,1)}), bf16[13312,512]{1,0:T(8,128)(2,1)}) %all-gather.5.cloned.1.call-update) | async-done | bytes 13631504 | tf_op jit(solution)/shard_map/all_gather | solution.py:390
  268.5 46.2 %shard_map.155 = f32[208,512]{1,0:T(8,128)} custom-call(s32[1]{0:T(128)} %bitcast.21.meta_ref, s32[32]{0:T(128)} %lengths_ref.1, bf16[208,512]{1,0:T(8,128)(2,1)} %bitcast.82, bf16[13312,512]{1,0:T(8,128)(2,1)} %all-gather.5.cloned.1.call-done.k_ref.v_ref, bf16[13312,512]{1,0:T(8,128)(2,1)} %all-gather.5.cloned.1.call-done.k_ref.v_ref), custom_call_target="tpu_custom_call" | custom-call | flops 13958643712 | bytes 14270464 | tf_op jit(solution)/shard_map/pallas_call | solution.py:225
  314.7 3.1 convolution_convert_fusion
  317.8 29.1 %shard_map.156 = bf16[8,64,1664]{2,1,0:T(8,128)(2,1)} custom-call(bf16[8,64,1664]{2,1,0:T(8,128)(2,1)} %bitcast.66), custom_call_target="tpu_custom_call" | custom-call | tf_op jit(solution)/shard_map/pallas_call | solution.py:100
  346.9 1.7 convert_reduce_fusion
  348.6 1.7 add_convert_fusion
  (46 shorter events, 1.3 us)
Async XLA Ops:
  7.2 87.4 %copy-start = (bf16[832,1664]{1,0:T(8,128)(2,1)S(1)}, bf16[832,1664]{1,0:T(8,128)(2,1)}, u32[]{:S(2)}) copy-start(bf16[832,1664]{1,0:T(8,128)(2,1)} %param.22) | copy-start | bytes 8306692
  7.2 152.5 %all-gather.3.cloned.1.call-start = ((), (), s32[]{:S(2)}) async-start(), calls=%async_computation | async-start | bytes 1916928 | tf_op jit(solution)/shard_map/all_gather | solution.py:356
  7.9 260.6 %all-gather.5.cloned.1.call-start = ((), (), s32[]{:S(2)}) async-start(), calls=%async_computation.1 | async-start | bytes 14057472 | tf_op jit(solution)/shard_map/all_gather | solution.py:390
  48.0 2.1 copy-start.7
  51.5 1.9 copy-start.6
  80.7 3.8 %copy-start.1 = (bf16[2,32,1664]{2,1,0:T(8,128)(2,1)S(1)}, bf16[2,32,1664]{2,1,0:T(8,128)(2,1)}, u32[]{:S(2)}) copy-start(bf16[2,32,1664]{2,1,0:T(8,128)(2,1)} %param.13) | copy-start | bytes 638980
  80.8 4.2 %copy-start.5 = (f32[1664]{0:T(1024)S(1)}, f32[1664]{0:T(1024)}, u32[]{:S(2)}) copy-start(f32[1664]{0:T(1024)} %param.21) | copy-start | bytes 19972
  159.7 2.6 copy-start.8
  159.7 2.6 copy-start.9
  162.3 1.5 copy-start.4
  163.8 1.1 copy-start.2
  164.9 149.8 %copy-start.3 = (bf16[512,2,104]{0,2,1:T(8,128)(2,1)}, bf16[512,2,104]{0,2,1:T(8,128)(2,1)S(1)}, u32[]{:S(2)}) copy-start(bf16[512,2,104]{0,2,1:T(8,128)(2,1)S(1)} %pad_maximum_fusion.2) | copy-start | bytes 638980
Sparse Core Ops, SparseCore 0:
  9.8 49.0 all-gather.2
  165.9 102.6 all-gather.4

commit v12 on v11

--- a/solution.py
+++ b/solution.py
@@ -402,10 +402,12 @@
     )
     own_rows = text_rows.shape[0]
 
-    def text_term(offset, row_count):
-        return jnp.dot(attended_rows, text_output, preferred_element_type=jnp.float32)
-
-    text_sum = summed_rows(text_term, own_rows, 4)
+    full_output = lax.all_gather(text_output, "tp", axis=0, tiled=True)
+    head_pieces = tp_exchange(
+        attended_rows.reshape(tp_ways, own_rows, local_width), tp_ways, False, 4
+    )
+    mixed_rows = jnp.transpose(head_pieces, (1, 0, 2)).reshape(own_rows, tp_ways * local_width)
+    text_sum = jnp.dot(mixed_rows, full_output, preferred_element_type=jnp.float32)
     residual = lax.dynamic_slice_in_dim(embedded, tp_index * own_rows, own_rows, 0)
     hidden = (residual.astype(jnp.float32) + text_sum).astype(jnp.bfloat16)
     return (hidden, key_flat, value_rows)

time: 358 us -> 355 us (level); the launches traced: 357 us -> 348 us
  Pallas kernels: 196 us -> 176 us
  waiting for transfers between devices: 101 us -> 110 us
    pallas_call x8, Pallas kernels: 149 us -> 130 us  [tp_exchange(): pl.pallas_call(functools.partial(exchange_kernel, axis, ways, stride, gat...]
    all_gather x0 -> x1, waiting for transfers between devices: none -> 8.68 us  [shards(): full_output = lax.all_gather(text_output, 'tp', axis=0, tiled=True)]
  transfers between devices with their start and end apart: 2 -> 3, of which waited for: 1 -> 2; matrix products, arithmetic and copies ran while one was open for 9% -> 11% of each run, Pallas kernels for 34% -> 51%
where the time goes in v12:
time: 355 us; the launch traced here: 348 us
  Pallas kernels  176 us (50%)
  waiting for transfers between devices  110 us (31%)
  matrix products  21 us (6%)
  local copies, waits for them, and re-layouts  14.7 us (4%)
  between operations  14.2 us (4%)
  other arithmetic  12.7 us (4%)
    pallas_call x8, Pallas kernels, tp_exchange(): pl.pallas_call(functools.partial(exchange_kernel, axis, ways, stride, gat...  130 us
    all_gather x1, waiting for transfers between devices, shards(): lax.all_gather(jnp.concatenate([jnp.transpose(key_flat), jnp.transpose(va...  99.7 us
    pallas_call x1, Pallas kernels, causal_attention(): pl.pallas_call(attention_kernel, grid_spec=grid_spec, out_shape=jax.Shape...  46 us
    all_gather x1, waiting for transfers between devices, shards(): full_output = lax.all_gather(text_output, 'tp', axis=0, tiled=True)  8.68 us
  transfers between devices with their start and end apart: 3, of which 2 were waited for; matrix products, arithmetic and copies ran while one was open for 11% of the time, Pallas kernels for 51%

profile of v12, /device:TPU:223, one launch (start us, length us, event | category | flops | bytes accessed | tf_op | source)
XLA Modules:
  0.0 348.2 jit_solution(17468222142465078892)
XLA Ops:
  7.2 0.7 all-gather.4.cloned.1.call-update
  8.0 1.1 convert_reduce_fusion.1
  9.1 1.1 fusion.27
  10.2 1.8 fusion.29.x_ref
  12.0 33.4 %shard_map.148 = bf16[8,2,32,1664]{3,2,1,0:T(8,128)(2,1)} custom-call(bf16[2,32,1664]{2,1,0:T(8,128)(2,1)} %fusion.29.x_ref), custom_call_target="tpu_custom_call" | custom-call | tf_op jit(solution)/shard_map/pallas_call | solution.py:100
  45.4 1.8 copy.29
  47.1 0.3 copy-done.8
  47.5 1.3 convolution_convert_fusion.3
  49.1 0.6 fusion.63
  49.6 1.3 fusion.18
  51.1 2.6 fusion.20
  53.7 1.1 copy.31
  54.8 0.2 dot_general.34
  55.1 3.0 convolution_convert_fusion.1.x_ref
  58.0 19.7 %shard_map.149 = bf16[8,64,1664]{2,1,0:T(8,128)(2,1)} custom-call(bf16[8,64,1664]{2,1,0:T(8,128)(2,1)} %convolution_convert_fusion.1.x_ref), custom_call_target="tpu_custom_call" | custom-call | tf_op jit(solution)/shard_map/pallas_call | solution.py:100
  77.8 2.6 convert_reduce_fusion
  80.3 1.3 reshape.255
  81.8 0.2 fusion.30
  82.1 0.2 reshape.256
  82.4 0.7 copy.33
  83.1 7.5 %shard_map.150 = bf16[8,2,8,832]{3,2,1,0:T(8,128)(2,1)} custom-call(bf16[8,2,8,832]{3,2,1,0:T(8,128)(2,1)} %bitcast.76), custom_call_target="tpu_custom_call" | custom-call | tf_op jit(solution)/shard_map/pallas_call | solution.py:100
  90.6 1.0 copy.34
  91.5 1.4 fusion.7.x_ref
  92.9 7.9 %shard_map.151 = bf16[8,16,1664]{2,1,0:T(8,128)(2,1)} custom-call(bf16[8,16,1664]{2,1,0:T(8,128)(2,1)} %fusion.7.x_ref), custom_call_target="tpu_custom_call" | custom-call | tf_op jit(solution)/shard_map/pallas_call | solution.py:100
  100.8 1.7 reduce_sum.111.x_ref
  102.5 8.7 %shard_map.152.x_ref = bf16[4,16,1664]{2,1,0:T(8,128)(2,1)} custom-call(bf16[16,1664]{1,0:T(8,128)(2,1)} %reduce_sum.111.x_ref), custom_call_target="tpu_custom_call" | custom-call | tf_op jit(solution)/shard_map/pallas_call | solution.py:100
  111.2 33.3 %shard_map.153 = bf16[8,4,16,1664]{3,2,1,0:T(8,128)(2,1)} custom-call(bf16[4,16,1664]{2,1,0:T(8,128)(2,1)} %shard_map.152.x_ref), custom_call_target="tpu_custom_call" | custom-call | tf_op jit(solution)/shard_map/pallas_call | solution.py:100
  144.5 2.8 copy.35
  147.7 2.4 convolution_convert_fusion.2.x_ref
  150.1 8.5 %shard_map.154 = bf16[8,16,1664]{2,1,0:T(8,128)(2,1)} custom-call(bf16[16,1664]{1,0:T(8,128)(2,1)} %convolution_convert_fusion.2.x_ref), custom_call_target="tpu_custom_call" | custom-call | tf_op jit(solution)/shard_map/pallas_call | solution.py:100
  159.1 0.5 multiply_cosine_fusion
  159.6 2.6 fusion.1
  162.2 1.5 fusion.11
  164.0 0.8 copy-done.2
  164.8 0.8 pad_maximum_fusion
  165.7 0.2 all-gather.8.cloned.1.call-start
  165.9 0.5 all-gather.8.cloned.1.call-update
  166.4 1.7 slice.60
  168.1 0.7 pad_maximum_fusion.1
  168.8 99.7 %all-gather.6.cloned.1.call-done.k_ref.v_ref = bf16[13312,512]{1,0:T(8,128)(2,1)} async-done(((bf16[416,512]{1,0:T(8,128)(2,1)}), bf16[13312,512]{1,0:T(8,128)(2,1)}) %all-gather.6.cloned.1.call-update) | async-done | bytes 13631504 | tf_op jit(solution)/shard_map/all_gather | solution.py:390
  268.5 46.0 %shard_map.155 = f32[208,512]{1,0:T(8,128)} custom-call(s32[1]{0:T(128)} %bitcast.21.meta_ref, s32[32]{0:T(128)} %lengths_ref.1, bf16[208,512]{1,0:T(8,128)(2,1)} %bitcast.87, bf16[13312,512]{1,0:T(8,128)(2,1)} %all-gather.6.cloned.1.call-done.k_ref.v_ref, bf16[13312,512]{1,0:T(8,128)(2,1)} %all-gather.6.cloned.1.call-done.k_ref.v_ref), custom_call_target="tpu_custom_call" | custom-call | flops 13958643712 | bytes 14270464 | tf_op jit(solution)/shard_map/pallas_call | solution.py:225
  314.5 1.0 convert_bitcast_fusion
  315.5 0.8 copy.36
  316.4 11.0 %shard_map.156 = bf16[8,64,208]{2,1,0:T(8,128)(2,1)} custom-call(bf16[8,64,208]{2,1,0:T(8,128)(2,1)} %bitcast.74), custom_call_target="tpu_custom_call" | custom-call | tf_op jit(solution)/shard_map/pallas_call | solution.py:100
  327.3 1.1 copy.37
  328.4 0.3 reshape.264
  328.7 8.7 %all-gather.8.cloned.1.call-done = bf16[1664,1664]{1,0:T(8,128)(2,1)} async-done(((bf16[208,1664]{1,0:T(8,128)(2,1)}), bf16[1664,1664]{1,0:T(8,128)(2,1)}) %all-gather.8.cloned.1.call-update) | async-done | bytes 5537808 | tf_op jit(solution)/shard_map/all_gather | solution.py:405
  337.4 4.3 %fusion.10 = bf16[64,1664]{1,0:T(8,128)(2,1)} fusion(bf16[64,1664]{1,0:T(8,128)(2,1)S(1)} %reshape.264, bf16[1664,1664]{1,0:T(8,128)(2,1)} %all-gather.8.cloned.1.call-done, bf16[512,1664]{1,0:T(8,128)(2,1)} %copy-done.4, s32[]{:T(128)S(6)} %select_n.72), kind=kOutput, calls=%fused_computation.14 | convolution fusion | flops 354738176 | bytes 6176772 | tf_op jit(solution)/shard_map/dot_general | solution.py:410
  (53 shorter events, 1.9 us)
Async XLA Ops:
  7.2 84.4 %copy-start = (bf16[832,1664]{1,0:T(8,128)(2,1)S(1)}, bf16[832,1664]{1,0:T(8,128)(2,1)}, u32[]{:S(2)}) copy-start(bf16[832,1664]{1,0:T(8,128)(2,1)} %param.22) | copy-start | bytes 8306692
  7.2 152.4 %all-gather.4.cloned.1.call-start = ((), (), s32[]{:S(2)}) async-start(), calls=%async_computation | async-start | bytes 1916928 | tf_op jit(solution)/shard_map/all_gather | solution.py:356
  7.9 260.6 %all-gather.6.cloned.1.call-start = ((), (), s32[]{:S(2)}) async-start(), calls=%async_computation.1 | async-start | bytes 14057472 | tf_op jit(solution)/shard_map/all_gather | solution.py:390
  45.4 2.1 copy-start.8
  47.5 1.4 copy-start.6
  77.8 3.8 %copy-start.1 = (bf16[2,32,1664]{2,1,0:T(8,128)(2,1)S(1)}, bf16[2,32,1664]{2,1,0:T(8,128)(2,1)}, u32[]{:S(2)}) copy-start(bf16[2,32,1664]{2,1,0:T(8,128)(2,1)} %param.13) | copy-start | bytes 638980
  77.8 4.2 %copy-start.5 = (f32[1664]{0:T(1024)S(1)}, f32[1664]{0:T(1024)}, u32[]{:S(2)}) copy-start(f32[1664]{0:T(1024)} %param.21) | copy-start | bytes 19972
  144.5 2.8 copy-start.7
  159.6 2.6 copy-start.9
  159.6 2.6 copy-start.10
  162.2 1.5 copy-start.4
  163.7 1.0 copy-start.2
  164.8 149.7 %copy-start.3 = (bf16[512,2,104]{0,2,1:T(8,128)(2,1)}, bf16[512,2,104]{0,2,1:T(8,128)(2,1)S(1)}, u32[]{:S(2)}) copy-start(bf16[512,2,104]{0,2,1:T(8,128)(2,1)S(1)} %pad_maximum_fusion.2) | copy-start | bytes 638980
  165.7 171.7 %all-gather.8.cloned.1.call-start = ((), (), s32[]{:S(2)}) async-start(), calls=%async_computation.2 | async-start | bytes 6230016 | tf_op jit(solution)/shard_map/all_gather | solution.py:405
Sparse Core Ops, SparseCore 0:
  9.8 47.3 all-gather.3
  165.8 102.6 all-gather.5
  270.3 67.0 all-gather.7

commit v13 on v12

--- a/solution.py
+++ b/solution.py
@@ -341,6 +341,8 @@
     )
     senders = rank_dest == seq_index
     segment = seq_gathered(visual_part, seq_ways, (6, 7)).reshape(-1, model_width)
+    full_output = lax.all_gather(text_output, "tp", axis=0, tiled=True)
+    full_output, segment = lax.optimization_barrier((full_output, segment))
     row_count = segment.shape[0]
     sources = jnp.arange(row_count, dtype=jnp.int32) // part_rows
     wanted = jnp.any(
@@ -402,7 +404,6 @@
     )
     own_rows = text_rows.shape[0]
 
-    full_output = lax.all_gather(text_output, "tp", axis=0, tiled=True)
     head_pieces = tp_exchange(
         attended_rows.reshape(tp_ways, own_rows, local_width), tp_ways, False, 4
     )

time: 355 us -> 368 us (1.037); the launches traced: 348 us -> 368 us
  Pallas kernels: 176 us -> 203 us
  waiting for transfers between devices: 110 us -> 101 us
    pallas_call x8, Pallas kernels: 130 us -> 157 us  [tp_exchange(): pl.pallas_call(functools.partial(exchange_kernel, axis, ways, stride, gat...]
    all_gather x1, waiting for transfers between devices: 8.68 us -> 0.02 us  [shards(): full_output = lax.all_gather(text_output, 'tp', axis=0, tiled=True)]
  transfers between devices with their start and end apart: 3 -> 3, of which waited for: 2 -> 1; matrix products, arithmetic and copies ran while one was open for 11% -> 10% of each run, Pallas kernels for 51% -> 40%
where the time goes in v13:
time: 368 us
  Pallas kernels  203 us (55%)
  waiting for transfers between devices  101 us (27%)
  matrix products  21 us (6%)
  local copies, waits for them, and re-layouts  16 us (4%)
  between operations  14.1 us (4%)
  other arithmetic  12.6 us (3%)
    pallas_call x8, Pallas kernels, tp_exchange(): pl.pallas_call(functools.partial(exchange_kernel, axis, ways, stride, gat...  157 us
    all_gather x1, waiting for transfers between devices, shards(): lax.all_gather(jnp.concatenate([jnp.transpose(key_flat), jnp.transpose(va...  99.5 us
    pallas_call x1, Pallas kernels, causal_attention(): pl.pallas_call(attention_kernel, grid_spec=grid_spec, out_shape=jax.Shape...  46.2 us
  transfers between devices with their start and end apart: 3, of which 1 were waited for; matrix products, arithmetic and copies ran while one was open for 10% of the time, Pallas kernels for 40%

profile of v13, /device:TPU:223, one launch (start us, length us, event | category | flops | bytes accessed | tf_op | source)
XLA Modules:
  0.0 367.6 jit_solution(10793624360309154683)
XLA Ops:
  7.2 0.7 all-gather.4.cloned.1.call-update
  8.0 0.7 all-gather.6.cloned.1.call-update
  8.7 0.8 reshape.248
  9.5 0.7 dynamic_slice.6
  10.3 1.0 convert_reduce_fusion.1
  11.3 1.1 fusion.27
  12.5 1.8 fusion.29.x_ref
  14.3 39.7 %shard_map.148 = bf16[8,2,32,1664]{3,2,1,0:T(8,128)(2,1)} custom-call(bf16[2,32,1664]{2,1,0:T(8,128)(2,1)} %fusion.29.x_ref), custom_call_target="tpu_custom_call" | custom-call | tf_op jit(solution)/shard_map/pallas_call | solution.py:100
  54.0 1.7 copy.29
  55.8 0.3 copy-done.7
  56.1 1.3 convolution_convert_fusion.3
  57.5 0.6 fusion.63
  58.1 1.3 fusion.18
  60.0 2.6 fusion.20
  62.6 1.1 copy.31
  63.7 0.2 dot_general.34
  64.0 3.0 convolution_convert_fusion.1.x_ref
  66.9 43.2 %shard_map.149 = bf16[8,64,1664]{2,1,0:T(8,128)(2,1)} custom-call(bf16[8,64,1664]{2,1,0:T(8,128)(2,1)} %convolution_convert_fusion.1.x_ref), custom_call_target="tpu_custom_call" | custom-call | tf_op jit(solution)/shard_map/pallas_call | solution.py:100
  110.2 2.6 convert_reduce_fusion
  112.7 1.3 reshape.255
  114.1 0.2 fusion.30
  114.5 0.2 reshape.256
  114.8 0.7 copy.33
  115.5 6.5 %shard_map.150 = bf16[8,2,8,832]{3,2,1,0:T(8,128)(2,1)} custom-call(bf16[8,2,8,832]{3,2,1,0:T(8,128)(2,1)} %bitcast.76), custom_call_target="tpu_custom_call" | custom-call | tf_op jit(solution)/shard_map/pallas_call | solution.py:100
  122.0 1.0 copy.34
  123.0 1.4 fusion.7.x_ref
  124.4 9.6 %shard_map.151 = bf16[8,16,1664]{2,1,0:T(8,128)(2,1)} custom-call(bf16[8,16,1664]{2,1,0:T(8,128)(2,1)} %fusion.7.x_ref), custom_call_target="tpu_custom_call" | custom-call | tf_op jit(solution)/shard_map/pallas_call | solution.py:100
  134.0 1.7 reduce_sum.111.x_ref
  135.7 9.7 %shard_map.152.x_ref = bf16[4,16,1664]{2,1,0:T(8,128)(2,1)} custom-call(bf16[16,1664]{1,0:T(8,128)(2,1)} %reduce_sum.111.x_ref), custom_call_target="tpu_custom_call" | custom-call | tf_op jit(solution)/shard_map/pallas_call | solution.py:100
  145.4 31.3 %shard_map.153 = bf16[8,4,16,1664]{3,2,1,0:T(8,128)(2,1)} custom-call(bf16[4,16,1664]{2,1,0:T(8,128)(2,1)} %shard_map.152.x_ref), custom_call_target="tpu_custom_call" | custom-call | tf_op jit(solution)/shard_map/pallas_call | solution.py:100
  176.8 2.8 copy.35
  179.8 0.5 multiply_cosine_fusion
  180.4 2.4 convolution_convert_fusion.2.x_ref
  182.8 8.6 %shard_map.154 = bf16[8,16,1664]{2,1,0:T(8,128)(2,1)} custom-call(bf16[16,1664]{1,0:T(8,128)(2,1)} %convolution_convert_fusion.2.x_ref), custom_call_target="tpu_custom_call" | custom-call | tf_op jit(solution)/shard_map/pallas_call | solution.py:100
  191.4 2.6 fusion.1
  194.1 1.5 fusion.11
  195.8 0.8 copy-done.2
  196.6 0.8 pad_maximum_fusion
  197.5 1.7 slice.60
  199.2 0.7 pad_maximum_fusion.1
  199.9 99.5 %all-gather.8.cloned.1.call-done.k_ref.v_ref = bf16[13312,512]{1,0:T(8,128)(2,1)} async-done(((bf16[416,512]{1,0:T(8,128)(2,1)}), bf16[13312,512]{1,0:T(8,128)(2,1)}) %all-gather.8.cloned.1.call-update) | async-done | bytes 13631504 | tf_op jit(solution)/shard_map/all_gather | solution.py:392
  299.5 46.2 %shard_map.155 = f32[208,512]{1,0:T(8,128)} custom-call(s32[1]{0:T(128)} %bitcast.21.meta_ref, s32[32]{0:T(128)} %lengths_ref.1, bf16[208,512]{1,0:T(8,128)(2,1)} %bitcast.87, bf16[13312,512]{1,0:T(8,128)(2,1)} %all-gather.8.cloned.1.call-done.k_ref.v_ref, bf16[13312,512]{1,0:T(8,128)(2,1)} %all-gather.8.cloned.1.call-done.k_ref.v_ref), custom_call_target="tpu_custom_call" | custom-call | flops 13958643712 | bytes 14270464 | tf_op jit(solution)/shard_map/pallas_call | solution.py:225
  345.6 1.0 convert_bitcast_fusion
  346.7 0.8 copy.36
  347.5 7.8 %shard_map.156 = bf16[8,64,208]{2,1,0:T(8,128)(2,1)} custom-call(bf16[8,64,208]{2,1,0:T(8,128)(2,1)} %bitcast.74), custom_call_target="tpu_custom_call" | custom-call | tf_op jit(solution)/shard_map/pallas_call | solution.py:100
  355.3 1.1 copy.37
  356.4 0.3 reshape.264
  356.7 4.3 %fusion.10 = bf16[64,1664]{1,0:T(8,128)(2,1)} fusion(bf16[64,1664]{1,0:T(8,128)(2,1)S(1)} %reshape.264, bf16[1664,1664]{1,0:T(8,128)(2,1)} %all-gather.4.cloned.1.call-done, bf16[512,1664]{1,0:T(8,128)(2,1)} %copy-done.4, s32[]{:T(128)S(6)} %select_n.72), kind=kOutput, calls=%fused_computation.14 | convolution fusion | flops 354738176 | bytes 6176772 | tf_op jit(solution)/shard_map/dot_general | solution.py:411
  (51 shorter events, 1.8 us)
Async XLA Ops:
  7.2 115.8 %copy-start = (bf16[832,1664]{1,0:T(8,128)(2,1)S(1)}, bf16[832,1664]{1,0:T(8,128)(2,1)}, u32[]{:S(2)}) copy-start(bf16[832,1664]{1,0:T(8,128)(2,1)} %param.22) | copy-start | bytes 8306692
  7.2 173.2 %all-gather.4.cloned.1.call-start = ((), (), s32[]{:S(2)}) async-start(), calls=%async_computation | async-start | bytes 6230016 | tf_op jit(solution)/shard_map/all_gather | solution.py:344
  7.9 183.5 %all-gather.6.cloned.1.call-start = ((), (), s32[]{:S(2)}) async-start(), calls=%async_computation.1 | async-start | bytes 1916928 | tf_op jit(solution)/shard_map/all_gather | solution.py:358
  8.7 290.8 %all-gather.8.cloned.1.call-start = ((), (), s32[]{:S(2)}) async-start(), calls=%async_computation.2 | async-start | bytes 14057472 | tf_op jit(solution)/shard_map/all_gather | solution.py:392
  54.0 2.1 copy-start.7
  57.5 1.9 copy-start.6
  110.2 3.8 %copy-start.1 = (bf16[2,32,1664]{2,1,0:T(8,128)(2,1)S(1)}, bf16[2,32,1664]{2,1,0:T(8,128)(2,1)}, u32[]{:S(2)}) copy-start(bf16[2,32,1664]{2,1,0:T(8,128)(2,1)} %param.13) | copy-start | bytes 638980
  110.2 4.2 %copy-start.5 = (f32[1664]{0:T(1024)S(1)}, f32[1664]{0:T(1024)}, u32[]{:S(2)}) copy-start(f32[1664]{0:T(1024)} %param.21) | copy-start | bytes 19972
  191.4 2.6 copy-start.8
  191.4 2.6 copy-start.9
  194.0 1.5 copy-start.4
  195.5 1.0 copy-start.2
  196.6 149.0 %copy-start.3 = (bf16[512,2,104]{0,2,1:T(8,128)(2,1)}, bf16[512,2,104]{0,2,1:T(8,128)(2,1)S(1)}, u32[]{:S(2)}) copy-start(bf16[512,2,104]{0,2,1:T(8,128)(2,1)S(1)} %pad_maximum_fusion.2) | copy-start | bytes 638980
Sparse Core Ops, SparseCore 0:
  9.8 104.0 all-gather.3
  115.7 42.4 all-gather.5
  197.6 101.8 all-gather.7

commit v14 on v12

--- a/solution.py
+++ b/solution.py
@@ -340,6 +340,8 @@
         1,
     )
     senders = rank_dest == seq_index
+    late_output, visual_part = lax.optimization_barrier((text_output, visual_part))
+    full_output = lax.all_gather(late_output, "tp", axis=0, tiled=True)
     segment = seq_gathered(visual_part, seq_ways, (6, 7)).reshape(-1, model_width)
     row_count = segment.shape[0]
     sources = jnp.arange(row_count, dtype=jnp.int32) // part_rows
@@ -371,6 +373,7 @@
         placement.astype(jnp.bfloat16), visual_block, preferred_element_type=jnp.float32
     ).astype(jnp.bfloat16)
     embedded = jnp.where(covered[:, None], placed, text_block)
+    full_output, embedded = lax.optimization_barrier((full_output, embedded))
     text_normed = rms_normed(embedded, text_gain).astype(jnp.bfloat16)
     text_heads = jnp.dot(
         text_normed,
@@ -402,7 +405,6 @@
     )
     own_rows = text_rows.shape[0]
 
-    full_output = lax.all_gather(text_output, "tp", axis=0, tiled=True)
     head_pieces = tp_exchange(
         attended_rows.reshape(tp_ways, own_rows, local_width), tp_ways, False, 4
     )

time: 355 us -> 361 us (1.017); the launches traced: 348 us -> 360 us
  Pallas kernels: 176 us -> 184 us
    pallas_call x8, Pallas kernels: 130 us -> 138 us  [tp_exchange(): pl.pallas_call(functools.partial(exchange_kernel, axis, ways, stride, gat...]
  transfers between devices with their start and end apart: 3 -> 3, of which waited for: 2 -> 2; matrix products, arithmetic and copies ran while one was open for 11% -> 10% of each run, Pallas kernels for 51% -> 36%
where the time goes in v14:
time: 361 us; the launch traced here: 360 us
  Pallas kernels  184 us (51%)
  waiting for transfers between devices  112 us (31%)
  matrix products  22 us (6%)
  other arithmetic  14.7 us (4%)
  between operations  14.2 us (4%)
  local copies, waits for them, and re-layouts  13.5 us (4%)
    pallas_call x8, Pallas kernels, tp_exchange(): pl.pallas_call(functools.partial(exchange_kernel, axis, ways, stride, gat...  138 us
    all_gather x1, waiting for transfers between devices, shards(): lax.all_gather(jnp.concatenate([jnp.transpose(key_flat), jnp.transpose(va...  102 us
    pallas_call x1, Pallas kernels, causal_attention(): pl.pallas_call(attention_kernel, grid_spec=grid_spec, out_shape=jax.Shape...  46 us
    all_gather x1, waiting for transfers between devices, shards(): full_output = lax.all_gather(late_output, 'tp', axis=0, tiled=True)  9.14 us
  transfers between devices with their start and end apart: 3, of which 2 were waited for; matrix products, arithmetic and copies ran while one was open for 10% of the time, Pallas kernels for 36%

profile of v14, /device:TPU:223, one launch (start us, length us, event | category | flops | bytes accessed | tf_op | source)
XLA Modules:
  0.0 359.9 jit_solution(8397903619741091048)
XLA Ops:
  7.2 0.7 all-gather.6.cloned.1.call-update
  8.0 1.1 convert_reduce_fusion.1
  9.1 1.1 fusion.27
  10.2 1.8 fusion.29.x_ref
  12.0 33.4 %shard_map.148 = bf16[8,2,32,1664]{3,2,1,0:T(8,128)(2,1)} custom-call(bf16[2,32,1664]{2,1,0:T(8,128)(2,1)} %fusion.29.x_ref), custom_call_target="tpu_custom_call" | custom-call | tf_op jit(solution)/shard_map/pallas_call | solution.py:100
  45.4 1.8 copy.29
  47.1 0.3 copy-done.8
  47.5 1.3 convolution_convert_fusion.3
  49.1 0.6 fusion.63
  49.6 1.3 fusion.18
  51.0 2.6 fusion.20
  53.6 1.1 copy.31
  54.7 0.2 dot_general.34
  55.0 3.0 convolution_convert_fusion.1.x_ref
  57.9 19.7 %shard_map.149 = bf16[8,64,1664]{2,1,0:T(8,128)(2,1)} custom-call(bf16[8,64,1664]{2,1,0:T(8,128)(2,1)} %convolution_convert_fusion.1.x_ref), custom_call_target="tpu_custom_call" | custom-call | tf_op jit(solution)/shard_map/pallas_call | solution.py:100
  77.7 2.6 convert_reduce_fusion
  80.3 1.3 reshape.253
  81.7 0.2 fusion.30
  82.0 0.2 reshape.254
  82.3 0.7 copy.33
  83.0 7.5 %shard_map.150 = bf16[8,2,8,832]{3,2,1,0:T(8,128)(2,1)} custom-call(bf16[8,2,8,832]{3,2,1,0:T(8,128)(2,1)} %bitcast.77), custom_call_target="tpu_custom_call" | custom-call | tf_op jit(solution)/shard_map/pallas_call | solution.py:100
  90.5 1.0 copy.34
  91.4 1.4 fusion.7.x_ref
  92.8 7.9 %shard_map.151 = bf16[8,16,1664]{2,1,0:T(8,128)(2,1)} custom-call(bf16[8,16,1664]{2,1,0:T(8,128)(2,1)} %fusion.7.x_ref), custom_call_target="tpu_custom_call" | custom-call | tf_op jit(solution)/shard_map/pallas_call | solution.py:100
  100.7 1.7 reduce_sum.108.x_ref
  102.4 0.2 all-gather.8.cloned.1.call-start
  103.4 8.7 %shard_map.152.x_ref = bf16[4,16,1664]{2,1,0:T(8,128)(2,1)} custom-call(bf16[16,1664]{1,0:T(8,128)(2,1)} %reduce_sum.108.x_ref), custom_call_target="tpu_custom_call" | custom-call | tf_op jit(solution)/shard_map/pallas_call | solution.py:100
  112.1 38.5 %shard_map.153 = bf16[8,4,16,1664]{3,2,1,0:T(8,128)(2,1)} custom-call(bf16[4,16,1664]{2,1,0:T(8,128)(2,1)} %shard_map.152.x_ref), custom_call_target="tpu_custom_call" | custom-call | tf_op jit(solution)/shard_map/pallas_call | solution.py:100
  150.5 1.6 copy.35
  152.3 1.0 convolution_convert_fusion.2.x_ref
  153.2 14.2 %shard_map.154 = bf16[8,16,1664]{2,1,0:T(8,128)(2,1)} custom-call(bf16[16,1664]{1,0:T(8,128)(2,1)} %convolution_convert_fusion.2.x_ref), custom_call_target="tpu_custom_call" | custom-call | tf_op jit(solution)/shard_map/pallas_call | solution.py:100
  167.7 0.5 multiply_cosine_fusion
  168.2 3.4 fusion.4
  171.6 9.1 %all-gather.4.cloned.1.call-done = bf16[1664,1664]{1,0:T(8,128)(2,1)} async-done(((bf16[208,1664]{1,0:T(8,128)(2,1)}), bf16[1664,1664]{1,0:T(8,128)(2,1)}) %all-gather.4.cloned.1.call-update) | async-done | bytes 5537808 | tf_op jit(solution)/shard_map/all_gather | solution.py:344
  180.8 2.0 fusion.1
  182.8 3.1 fusion.11
  186.1 0.8 copy-done.3
  186.9 0.8 pad_maximum_fusion
  187.8 1.7 slice.60
  189.5 0.7 pad_maximum_fusion.1
  190.2 101.7 %all-gather.8.cloned.1.call-done.k_ref.v_ref = bf16[13312,512]{1,0:T(8,128)(2,1)} async-done(((bf16[416,512]{1,0:T(8,128)(2,1)}), bf16[13312,512]{1,0:T(8,128)(2,1)}) %all-gather.8.cloned.1.call-update) | async-done | bytes 13631504 | tf_op jit(solution)/shard_map/all_gather | solution.py:393
  291.9 46.0 %shard_map.155 = f32[208,512]{1,0:T(8,128)} custom-call(s32[1]{0:T(128)} %bitcast.21.meta_ref, s32[32]{0:T(128)} %lengths_ref.1, bf16[208,512]{1,0:T(8,128)(2,1)} %bitcast.87, bf16[13312,512]{1,0:T(8,128)(2,1)} %all-gather.8.cloned.1.call-done.k_ref.v_ref, bf16[13312,512]{1,0:T(8,128)(2,1)} %all-gather.8.cloned.1.call-done.k_ref.v_ref), custom_call_target="tpu_custom_call" | custom-call | flops 13958643712 | bytes 14270464 | tf_op jit(solution)/shard_map/pallas_call | solution.py:225
  337.9 1.0 convert_bitcast_fusion
  339.0 0.8 copy.36
  339.8 7.8 %shard_map.156 = bf16[8,64,208]{2,1,0:T(8,128)(2,1)} custom-call(bf16[8,64,208]{2,1,0:T(8,128)(2,1)} %bitcast.75), custom_call_target="tpu_custom_call" | custom-call | tf_op jit(solution)/shard_map/pallas_call | solution.py:100
  347.6 1.1 copy.37
  348.7 0.3 reshape.264
  349.0 4.3 %fusion.10 = bf16[64,1664]{1,0:T(8,128)(2,1)} fusion(bf16[64,1664]{1,0:T(8,128)(2,1)S(1)} %reshape.264, bf16[1664,1664]{1,0:T(8,128)(2,1)} %all-gather.4.cloned.1.call-done, bf16[512,1664]{1,0:T(8,128)(2,1)} %fusion.4, s32[]{:T(128)S(6)} %select_n.72), kind=kOutput, calls=%fused_computation.14 | convolution fusion | flops 354738176 | bytes 6176772 | tf_op jit(solution)/shard_map/dot_general | solution.py:412
  (52 shorter events, 1.9 us)
Async XLA Ops:
  7.2 84.3 %copy-start = (bf16[832,1664]{1,0:T(8,128)(2,1)S(1)}, bf16[832,1664]{1,0:T(8,128)(2,1)}, u32[]{:S(2)}) copy-start(bf16[832,1664]{1,0:T(8,128)(2,1)} %param.22) | copy-start | bytes 8306692
  7.2 161.0 %all-gather.6.cloned.1.call-start = ((), (), s32[]{:S(2)}) async-start(), calls=%async_computation.1 | async-start | bytes 1916928 | tf_op jit(solution)/shard_map/all_gather | solution.py:358
  7.9 172.9 %all-gather.4.cloned.1.call-start = ((), (), s32[]{:S(2)}) async-start(), calls=%async_computation | async-start | bytes 6230016 | tf_op jit(solution)/shard_map/all_gather | solution.py:344
  45.4 2.1 copy-start.8
  47.5 1.4 copy-start.6
  77.7 3.8 %copy-start.2 = (bf16[2,32,1664]{2,1,0:T(8,128)(2,1)S(1)}, bf16[2,32,1664]{2,1,0:T(8,128)(2,1)}, u32[]{:S(2)}) copy-start(bf16[2,32,1664]{2,1,0:T(8,128)(2,1)} %param.13) | copy-start | bytes 638980
  77.7 4.2 %copy-start.5 = (f32[1664]{0:T(1024)S(1)}, f32[1664]{0:T(1024)}, u32[]{:S(2)}) copy-start(f32[1664]{0:T(1024)} %param.21) | copy-start | bytes 19972
  92.8 10.0 %copy-start.7 = (s32[64]{0:T(128)S(1)}, s32[64]{0:T(128)}, u32[]{:S(2)}) copy-start(s32[64]{0:T(128)} %param.16) | copy-start | bytes 772
  102.4 189.5 %all-gather.8.cloned.1.call-start = ((), (), s32[]{:S(2)}) async-start(), calls=%async_computation.2 | async-start | bytes 14057472 | tf_op jit(solution)/shard_map/all_gather | solution.py:393
  168.2 14.6 %copy-start.9 = (f32[1664]{0:T(1024)S(1)}, f32[1664]{0:T(1024)}, u32[]{:S(2)}) copy-start(f32[1664]{0:T(1024)} %param.23) | copy-start | bytes 19972
  180.8 2.0 copy-start.1
  185.8 1.0 copy-start.3
  186.9 151.0 %copy-start.4 = (bf16[512,2,104]{0,2,1:T(8,128)(2,1)}, bf16[512,2,104]{0,2,1:T(8,128)(2,1)S(1)}, u32[]{:S(2)}) copy-start(bf16[512,2,104]{0,2,1:T(8,128)(2,1)S(1)} %pad_maximum_fusion.2) | copy-start | bytes 638980
Sparse Core Ops, SparseCore 0:
  9.8 47.3 all-gather.5
  102.6 78.1 all-gather.3
  187.9 103.9 all-gather.7

commit v15 on v12

--- a/solution.py
+++ b/solution.py
@@ -387,8 +387,11 @@
     ).astype(jnp.bfloat16)
     value_rows = text_heads[:, 2 * local_width :].astype(jnp.bfloat16)
     key_flat = key_rows.reshape(rows_per_block, local_width)
+    kv_operand = jnp.concatenate([jnp.transpose(key_flat), jnp.transpose(value_rows)], 0)
+    kv_operand, late_output = lax.optimization_barrier((kv_operand, text_output))
+    full_output = tp_exchange(late_output, tp_ways, True, 8).reshape(-1, model_width)
     key_value_all = lax.all_gather(
-        jnp.concatenate([jnp.transpose(key_flat), jnp.transpose(value_rows)], 0),
+        kv_operand,
         "seq",
         axis=0,
         tiled=True,
@@ -402,7 +405,6 @@
     )
     own_rows = text_rows.shape[0]
 
-    full_output = lax.all_gather(text_output, "tp", axis=0, tiled=True)
     head_pieces = tp_exchange(
         attended_rows.reshape(tp_ways, own_rows, local_width), tp_ways, False, 4
     )

time: 355 us -> 378 us (1.065); the launches traced: 348 us -> 377 us
  Pallas kernels: 176 us -> 316 us
  waiting for transfers between devices: 110 us -> 0.72 us
    pallas_call x8 -> x9, Pallas kernels: 130 us -> 270 us  [tp_exchange(): pl.pallas_call(functools.partial(exchange_kernel, axis, ways, stride, gat...]
    all_gather x2 -> x1, waiting for transfers between devices: 108 us -> 0.01 us  [shards(): key_value_all = lax.all_gather(kv_operand, 'seq', axis=0, tiled=True)]
  transfers between devices with their start and end apart: 3 -> 2, of which waited for: 2 -> 0; matrix products, arithmetic and copies ran while one was open for 11% -> 9% of each run, Pallas kernels for 51% -> 69%
where the time goes in v15:
time: 378 us; the launch traced here: 377 us
  Pallas kernels  316 us (84%)
  matrix products  19.6 us (5%)
  between operations  14.4 us (4%)
  local copies, waits for them, and re-layouts  13.5 us (4%)
  other arithmetic  12.6 us (3%)
    pallas_call x9, Pallas kernels, tp_exchange(): pl.pallas_call(functools.partial(exchange_kernel, axis, ways, stride, gat...  270 us
    pallas_call x1, Pallas kernels, causal_attention(): pl.pallas_call(attention_kernel, grid_spec=grid_spec, out_shape=jax.Shape...  46.2 us
  transfers between devices with their start and end apart: 2, of which 0 were waited for; matrix products, arithmetic and copies ran while one was open for 9% of the time, Pallas kernels for 69%

profile of v15, /device:TPU:223, one launch (start us, length us, event | category | flops | bytes accessed | tf_op | source)
XLA Modules:
  0.0 377.0 jit_solution(12889422097505882114)
XLA Ops:
  7.2 0.7 all-gather.3.cloned.1.call-update
  8.0 0.8 reshape.247
  8.8 0.7 dynamic_slice.6
  9.6 1.0 convert_reduce_fusion.1
  10.6 1.1 fusion.28
  11.8 1.8 fusion.30.x_ref
  13.5 34.5 %shard_map.148 = bf16[8,2,32,1664]{3,2,1,0:T(8,128)(2,1)} custom-call(bf16[2,32,1664]{2,1,0:T(8,128)(2,1)} %fusion.30.x_ref), custom_call_target="tpu_custom_call" | custom-call | tf_op jit(solution)/shard_map/pallas_call | solution.py:100
  48.0 1.8 copy.28
  49.8 0.3 copy-done.7
  50.1 1.3 convolution_convert_fusion.3
  51.6 0.6 fusion.65
  52.1 1.3 fusion.19
  54.0 2.6 fusion.21
  56.6 1.1 copy.30
  57.8 0.2 dot_general.34
  58.0 3.0 convolution_convert_fusion.1.x_ref
  61.0 19.8 %shard_map.149 = bf16[8,64,1664]{2,1,0:T(8,128)(2,1)} custom-call(bf16[8,64,1664]{2,1,0:T(8,128)(2,1)} %convolution_convert_fusion.1.x_ref), custom_call_target="tpu_custom_call" | custom-call | tf_op jit(solution)/shard_map/pallas_call | solution.py:100
  80.8 2.6 convert_reduce_fusion
  83.3 1.3 reshape.254
  84.7 0.2 fusion.31
  85.0 0.1 fusion.33
  85.1 0.2 reshape.255
  85.3 0.7 copy.32
  86.1 7.6 %shard_map.150 = bf16[8,2,8,832]{3,2,1,0:T(8,128)(2,1)} custom-call(bf16[8,2,8,832]{3,2,1,0:T(8,128)(2,1)} %bitcast.82), custom_call_target="tpu_custom_call" | custom-call | tf_op jit(solution)/shard_map/pallas_call | solution.py:100
  93.6 1.0 copy.33
  94.6 1.4 fusion.7.x_ref
  96.0 7.9 %shard_map.151 = bf16[8,16,1664]{2,1,0:T(8,128)(2,1)} custom-call(bf16[8,16,1664]{2,1,0:T(8,128)(2,1)} %fusion.7.x_ref), custom_call_target="tpu_custom_call" | custom-call | tf_op jit(solution)/shard_map/pallas_call | solution.py:100
  103.9 1.7 reduce_sum.111.x_ref
  105.6 9.0 %shard_map.152.x_ref = bf16[4,16,1664]{2,1,0:T(8,128)(2,1)} custom-call(bf16[16,1664]{1,0:T(8,128)(2,1)} %reduce_sum.111.x_ref), custom_call_target="tpu_custom_call" | custom-call | tf_op jit(solution)/shard_map/pallas_call | solution.py:100
  114.6 32.9 %shard_map.153 = bf16[8,4,16,1664]{3,2,1,0:T(8,128)(2,1)} custom-call(bf16[4,16,1664]{2,1,0:T(8,128)(2,1)} %shard_map.152.x_ref), custom_call_target="tpu_custom_call" | custom-call | tf_op jit(solution)/shard_map/pallas_call | solution.py:100
  147.5 1.6 copy.34
  149.2 1.0 convolution_convert_fusion.2.x_ref
  150.2 8.8 %shard_map.154 = bf16[8,16,1664]{2,1,0:T(8,128)(2,1)} custom-call(bf16[16,1664]{1,0:T(8,128)(2,1)} %convolution_convert_fusion.2.x_ref), custom_call_target="tpu_custom_call" | custom-call | tf_op jit(solution)/shard_map/pallas_call | solution.py:100
  159.0 0.2 fusion.38
  159.2 0.5 multiply_cosine_fusion
  159.7 2.6 fusion.1
  162.3 1.5 fusion.12
  163.9 0.2 subtract_convert_fusion.1
  164.1 0.8 copy-done.2
  164.9 0.8 pad_maximum_fusion
  165.7 1.7 slice.60
  167.4 140.7 %shard_map.157 = bf16[8,208,1664]{2,1,0:T(8,128)(2,1)} custom-call(bf16[208,1664]{1,0:T(8,128)(2,1)} %x_ref), custom_call_target="tpu_custom_call" | custom-call | tf_op jit(solution)/shard_map/pallas_call | solution.py:100
  308.1 0.7 pad_maximum_fusion.1
  308.9 46.2 %shard_map.155 = f32[208,512]{1,0:T(8,128)} custom-call(s32[1]{0:T(128)} %bitcast.21.meta_ref, s32[32]{0:T(128)} %lengths_ref.1, bf16[208,512]{1,0:T(8,128)(2,1)} %bitcast.93, bf16[13312,512]{1,0:T(8,128)(2,1)} %all-gather.5.cloned.1.call-done.k_ref.v_ref, bf16[13312,512]{1,0:T(8,128)(2,1)} %all-gather.5.cloned.1.call-done.k_ref.v_ref), custom_call_target="tpu_custom_call" | custom-call | flops 13958643712 | bytes 14270464 | tf_op jit(solution)/shard_map/pallas_call | solution.py:225
  355.0 1.0 convert_bitcast_fusion
  356.1 0.8 copy.35
  356.9 8.8 %shard_map.156 = bf16[8,64,208]{2,1,0:T(8,128)(2,1)} custom-call(bf16[8,64,208]{2,1,0:T(8,128)(2,1)} %bitcast.81), custom_call_target="tpu_custom_call" | custom-call | tf_op jit(solution)/shard_map/pallas_call | solution.py:100
  365.7 4.5 %fusion.11 = bf16[64,1664]{1,0:T(8,128)(2,1)} fusion(bf16[8,208,1664]{2,1,0:T(8,128)(2,1)} %shard_map.157, bf16[8,64,208]{2,1,0:T(8,128)(2,1)} %shard_map.156, bf16[512,1664]{1,0:T(8,128)(2,1)} %copy-done.4, s32[]{:T(128)S(6)} %select_n.72), kind=kOutput, calls=%fused_computation.15 | convolution fusion | flops 354738176 | bytes 6176772 | tf_op jit(solution)/shard_map/dot_general | solution.py:412
  (47 shorter events, 1.3 us)
Async XLA Ops:
  7.2 87.4 %copy-start = (bf16[832,1664]{1,0:T(8,128)(2,1)S(1)}, bf16[832,1664]{1,0:T(8,128)(2,1)}, u32[]{:S(2)}) copy-start(bf16[832,1664]{1,0:T(8,128)(2,1)} %param.22) | copy-start | bytes 8306692
  7.2 152.5 %all-gather.3.cloned.1.call-start = ((), (), s32[]{:S(2)}) async-start(), calls=%async_computation | async-start | bytes 1916928 | tf_op jit(solution)/shard_map/all_gather | solution.py:356
  7.9 300.9 %all-gather.5.cloned.1.call-start = ((), (), s32[]{:S(2)}) async-start(), calls=%async_computation.1 | async-start | bytes 14057472 | tf_op jit(solution)/shard_map/all_gather | solution.py:393
  48.0 2.1 copy-start.7
  51.5 1.9 copy-start.6
  80.7 3.8 %copy-start.1 = (bf16[2,32,1664]{2,1,0:T(8,128)(2,1)S(1)}, bf16[2,32,1664]{2,1,0:T(8,128)(2,1)}, u32[]{:S(2)}) copy-start(bf16[2,32,1664]{2,1,0:T(8,128)(2,1)} %param.13) | copy-start | bytes 638980
  80.8 4.2 %copy-start.5 = (f32[1664]{0:T(1024)S(1)}, f32[1664]{0:T(1024)}, u32[]{:S(2)}) copy-start(f32[1664]{0:T(1024)} %param.21) | copy-start | bytes 19972
  159.7 2.6 copy-start.8
  159.7 2.6 copy-start.9
  162.3 1.5 copy-start.4
  163.8 1.1 copy-start.2
  164.9 143.3 %copy-start.3 = (bf16[512,2,104]{0,2,1:T(8,128)(2,1)}, bf16[512,2,104]{0,2,1:T(8,128)(2,1)S(1)}, u32[]{:S(2)}) copy-start(bf16[512,2,104]{0,2,1:T(8,128)(2,1)S(1)} %pad_maximum_fusion.2) | copy-start | bytes 638980
Sparse Core Ops, SparseCore 0:
  9.8 49.0 all-gather.2
  165.8 135.2 all-gather.4

commit v16 on v12

--- a/solution.py
+++ b/solution.py
@@ -261,9 +261,11 @@
     head_count = local_width // HEAD
     patch_normed = layer_normed(pixels, vision_gain).astype(jnp.bfloat16)
     packed_project = vision_project.reshape(model_width, 3 * local_width)
+    patch_rows = gathered_patches(patch_normed, 0)
+    later_text, patch_rows = lax.optimization_barrier((text_rows, patch_rows))
     projected = jnp.einsum(
         "npd,de->npe",
-        gathered_patches(patch_normed, 0),
+        patch_rows,
         packed_project,
         preferred_element_type=jnp.float32,
     ).astype(jnp.bfloat16)
@@ -353,7 +355,7 @@
     arrived = jnp.dot(
         selector.astype(jnp.bfloat16), segment, preferred_element_type=jnp.float32
     ).astype(jnp.bfloat16)
-    text_block = lax.all_gather(text_rows, "tp", axis=0, tiled=True)
+    text_block = lax.all_gather(later_text, "tp", axis=0, tiled=True)
     visual_block = tp_exchange(arrived, tp_ways, True, 5).reshape(-1, model_width)
     landed = dest_table == seq_index
     local_starts = jnp.sum(jnp.where(landed, start_table - seq_index * rows_per_block, 0), 0)

time: 355 us -> 364 us (1.025)
  Pallas kernels: 176 us -> 182 us
    pallas_call x8, Pallas kernels: 130 us -> 136 us  [tp_exchange(): pl.pallas_call(functools.partial(exchange_kernel, axis, ways, stride, gat...]
  transfers between devices with their start and end apart: 3 -> 3, of which waited for: 2 -> 2; matrix products, arithmetic and copies ran while one was open for 11% -> 10% of each run, Pallas kernels for 51% -> 44%
where the time goes in v16:
time: 364 us; the launch traced here: 357 us
  Pallas kernels  182 us (50%)
  waiting for transfers between devices  109 us (30%)
  matrix products  23.1 us (6%)
  local copies, waits for them, and re-layouts  15.4 us (4%)
  between operations  14.1 us (4%)
  other arithmetic  12.8 us (4%)
    pallas_call x8, Pallas kernels, tp_exchange(): pl.pallas_call(functools.partial(exchange_kernel, axis, ways, stride, gat...  136 us
    all_gather x1, waiting for transfers between devices, shards(): lax.all_gather(jnp.concatenate([jnp.transpose(key_flat), jnp.transpose(va...  100 us
    pallas_call x1, Pallas kernels, causal_attention(): pl.pallas_call(attention_kernel, grid_spec=grid_spec, out_shape=jax.Shape...  45.9 us
    all_gather x1, waiting for transfers between devices, shards(): full_output = lax.all_gather(text_output, 'tp', axis=0, tiled=True)  8.7 us
  transfers between devices with their start and end apart: 3, of which 2 were waited for; matrix products, arithmetic and copies ran while one was open for 10% of the time, Pallas kernels for 44%

profile of v16, /device:TPU:223, one launch (start us, length us, event | category | flops | bytes accessed | tf_op | source)
XLA Modules:
  0.0 357.3 jit_solution(8389572561301831607)
XLA Ops:
  7.2 1.2 convert_reduce_fusion.1
  8.4 1.1 fusion.27
  9.6 1.8 fusion.29.x_ref
  11.3 26.1 %shard_map.148 = bf16[8,2,32,1664]{3,2,1,0:T(8,128)(2,1)} custom-call(bf16[2,32,1664]{2,1,0:T(8,128)(2,1)} %fusion.29.x_ref), custom_call_target="tpu_custom_call" | custom-call | tf_op jit(solution)/shard_map/pallas_call | solution.py:100
  37.5 2.8 copy.29
  40.3 3.4 convolution_convert_fusion.3
  44.0 0.6 fusion.63
  44.6 1.3 fusion.18
  46.0 2.6 fusion.20
  48.6 1.1 copy.31
  49.8 0.2 dot_general.34
  50.0 3.0 convolution_convert_fusion.1.x_ref
  53.0 38.3 %shard_map.149 = bf16[8,64,1664]{2,1,0:T(8,128)(2,1)} custom-call(bf16[8,64,1664]{2,1,0:T(8,128)(2,1)} %convolution_convert_fusion.1.x_ref), custom_call_target="tpu_custom_call" | custom-call | tf_op jit(solution)/shard_map/pallas_call | solution.py:100
  91.3 2.6 convert_reduce_fusion
  93.9 1.3 reshape.255
  95.3 0.2 fusion.30
  95.7 0.2 reshape.256
  95.9 0.7 copy.33
  96.6 7.3 %shard_map.150 = bf16[8,2,8,832]{3,2,1,0:T(8,128)(2,1)} custom-call(bf16[8,2,8,832]{3,2,1,0:T(8,128)(2,1)} %bitcast.76), custom_call_target="tpu_custom_call" | custom-call | tf_op jit(solution)/shard_map/pallas_call | solution.py:100
  103.9 1.0 copy.34
  104.9 1.4 fusion.7.x_ref
  106.3 7.9 %shard_map.151 = bf16[8,16,1664]{2,1,0:T(8,128)(2,1)} custom-call(bf16[8,16,1664]{2,1,0:T(8,128)(2,1)} %fusion.7.x_ref), custom_call_target="tpu_custom_call" | custom-call | tf_op jit(solution)/shard_map/pallas_call | solution.py:100
  114.2 1.7 reduce_sum.111.x_ref
  115.9 8.4 %shard_map.152.x_ref = bf16[4,16,1664]{2,1,0:T(8,128)(2,1)} custom-call(bf16[16,1664]{1,0:T(8,128)(2,1)} %reduce_sum.111.x_ref), custom_call_target="tpu_custom_call" | custom-call | tf_op jit(solution)/shard_map/pallas_call | solution.py:100
  124.3 28.3 %shard_map.153 = bf16[8,4,16,1664]{3,2,1,0:T(8,128)(2,1)} custom-call(bf16[4,16,1664]{2,1,0:T(8,128)(2,1)} %shard_map.152.x_ref), custom_call_target="tpu_custom_call" | custom-call | tf_op jit(solution)/shard_map/pallas_call | solution.py:100
  152.6 2.8 copy.35
  155.8 2.4 convolution_convert_fusion.2.x_ref
  158.2 9.0 %shard_map.154 = bf16[8,16,1664]{2,1,0:T(8,128)(2,1)} custom-call(bf16[16,1664]{1,0:T(8,128)(2,1)} %convolution_convert_fusion.2.x_ref), custom_call_target="tpu_custom_call" | custom-call | tf_op jit(solution)/shard_map/pallas_call | solution.py:100
  167.6 0.2 fusion.36
  167.7 0.5 multiply_cosine_fusion
  168.3 2.6 fusion.1
  170.9 1.5 fusion.11
  172.5 0.2 subtract_convert_fusion
  172.6 0.8 copy-done.2
  173.4 0.8 pad_maximum_fusion
  174.3 0.2 all-gather.8.cloned.1.call-start
  174.5 0.5 all-gather.8.cloned.1.call-update
  175.0 1.7 slice.60
  176.8 0.7 pad_maximum_fusion.1
  177.5 100.1 %all-gather.6.cloned.1.call-done.k_ref.v_ref = bf16[13312,512]{1,0:T(8,128)(2,1)} async-done(((bf16[416,512]{1,0:T(8,128)(2,1)}), bf16[13312,512]{1,0:T(8,128)(2,1)}) %all-gather.6.cloned.1.call-update) | async-done | bytes 13631504 | tf_op jit(solution)/shard_map/all_gather | solution.py:392
  277.6 45.9 %shard_map.155 = f32[208,512]{1,0:T(8,128)} custom-call(s32[1]{0:T(128)} %bitcast.21.meta_ref, s32[32]{0:T(128)} %lengths_ref.1, bf16[208,512]{1,0:T(8,128)(2,1)} %bitcast.87, bf16[13312,512]{1,0:T(8,128)(2,1)} %all-gather.6.cloned.1.call-done.k_ref.v_ref, bf16[13312,512]{1,0:T(8,128)(2,1)} %all-gather.6.cloned.1.call-done.k_ref.v_ref), custom_call_target="tpu_custom_call" | custom-call | flops 13958643712 | bytes 14270464 | tf_op jit(solution)/shard_map/pallas_call | solution.py:225
  323.5 1.0 convert_bitcast_fusion
  324.6 0.8 copy.36
  325.4 11.0 %shard_map.156 = bf16[8,64,208]{2,1,0:T(8,128)(2,1)} custom-call(bf16[8,64,208]{2,1,0:T(8,128)(2,1)} %bitcast.74), custom_call_target="tpu_custom_call" | custom-call | tf_op jit(solution)/shard_map/pallas_call | solution.py:100
  336.4 1.1 copy.37
  337.5 0.3 reshape.264
  337.8 8.7 %all-gather.8.cloned.1.call-done = bf16[1664,1664]{1,0:T(8,128)(2,1)} async-done(((bf16[208,1664]{1,0:T(8,128)(2,1)}), bf16[1664,1664]{1,0:T(8,128)(2,1)}) %all-gather.8.cloned.1.call-update) | async-done | bytes 5537808 | tf_op jit(solution)/shard_map/all_gather | solution.py:407
  346.5 4.3 %fusion.10 = bf16[64,1664]{1,0:T(8,128)(2,1)} fusion(bf16[64,1664]{1,0:T(8,128)(2,1)S(1)} %reshape.264, bf16[1664,1664]{1,0:T(8,128)(2,1)} %all-gather.8.cloned.1.call-done, bf16[512,1664]{1,0:T(8,128)(2,1)} %copy-done.4, s32[]{:T(128)S(6)} %select_n.72), kind=kOutput, calls=%fused_computation.14 | convolution fusion | flops 354738176 | bytes 6176772 | tf_op jit(solution)/shard_map/dot_general | solution.py:412
  (51 shorter events, 1.6 us)
Async XLA Ops:
  7.2 97.7 %copy-start = (bf16[832,1664]{1,0:T(8,128)(2,1)S(1)}, bf16[832,1664]{1,0:T(8,128)(2,1)}, u32[]{:S(2)}) copy-start(bf16[832,1664]{1,0:T(8,128)(2,1)} %param.22) | copy-start | bytes 8306692
  7.2 161.1 %all-gather.4.cloned.1.call-start = ((), (), s32[]{:S(2)}) async-start(), calls=%async_computation | async-start | bytes 1916928 | tf_op jit(solution)/shard_map/all_gather | solution.py:358
  40.3 237.3 %all-gather.6.cloned.1.call-start = ((), (), s32[]{:S(2)}) async-start(), calls=%async_computation.1 | async-start | bytes 14057472 | tf_op jit(solution)/shard_map/all_gather | solution.py:392
  40.3 3.5 copy-start.6
  91.3 3.8 %copy-start.1 = (bf16[2,32,1664]{2,1,0:T(8,128)(2,1)S(1)}, bf16[2,32,1664]{2,1,0:T(8,128)(2,1)}, u32[]{:S(2)}) copy-start(bf16[2,32,1664]{2,1,0:T(8,128)(2,1)} %param.13) | copy-start | bytes 638980
  91.3 4.2 %copy-start.5 = (f32[1664]{0:T(1024)S(1)}, f32[1664]{0:T(1024)}, u32[]{:S(2)}) copy-start(f32[1664]{0:T(1024)} %param.21) | copy-start | bytes 19972
  152.6 2.8 copy-start.7
  168.2 2.6 copy-start.8
  168.3 2.6 copy-start.9
  170.8 1.5 copy-start.4
  172.3 1.0 copy-start.2
  173.4 150.1 %copy-start.3 = (bf16[512,2,104]{0,2,1:T(8,128)(2,1)}, bf16[512,2,104]{0,2,1:T(8,128)(2,1)S(1)}, u32[]{:S(2)}) copy-start(bf16[512,2,104]{0,2,1:T(8,128)(2,1)S(1)} %pad_maximum_fusion.2) | copy-start | bytes 638980
  174.3 172.1 %all-gather.8.cloned.1.call-start = ((), (), s32[]{:S(2)}) async-start(), calls=%async_computation.2 | async-start | bytes 6230016 | tf_op jit(solution)/shard_map/all_gather | solution.py:407
Sparse Core Ops, SparseCore 0:
  40.4 54.0 all-gather.3
  174.4 103.0 all-gather.5
  279.4 67.0 all-gather.7

commit v17 on v12

--- a/solution.py
+++ b/solution.py
@@ -262,11 +262,11 @@
     patch_normed = layer_normed(pixels, vision_gain).astype(jnp.bfloat16)
     packed_project = vision_project.reshape(model_width, 3 * local_width)
     projected = jnp.einsum(
-        "npd,de->npe",
-        gathered_patches(patch_normed, 0),
+        "tnid,de->ntie",
+        tp_exchange(patch_normed, tp_ways, True, 0),
         packed_project,
         preferred_element_type=jnp.float32,
-    ).astype(jnp.bfloat16)
+    ).astype(jnp.bfloat16).reshape(picture_total, patch_total, 3 * local_width)
     queries = projected[..., :local_width].reshape(picture_total, patch_total, head_count, HEAD)
     key_heads = projected[..., local_width : 2 * local_width].reshape(
         picture_total, patch_total, head_count, HEAD

time: 355 us -> 357 us (level)
  transfers between devices with their start and end apart: 3 -> 3, of which waited for: 2 -> 2; matrix products, arithmetic and copies ran while one was open for 11% -> 12% of each run, Pallas kernels for 51% -> 50%
where the time goes in v17:
time: 357 us; the launch traced here: 351 us
  Pallas kernels  176 us (49%)
  waiting for transfers between devices  110 us (31%)
  matrix products  23.7 us (7%)
  local copies, waits for them, and re-layouts  14.4 us (4%)
  between operations  14.2 us (4%)
  other arithmetic  12.7 us (4%)
    pallas_call x8, Pallas kernels, tp_exchange(): pl.pallas_call(functools.partial(exchange_kernel, axis, ways, stride, gat...  130 us
    all_gather x1, waiting for transfers between devices, shards(): lax.all_gather(jnp.concatenate([jnp.transpose(key_flat), jnp.transpose(va...  99.6 us
    pallas_call x1, Pallas kernels, causal_attention(): pl.pallas_call(attention_kernel, grid_spec=grid_spec, out_shape=jax.Shape...  46 us
    all_gather x1, waiting for transfers between devices, shards(): full_output = lax.all_gather(text_output, 'tp', axis=0, tiled=True)  8.67 us
  transfers between devices with their start and end apart: 3, of which 2 were waited for; matrix products, arithmetic and copies ran while one was open for 12% of the time, Pallas kernels for 50%

profile of v17, /device:TPU:223, one launch (start us, length us, event | category | flops | bytes accessed | tf_op | source)
XLA Modules:
  0.0 350.6 jit_solution(13928614196692445291)
XLA Ops:
  7.2 0.7 all-gather.4.cloned.1.call-update
  8.0 1.1 convert_reduce_fusion.1
  9.1 1.1 fusion.28
  10.2 1.8 fusion.30.x_ref
  12.0 33.4 %shard_map.148 = bf16[8,2,32,1664]{3,2,1,0:T(8,128)(2,1)} custom-call(bf16[2,32,1664]{2,1,0:T(8,128)(2,1)} %fusion.30.x_ref), custom_call_target="tpu_custom_call" | custom-call | tf_op jit(solution)/shard_map/pallas_call | solution.py:100
  45.4 3.7 %fusion.19 = bf16[2,8,32,624]{3,2,0,1:T(8,128)(2,1)S(1)} fusion(bf16[8,2,32,1664]{3,2,1,0:T(8,128)(2,1)} %shard_map.148, bf16[1664,624,1,1]{0,1,3,2:T(8,128)(2,1)} %bitcast.91), kind=kOutput, calls=%fused_computation.25 | convolution fusion | flops 1063575552 | bytes 4419584 | tf_op jit(solution)/shard_map/tnid,de->ntie/dot_general | solution.py:264
  49.2 0.2 fusion.63
  49.4 0.8 copy.34
  50.2 0.8 copy.35
  51.0 0.8 dynamic_slice.6
  51.9 1.6 fusion.64
  53.5 1.3 fusion.18
  55.1 1.9 fusion.21
  57.2 0.2 dot_general.34
  57.5 3.0 convolution_convert_fusion.1.x_ref
  60.4 19.7 %shard_map.149 = bf16[8,64,1664]{2,1,0:T(8,128)(2,1)} custom-call(bf16[8,64,1664]{2,1,0:T(8,128)(2,1)} %convolution_convert_fusion.1.x_ref), custom_call_target="tpu_custom_call" | custom-call | tf_op jit(solution)/shard_map/pallas_call | solution.py:100
  80.2 2.6 convert_reduce_fusion
  82.8 1.3 reshape.255
  84.6 0.2 reshape.256
  84.8 0.7 copy.39
  85.5 7.5 %shard_map.150 = bf16[8,2,8,832]{3,2,1,0:T(8,128)(2,1)} custom-call(bf16[8,2,8,832]{3,2,1,0:T(8,128)(2,1)} %bitcast.78), custom_call_target="tpu_custom_call" | custom-call | tf_op jit(solution)/shard_map/pallas_call | solution.py:100
  93.0 1.0 copy.40
  93.9 1.4 fusion.7.x_ref
  95.3 7.9 %shard_map.151 = bf16[8,16,1664]{2,1,0:T(8,128)(2,1)} custom-call(bf16[8,16,1664]{2,1,0:T(8,128)(2,1)} %fusion.7.x_ref), custom_call_target="tpu_custom_call" | custom-call | tf_op jit(solution)/shard_map/pallas_call | solution.py:100
  103.2 1.7 reduce_sum.111.x_ref
  104.9 8.7 %shard_map.152.x_ref = bf16[4,16,1664]{2,1,0:T(8,128)(2,1)} custom-call(bf16[16,1664]{1,0:T(8,128)(2,1)} %reduce_sum.111.x_ref), custom_call_target="tpu_custom_call" | custom-call | tf_op jit(solution)/shard_map/pallas_call | solution.py:100
  113.6 33.3 %shard_map.153 = bf16[8,4,16,1664]{3,2,1,0:T(8,128)(2,1)} custom-call(bf16[4,16,1664]{2,1,0:T(8,128)(2,1)} %shard_map.152.x_ref), custom_call_target="tpu_custom_call" | custom-call | tf_op jit(solution)/shard_map/pallas_call | solution.py:100
  146.9 2.8 copy.41
  150.1 2.4 convolution_convert_fusion.2.x_ref
  152.5 8.5 %shard_map.154 = bf16[8,16,1664]{2,1,0:T(8,128)(2,1)} custom-call(bf16[16,1664]{1,0:T(8,128)(2,1)} %convolution_convert_fusion.2.x_ref), custom_call_target="tpu_custom_call" | custom-call | tf_op jit(solution)/shard_map/pallas_call | solution.py:100
  161.5 0.5 multiply_cosine_fusion
  162.1 2.6 fusion.1
  164.7 1.5 fusion.11
  166.4 0.8 copy-done.2
  167.2 0.8 pad_maximum_fusion
  168.1 0.2 all-gather.8.cloned.1.call-start
  168.3 0.5 all-gather.8.cloned.1.call-update
  168.8 1.7 slice.60
  170.6 0.7 pad_maximum_fusion.1
  171.3 99.6 %all-gather.6.cloned.1.call-done.k_ref.v_ref = bf16[13312,512]{1,0:T(8,128)(2,1)} async-done(((bf16[416,512]{1,0:T(8,128)(2,1)}), bf16[13312,512]{1,0:T(8,128)(2,1)}) %all-gather.6.cloned.1.call-update) | async-done | bytes 13631504 | tf_op jit(solution)/shard_map/all_gather | solution.py:390
  270.9 46.0 %shard_map.155 = f32[208,512]{1,0:T(8,128)} custom-call(s32[1]{0:T(128)} %bitcast.22.meta_ref, s32[32]{0:T(128)} %lengths_ref.1, bf16[208,512]{1,0:T(8,128)(2,1)} %bitcast.88, bf16[13312,512]{1,0:T(8,128)(2,1)} %all-gather.6.cloned.1.call-done.k_ref.v_ref, bf16[13312,512]{1,0:T(8,128)(2,1)} %all-gather.6.cloned.1.call-done.k_ref.v_ref), custom_call_target="tpu_custom_call" | custom-call | flops 13958643712 | bytes 14270464 | tf_op jit(solution)/shard_map/pallas_call | solution.py:225
  316.9 1.0 convert_bitcast_fusion
  317.9 0.8 copy.42
  318.8 10.9 %shard_map.156 = bf16[8,64,208]{2,1,0:T(8,128)(2,1)} custom-call(bf16[8,64,208]{2,1,0:T(8,128)(2,1)} %bitcast.76), custom_call_target="tpu_custom_call" | custom-call | tf_op jit(solution)/shard_map/pallas_call | solution.py:100
  329.7 1.1 copy.43
  330.8 0.3 reshape.264
  331.1 8.7 %all-gather.8.cloned.1.call-done = bf16[1664,1664]{1,0:T(8,128)(2,1)} async-done(((bf16[208,1664]{1,0:T(8,128)(2,1)}), bf16[1664,1664]{1,0:T(8,128)(2,1)}) %all-gather.8.cloned.1.call-update) | async-done | bytes 5537808 | tf_op jit(solution)/shard_map/all_gather | solution.py:405
  339.8 4.3 %fusion.10 = bf16[64,1664]{1,0:T(8,128)(2,1)} fusion(bf16[64,1664]{1,0:T(8,128)(2,1)S(1)} %reshape.264, bf16[1664,1664]{1,0:T(8,128)(2,1)} %all-gather.8.cloned.1.call-done, bf16[512,1664]{1,0:T(8,128)(2,1)} %copy-done.6, s32[]{:T(128)S(6)} %select_n.72), kind=kOutput, calls=%fused_computation.14 | convolution fusion | flops 354738176 | bytes 6176772 | tf_op jit(solution)/shard_map/dot_general | solution.py:410
  (58 shorter events, 2.3 us)
Async XLA Ops:
  7.2 86.8 %copy-start = (bf16[832,1664]{1,0:T(8,128)(2,1)S(1)}, bf16[832,1664]{1,0:T(8,128)(2,1)}, u32[]{:S(2)}) copy-start(bf16[832,1664]{1,0:T(8,128)(2,1)} %param.22) | copy-start | bytes 8306692
  7.2 154.9 %all-gather.4.cloned.1.call-start = ((), (), s32[]{:S(2)}) async-start(), calls=%async_computation | async-start | bytes 1916928 | tf_op jit(solution)/shard_map/all_gather | solution.py:356
  7.9 263.0 %all-gather.6.cloned.1.call-start = ((), (), s32[]{:S(2)}) async-start(), calls=%async_computation.1 | async-start | bytes 14057472 | tf_op jit(solution)/shard_map/all_gather | solution.py:390
  50.2 3.3 copy-start.3
  51.0 2.5 copy-start.4
  51.9 3.0 copy-start.8
  80.2 3.8 %copy-start.1 = (bf16[2,32,1664]{2,1,0:T(8,128)(2,1)S(1)}, bf16[2,32,1664]{2,1,0:T(8,128)(2,1)}, u32[]{:S(2)}) copy-start(bf16[2,32,1664]{2,1,0:T(8,128)(2,1)} %param.13) | copy-start | bytes 638980
  80.2 4.2 %copy-start.7 = (f32[1664]{0:T(1024)S(1)}, f32[1664]{0:T(1024)}, u32[]{:S(2)}) copy-start(f32[1664]{0:T(1024)} %param.21) | copy-start | bytes 19972
  146.9 2.8 copy-start.9
  162.0 2.6 copy-start.10
  162.1 2.6 copy-start.11
  164.6 1.5 copy-start.6
  166.1 1.0 copy-start.2
  167.2 149.7 %copy-start.5 = (bf16[512,2,104]{0,2,1:T(8,128)(2,1)}, bf16[512,2,104]{0,2,1:T(8,128)(2,1)S(1)}, u32[]{:S(2)}) copy-start(bf16[512,2,104]{0,2,1:T(8,128)(2,1)S(1)} %pad_maximum_fusion.2) | copy-start | bytes 638980
  168.1 171.7 %all-gather.8.cloned.1.call-start = ((), (), s32[]{:S(2)}) async-start(), calls=%async_computation.2 | async-start | bytes 6230016 | tf_op jit(solution)/shard_map/all_gather | solution.py:405
Sparse Core Ops, SparseCore 0:
  9.8 47.3 all-gather.3
  168.2 102.6 all-gather.5
  272.7 67.0 all-gather.7

commit v18 on v12

--- a/solution.py
+++ b/solution.py
@@ -197,7 +197,7 @@
         for h in range(heads):
             in_head = (feature >= h * HEAD) & (feature < (h + 1) * HEAD)
             result = jnp.where(in_head, acc_sc[h] / l_sc[h], result)
-        o_ref[...] = result
+        o_ref[...] = result.astype(o_ref.dtype)
 
 
 def causal_attention(query_flat, key_value_all, seq_index, block_lengths, rows_per_block):
@@ -225,7 +225,7 @@
     result = pl.pallas_call(
         attention_kernel,
         grid_spec=grid_spec,
-        out_shape=jax.ShapeDtypeStruct((width, rows), jnp.float32),
+        out_shape=jax.ShapeDtypeStruct((width, rows), jnp.bfloat16),
         compiler_params=pltpu.CompilerParams(dimension_semantics=("arbitrary",)),
         cost_estimate=pl.CostEstimate(
             flops=4 * heads * rows * keys_total * width,
@@ -233,7 +233,7 @@
             bytes_accessed=key_value_all.size * 2 + 3 * query_flat.size * 2,
         ),
     )(meta, block_lengths, jnp.transpose(query_flat), key_value_all, key_value_all)
-    return jnp.transpose(result).astype(jnp.bfloat16)
+    return jnp.transpose(result)
 
 
 def shards(

time: 355 us -> 355 us (level)
  transfers between devices with their start and end apart: 3 -> 3, of which waited for: 2 -> 2; matrix products, arithmetic and copies ran while one was open for 11% -> 11% of each run, Pallas kernels for 51% -> 50%
where the time goes in v18:
time: 355 us; the launch traced here: 348 us
  Pallas kernels  176 us (50%)
  waiting for transfers between devices  110 us (31%)
  matrix products  21 us (6%)
  local copies, waits for them, and re-layouts  15.7 us (4%)
  between operations  14.2 us (4%)
  other arithmetic  11.6 us (3%)
    pallas_call x8, Pallas kernels, tp_exchange(): pl.pallas_call(functools.partial(exchange_kernel, axis, ways, stride, gat...  130 us
    all_gather x1, waiting for transfers between devices, shards(): lax.all_gather(jnp.concatenate([jnp.transpose(key_flat), jnp.transpose(va...  99.7 us
    pallas_call x1, Pallas kernels, causal_attention(): pl.pallas_call(attention_kernel, grid_spec=grid_spec, out_shape=jax.Shape...  45.9 us
    all_gather x1, waiting for transfers between devices, shards(): full_output = lax.all_gather(text_output, 'tp', axis=0, tiled=True)  8.87 us
  transfers between devices with their start and end apart: 3, of which 2 were waited for; matrix products, arithmetic and copies ran while one was open for 11% of the time, Pallas kernels for 50%

profile of v18, /device:TPU:223, one launch (start us, length us, event | category | flops | bytes accessed | tf_op | source)
XLA Modules:
  0.0 348.2 jit_solution(12456759206947896464)
XLA Ops:
  7.2 0.7 all-gather.4.cloned.1.call-update
  8.0 1.1 convert_reduce_fusion.1
  9.1 1.1 fusion.27
  10.2 1.8 fusion.29.x_ref
  12.0 33.4 %shard_map.148 = bf16[8,2,32,1664]{3,2,1,0:T(8,128)(2,1)} custom-call(bf16[2,32,1664]{2,1,0:T(8,128)(2,1)} %fusion.29.x_ref), custom_call_target="tpu_custom_call" | custom-call | tf_op jit(solution)/shard_map/pallas_call | solution.py:100
  45.4 1.8 copy.29
  47.1 0.3 copy-done.8
  47.5 1.3 convolution_convert_fusion.3
  49.1 0.6 fusion.63
  49.6 1.3 fusion.18
  51.1 2.6 fusion.20
  53.7 1.1 copy.31
  54.8 0.2 dot_general.34
  55.1 3.0 convolution_convert_fusion.1.x_ref
  58.0 19.7 %shard_map.149 = bf16[8,64,1664]{2,1,0:T(8,128)(2,1)} custom-call(bf16[8,64,1664]{2,1,0:T(8,128)(2,1)} %convolution_convert_fusion.1.x_ref), custom_call_target="tpu_custom_call" | custom-call | tf_op jit(solution)/shard_map/pallas_call | solution.py:100
  77.8 2.6 convert_reduce_fusion
  80.3 1.3 reshape.255
  81.8 0.2 fusion.30
  82.1 0.2 reshape.256
  82.4 0.7 copy.33
  83.1 7.5 %shard_map.150 = bf16[8,2,8,832]{3,2,1,0:T(8,128)(2,1)} custom-call(bf16[8,2,8,832]{3,2,1,0:T(8,128)(2,1)} %bitcast.75), custom_call_target="tpu_custom_call" | custom-call | tf_op jit(solution)/shard_map/pallas_call | solution.py:100
  90.6 1.0 copy.34
  91.5 1.4 fusion.7.x_ref
  92.9 7.9 %shard_map.151 = bf16[8,16,1664]{2,1,0:T(8,128)(2,1)} custom-call(bf16[8,16,1664]{2,1,0:T(8,128)(2,1)} %fusion.7.x_ref), custom_call_target="tpu_custom_call" | custom-call | tf_op jit(solution)/shard_map/pallas_call | solution.py:100
  100.8 1.7 reduce_sum.111.x_ref
  102.5 8.7 %shard_map.152.x_ref = bf16[4,16,1664]{2,1,0:T(8,128)(2,1)} custom-call(bf16[16,1664]{1,0:T(8,128)(2,1)} %reduce_sum.111.x_ref), custom_call_target="tpu_custom_call" | custom-call | tf_op jit(solution)/shard_map/pallas_call | solution.py:100
  111.2 33.3 %shard_map.153 = bf16[8,4,16,1664]{3,2,1,0:T(8,128)(2,1)} custom-call(bf16[4,16,1664]{2,1,0:T(8,128)(2,1)} %shard_map.152.x_ref), custom_call_target="tpu_custom_call" | custom-call | tf_op jit(solution)/shard_map/pallas_call | solution.py:100
  144.5 2.8 copy.35
  147.7 2.4 convolution_convert_fusion.2.x_ref
  150.1 8.5 %shard_map.154 = bf16[8,16,1664]{2,1,0:T(8,128)(2,1)} custom-call(bf16[16,1664]{1,0:T(8,128)(2,1)} %convolution_convert_fusion.2.x_ref), custom_call_target="tpu_custom_call" | custom-call | tf_op jit(solution)/shard_map/pallas_call | solution.py:100
  159.1 0.5 multiply_cosine_fusion
  159.6 2.6 fusion.1
  162.2 1.5 fusion.11
  163.8 0.2 subtract_convert_fusion
  164.0 0.8 copy-done.2
  164.8 0.8 pad_maximum_fusion
  165.7 0.2 all-gather.8.cloned.1.call-start
  165.9 0.5 all-gather.8.cloned.1.call-update
  166.4 1.7 slice.60
  168.1 0.7 pad_maximum_fusion.1
  168.8 99.7 %all-gather.6.cloned.1.call-done.k_ref.v_ref = bf16[13312,512]{1,0:T(8,128)(2,1)} async-done(((bf16[416,512]{1,0:T(8,128)(2,1)}), bf16[13312,512]{1,0:T(8,128)(2,1)}) %all-gather.6.cloned.1.call-update) | async-done | bytes 13631504 | tf_op jit(solution)/shard_map/all_gather | solution.py:390
  268.5 45.9 %shard_map.155 = bf16[208,512]{1,0:T(8,128)(2,1)} custom-call(s32[1]{0:T(128)} %bitcast.21.meta_ref, s32[32]{0:T(128)} %lengths_ref.1, bf16[208,512]{1,0:T(8,128)(2,1)} %bitcast.86, bf16[13312,512]{1,0:T(8,128)(2,1)} %all-gather.6.cloned.1.call-done.k_ref.v_ref, bf16[13312,512]{1,0:T(8,128)(2,1)} %all-gather.6.cloned.1.call-done.k_ref.v_ref), custom_call_target="tpu_custom_call" | custom-call | flops 13958643712 | bytes 14270464 | tf_op jit(solution)/shard_map/pallas_call | solution.py:225
  314.4 1.8 copy.36
  316.2 11.0 %shard_map.156 = bf16[8,64,208]{2,1,0:T(8,128)(2,1)} custom-call(bf16[8,64,208]{2,1,0:T(8,128)(2,1)} %bitcast.73), custom_call_target="tpu_custom_call" | custom-call | tf_op jit(solution)/shard_map/pallas_call | solution.py:100
  327.1 1.1 copy.37
  328.2 0.3 reshape.264
  328.5 8.9 %all-gather.8.cloned.1.call-done = bf16[1664,1664]{1,0:T(8,128)(2,1)} async-done(((bf16[208,1664]{1,0:T(8,128)(2,1)}), bf16[1664,1664]{1,0:T(8,128)(2,1)}) %all-gather.8.cloned.1.call-update) | async-done | bytes 5537808 | tf_op jit(solution)/shard_map/all_gather | solution.py:405
  337.4 4.3 %fusion.10 = bf16[64,1664]{1,0:T(8,128)(2,1)} fusion(bf16[64,1664]{1,0:T(8,128)(2,1)S(1)} %reshape.264, bf16[1664,1664]{1,0:T(8,128)(2,1)} %all-gather.8.cloned.1.call-done, bf16[512,1664]{1,0:T(8,128)(2,1)} %copy-done.4, s32[]{:T(128)S(6)} %select_n.72), kind=kOutput, calls=%fused_computation.14 | convolution fusion | flops 354738176 | bytes 6176772 | tf_op jit(solution)/shard_map/dot_general | solution.py:410
  (52 shorter events, 1.7 us)
Async XLA Ops:
  7.2 84.4 %copy-start = (bf16[832,1664]{1,0:T(8,128)(2,1)S(1)}, bf16[832,1664]{1,0:T(8,128)(2,1)}, u32[]{:S(2)}) copy-start(bf16[832,1664]{1,0:T(8,128)(2,1)} %param.22) | copy-start | bytes 8306692
  7.2 152.4 %all-gather.4.cloned.1.call-start = ((), (), s32[]{:S(2)}) async-start(), calls=%async_computation | async-start | bytes 1916928 | tf_op jit(solution)/shard_map/all_gather | solution.py:356
  7.9 260.6 %all-gather.6.cloned.1.call-start = ((), (), s32[]{:S(2)}) async-start(), calls=%async_computation.1 | async-start | bytes 14057472 | tf_op jit(solution)/shard_map/all_gather | solution.py:390
  45.4 2.1 copy-start.8
  47.5 1.4 copy-start.6
  77.8 3.8 %copy-start.1 = (bf16[2,32,1664]{2,1,0:T(8,128)(2,1)S(1)}, bf16[2,32,1664]{2,1,0:T(8,128)(2,1)}, u32[]{:S(2)}) copy-start(bf16[2,32,1664]{2,1,0:T(8,128)(2,1)} %param.13) | copy-start | bytes 638980
  77.8 4.2 %copy-start.5 = (f32[1664]{0:T(1024)S(1)}, f32[1664]{0:T(1024)}, u32[]{:S(2)}) copy-start(f32[1664]{0:T(1024)} %param.21) | copy-start | bytes 19972
  144.5 2.8 copy-start.7
  159.6 2.6 copy-start.9
  159.6 2.6 copy-start.10
  162.2 1.5 copy-start.4
  163.7 1.0 copy-start.2
  164.8 149.6 %copy-start.3 = (bf16[512,2,104]{0,2,1:T(8,128)(2,1)}, bf16[512,2,104]{0,2,1:T(8,128)(2,1)S(1)}, u32[]{:S(2)}) copy-start(bf16[512,2,104]{0,2,1:T(8,128)(2,1)S(1)} %pad_maximum_fusion.2) | copy-start | bytes 638980
  165.7 171.7 %all-gather.8.cloned.1.call-start = ((), (), s32[]{:S(2)}) async-start(), calls=%async_computation.2 | async-start | bytes 6230016 | tf_op jit(solution)/shard_map/all_gather | solution.py:405
Sparse Core Ops, SparseCore 0:
  9.8 47.3 all-gather.3
  165.8 102.6 all-gather.5
  270.3 67.0 all-gather.7
